TPU v7x, 128 devices: a whole 4x4x4 slice. The times are simulated.
128 devices in a mesh: tm: 8 (over z_lo, x), azim: 16 (over y, z_hi, core).
Axes of the slice: x: 4, y: 4, z: 4 (z_hi: 2, z_lo: 2; z = z_hi * 2 + z_lo), core: 2. Of those that a mesh axis runs over, the one named last changes fastest.
Arguments:
- initial_state: float32 [3, 64, 96, 256], P(None, 'azim'), may hold values from -6 to 6
- forcing: float32 [3, 64, 96, 256], P(None, 'azim'), may hold values from -12 to 12
- forward_radial: float32 [96, 96], replicated, may hold values from -0.21875 to 0.21875
- backward_radial: float32 [96, 96], replicated, may hold values from -0.21875 to 0.21875
- forward_axial: float32 [256, 256], replicated, may hold values from -0.125 to 0.125
- backward_axial: float32 [256, 256], replicated, may hold values from -0.125 to 0.125
- forward_radial_coarse: float32 [48, 48], replicated, may hold values from -0.3125 to 0.3125
- backward_radial_coarse: float32 [48, 48], replicated, may hold values from -0.3125 to 0.3125
- forward_axial_coarse: float32 [128, 128], replicated, may hold values from -0.1875 to 0.1875
- backward_axial_coarse: float32 [128, 128], replicated, may hold values from -0.1875 to 0.1875
- decay_radial: float32 [96], replicated, may hold values from 0.01 to 10
- decay_axial: float32 [256], replicated, may hold values from 0.01 to 10
- advection: float32 [96, 256], replicated, may hold values from -0.6 to 0.6
- diffusion: float32 [96], replicated, may hold values from 0.05 to 0.4
Outputs:
- end_states: float32 [8, 3, 64, 96, 256], P('tm', None, 'azim')
All inputs are finite; a program needn't handle non-finite values.
Results may differ from a plain program's by a relative error of at most 0.0001.
Values sent between devices are 32-bit elements; how exact they have to be, the bound alone decides.
No kernel may reach another device: no remote copies, remote signals or barrier semaphores. Data moves between devices by JAX's collectives and lax.ppermute only.
A program may use at most 64 MiB of HBM per device.

v0:
```python
import jax
import jax.numpy as jnp
from jax import lax
from jax.sharding import PartitionSpec as P

ITERS = 2


HI = lax.Precision.HIGHEST
time_step = 0.1


def with_halo(block, sides, width):
    for axis, dim in sides:
        count = lax.axis_size(axis)
        forward = [(i, i + 1) for i in range(count - 1)]
        forward.append((count - 1, 0))
        backward = [(target, source) for source, target in forward]
        low = lax.ppermute(
            lax.slice_in_dim(block, block.shape[dim] - width, None, axis=dim), axis, forward
        )
        high = lax.ppermute(lax.slice_in_dim(block, 0, width, axis=dim), axis, backward)
        block = jnp.concatenate([low, block, high], axis=dim)
    return block


def shifted(block, axis, distance):
    devices = range(lax.axis_size(axis))
    route = [(i - distance, i) for i in devices if i - distance in devices]
    return lax.ppermute(block, axis, route)


def to_phys(modes, backward_r, backward_z):
    inner = jnp.einsum("...ij,zj->...iz", modes, backward_z, precision=HI)
    return jnp.einsum("ri,...iz->...rz", backward_r, inner, precision=HI)


def to_modal(field, forward_r, forward_z):
    inner = jnp.einsum("...rz,jz->...rj", field, forward_z, precision=HI)
    return jnp.einsum("ir,...rj->...ij", forward_r, inner, precision=HI)


def forces(field, upper, lower, advect, diffuse):
    spread = advect * (upper - lower) + diffuse[:, None] * (upper - 2.0 * field + lower)
    zero_part = jnp.zeros_like(field[..., 0, :, :, :])
    turning = jnp.stack(
        [2.0 * field[..., 1, :, :, :], -2.0 * field[..., 0, :, :, :], zero_part], axis=-4
    )
    return spread + turning


def fine_push(modes, operators):
    backward_r, backward_z, forward_r, forward_z, advect, diffuse = operators
    field = to_phys(modes, backward_r, backward_z)
    widened = with_halo(field, (("azim", 1),), 1)
    return to_modal(
        forces(field, widened[:, 2:], widened[:, :-2], advect, diffuse), forward_r, forward_z
    )


def coarse_push(modes, operators):
    backward_r, backward_z, forward_r, forward_z, advect, diffuse = operators
    field = to_phys(modes, backward_r, backward_z)
    widened = with_halo(field, (("azim", 1),), 1)
    return to_modal(
        forces(field, widened[:, 2:], widened[:, :-2], advect, diffuse), forward_r, forward_z
    )


def per_device(
    initial_state,
    forcing,
    forward_radial,
    backward_radial,
    forward_axial,
    backward_axial,
    forward_radial_coarse,
    backward_radial_coarse,
    forward_axial_coarse,
    backward_axial_coarse,
    decay_radial,
    decay_axial,
    advection,
    diffusion,
):
    radial = forward_radial.shape[0]
    axial = forward_axial.shape[0]
    radial_c = forward_radial_coarse.shape[0]
    axial_c = forward_axial_coarse.shape[0]
    eye_r = jnp.eye(radial, dtype=jnp.float32)
    eye_z = jnp.eye(axial, dtype=jnp.float32)
    eye_rc = jnp.eye(radial_c, dtype=jnp.float32)
    eye_zc = jnp.eye(axial_c, dtype=jnp.float32)
    fine_set = (
        eye_r + backward_radial,
        eye_z + backward_axial,
        eye_r + forward_radial,
        eye_z + forward_axial,
        advection,
        diffusion,
    )
    coarse_set = (
        eye_rc + backward_radial_coarse,
        eye_zc + backward_axial_coarse,
        eye_rc + forward_radial_coarse,
        eye_zc + forward_axial_coarse,
        advection[::2, ::2],
        diffusion[::2],
    )
    spectrum = -(decay_radial[:, None] + decay_axial[None, :])
    coarse_spectrum = spectrum[:radial_c, :axial_c]
    half_step = 0.5 * time_step
    first_slice = (lax.axis_index("tm") == 0).astype(jnp.float32)
    restricted_init = initial_state[:, :, :radial_c, :axial_c]

    def propagate(state):
        return (state + time_step * coarse_push(state, coarse_set)) / (
            1.0 - time_step * coarse_spectrum
        )

    def widen(delta):
        return jnp.pad(delta, ((0, 0), (0, 0), (0, radial - radial_c), (0, axial - axial_c)))

    base_push = fine_push(initial_state, fine_set) + forcing
    nodes = [initial_state, initial_state, initial_state]
    pushes = [base_push, base_push, base_push]
    start = initial_state
    for turn_index in range(ITERS):
        totals = [pushes[node_index] + spectrum * nodes[node_index] for node_index in range(3)]
        if turn_index == 0:
            start_push = pushes[0]
        else:
            start_push = fine_push(start, fine_set) + forcing
        middle = (
            start
            + half_step * (start_push - pushes[0])
            - half_step * spectrum * nodes[1]
            + time_step * (5.0 / 24.0 * totals[0] + 1.0 / 3.0 * totals[1] - 1.0 / 24.0 * totals[2])
        ) / (1.0 - half_step * spectrum)
        middle_push = fine_push(middle, fine_set) + forcing
        ending = (
            middle
            + half_step * (middle_push - pushes[1])
            - half_step * spectrum * nodes[2]
            + time_step * (-1.0 / 24.0 * totals[0] + 1.0 / 3.0 * totals[1] + 5.0 / 24.0 * totals[2])
        ) / (1.0 - half_step * spectrum)
        ending_push = fine_push(ending, fine_set) + forcing
        nodes = [start, middle, ending]
        pushes = [start_push, middle_push, ending_push]
        totals = [pushes[node_index] + spectrum * nodes[node_index] for node_index in range(3)]
        integral = time_step * (totals[0] / 6.0 + 2.0 * totals[1] / 3.0 + totals[2] / 6.0)
        coarse_zero = nodes[0][:, :, :radial_c, :axial_c]
        coarse_one = nodes[2][:, :, :radial_c, :axial_c]
        constant = (
            integral[:, :, :radial_c, :axial_c]
            - time_step * coarse_push(coarse_zero, coarse_set)
            - time_step * coarse_spectrum * coarse_one
        ) / (1.0 - time_step * coarse_spectrum)

        def advance(section_index, running):
            latest, earlier = running
            arrived = shifted(latest, "tm", 1)
            begin_now = arrived + first_slice * restricted_init
            return (constant + propagate(begin_now), begin_now)

        coarse_end, coarse_begin = lax.fori_loop(
            0, lax.axis_size("tm"), advance, (constant, jnp.zeros_like(constant))
        )
        delta_zero = coarse_begin - coarse_zero
        delta_one = coarse_end - coarse_one
        nodes = [
            nodes[0] + widen(delta_zero),
            nodes[1] + widen(0.5 * (delta_zero + delta_one)),
            nodes[2] + widen(delta_one),
        ]
        if turn_index + 1 < ITERS:
            pushes = [fine_push(nodes[node_index], fine_set) + forcing for node_index in range(3)]
            arrived_end = shifted(nodes[2], "tm", 1)
            start = arrived_end + first_slice * initial_state
    return nodes[2][None]


def solution(mesh):
    in_specs = (
        P(None, "azim", None, None),
        P(None, "azim", None, None),
        P(),
        P(),
        P(),
        P(),
        P(),
        P(),
        P(),
        P(),
        P(),
        P(),
        P(),
        P(),
    )
    out_specs = P("tm", None, "azim", None, None)
    return jax.shard_map(
        per_device, mesh=mesh, in_specs=in_specs, out_specs=out_specs, check_vma=False
    )
```

profile of v0, /device:TPU:32, one launch (start us, length us, event | category | flops | bytes accessed | tf_op | source)
XLA Modules:
  0.0 513.9 jit_solution(12553103954712659054)
XLA Ops:
  0.0 2.5 convolution_bitcast_fusion.2
  3.8 4.9 collective-permute-start.6
  10.3 5.4 %collective-permute-start.12 = (f32[3,1,48,128]{3,2,1,0:T(8,128)}, f32[3,1,48,128]{3,2,1,0:T(8,128)}, u32[]{:S(2)}, u32[]{:S(2)}) collective-permute-start(f32[3,1,48,128]{3,2,1,0:T(8,128)} %get-tuple-element.241), channel_id=1, source_target_pairs={{1,0},{2,1},{3,2},{4,3},{5,4},{6,5},{7,6},{8,7},{9,8},{10,9},{11,1... | collective-permute-start | bytes 221192 | tf_op jit(solution)/shard_map/ppermute | solution.py:22
  20.0 2.8 add_divide_fusion.3
  27.1 4.8 collective-permute-start.8
  36.5 6.0 %collective-permute-done.9 = f32[3,1,96,256]{3,2,1,0:T(8,128)} collective-permute-done((f32[3,1,96,256]{3,2,1,0:T(8,128)}, f32[3,1,96,256]{3,2,1,0:T(8,128)}, u32[]{:S(2)}, u32[]{:S(2)}) %collective-permute-start.9) | collective-permute-done | bytes 294944 | tf_op jit(solution)/shard_map/ppermute | solution.py:19
  42.6 2.6 fusion.64
  51.9 2.0 collective-permute-done.10
  53.8 5.8 %collective-permute-done.11 = f32[3,1,96,256]{3,2,1,0:T(8,128)S(1)} collective-permute-done((f32[3,1,96,256]{3,2,1,0:T(8,128)S(1)}, f32[3,1,96,256]{3,2,1,0:T(8,128)S(1)}, u32[]{:S(2)}, u32[]{:S(2)}) %collective-permute-start.11) | collective-permute-done | bytes 294944 | tf_op jit(solution)/shard_map/ppermute | solution.py:19
  63.5 177.7 %while.22 = (s32[]{:T(128)}, f32[3,4,48,128]{3,2,1,0:T(8,128)}, f32[3,4,48,128]{3,2,1,0:T(8,128)}, f32[]{:T(128)}, f32[3,4,48,128]{3,2,1,0:T(8,128)S(1)}, /*inde...) while((s32[]{:T(128)}, f32[3,4,48,128]{3,2,1,0:T(8,128)}, ...), condition=%wide.region_1.0_spmd, body=%wide.region_0.0_spmd.sunk | while | flops 312815616 | bytes 8424801 | solution.py:166
  63.5 3.4 collective-permute-start
  67.0 8.3 %collective-permute-done = f32[3,4,48,128]{3,2,1,0:T(8,128)} collective-permute-done((f32[3,4,48,128]{3,2,1,0:T(8,128)}, f32[3,4,48,128]{3,2,1,0:T(8,128)}, u32[]{:S(2)}, u32[]{:S(2)}) %collective-permute-start) | collective-permute-done | bytes 294944 | tf_op jit(solution)/shard_map/while/body/eval_jaxpr/ppermute | solution.py:30
  79.3 5.5 %collective-permute-done.2 = f32[3,1,48,128]{3,2,1,0:T(8,128)S(1)} collective-permute-done((f32[3,1,48,128]{3,2,1,0:T(8,128)S(1)}, f32[3,1,48,128]{3,2,1,0:T(8,128)S(1)}, u32[]{:S(2)}, u32[]{:S(2)}) %collective-permute-start.2) | collective-permute-done | bytes 73760 | tf_op jit(solution)/shard_map/while/body/eval_jaxpr/ppermute | solution.py:19
  88.4 9.1 %collective-permute-done = f32[3,4,48,128]{3,2,1,0:T(8,128)} collective-permute-done((f32[3,4,48,128]{3,2,1,0:T(8,128)}, f32[3,4,48,128]{3,2,1,0:T(8,128)}, u32[]{:S(2)}, u32[]{:S(2)}) %collective-permute-start) | collective-permute-done | bytes 294944 | tf_op jit(solution)/shard_map/while/body/eval_jaxpr/ppermute | solution.py:30
  101.5 5.5 %collective-permute-done.2 = f32[3,1,48,128]{3,2,1,0:T(8,128)S(1)} collective-permute-done((f32[3,1,48,128]{3,2,1,0:T(8,128)S(1)}, f32[3,1,48,128]{3,2,1,0:T(8,128)S(1)}, u32[]{:S(2)}, u32[]{:S(2)}) %collective-permute-start.2) | collective-permute-done | bytes 73760 | tf_op jit(solution)/shard_map/while/body/eval_jaxpr/ppermute | solution.py:19
  110.6 9.1 %collective-permute-done = f32[3,4,48,128]{3,2,1,0:T(8,128)} collective-permute-done((f32[3,4,48,128]{3,2,1,0:T(8,128)}, f32[3,4,48,128]{3,2,1,0:T(8,128)}, u32[]{:S(2)}, u32[]{:S(2)}) %collective-permute-start) | collective-permute-done | bytes 294944 | tf_op jit(solution)/shard_map/while/body/eval_jaxpr/ppermute | solution.py:30
  123.7 5.5 %collective-permute-done.2 = f32[3,1,48,128]{3,2,1,0:T(8,128)S(1)} collective-permute-done((f32[3,1,48,128]{3,2,1,0:T(8,128)S(1)}, f32[3,1,48,128]{3,2,1,0:T(8,128)S(1)}, u32[]{:S(2)}, u32[]{:S(2)}) %collective-permute-start.2) | collective-permute-done | bytes 73760 | tf_op jit(solution)/shard_map/while/body/eval_jaxpr/ppermute | solution.py:19
  132.8 9.0 %collective-permute-done = f32[3,4,48,128]{3,2,1,0:T(8,128)} collective-permute-done((f32[3,4,48,128]{3,2,1,0:T(8,128)}, f32[3,4,48,128]{3,2,1,0:T(8,128)}, u32[]{:S(2)}, u32[]{:S(2)}) %collective-permute-start) | collective-permute-done | bytes 294944 | tf_op jit(solution)/shard_map/while/body/eval_jaxpr/ppermute | solution.py:30
  145.7 5.5 %collective-permute-done.2 = f32[3,1,48,128]{3,2,1,0:T(8,128)S(1)} collective-permute-done((f32[3,1,48,128]{3,2,1,0:T(8,128)S(1)}, f32[3,1,48,128]{3,2,1,0:T(8,128)S(1)}, u32[]{:S(2)}, u32[]{:S(2)}) %collective-permute-start.2) | collective-permute-done | bytes 73760 | tf_op jit(solution)/shard_map/while/body/eval_jaxpr/ppermute | solution.py:19
  154.9 9.0 %collective-permute-done = f32[3,4,48,128]{3,2,1,0:T(8,128)} collective-permute-done((f32[3,4,48,128]{3,2,1,0:T(8,128)}, f32[3,4,48,128]{3,2,1,0:T(8,128)}, u32[]{:S(2)}, u32[]{:S(2)}) %collective-permute-start) | collective-permute-done | bytes 294944 | tf_op jit(solution)/shard_map/while/body/eval_jaxpr/ppermute | solution.py:30
  167.8 5.5 %collective-permute-done.2 = f32[3,1,48,128]{3,2,1,0:T(8,128)S(1)} collective-permute-done((f32[3,1,48,128]{3,2,1,0:T(8,128)S(1)}, f32[3,1,48,128]{3,2,1,0:T(8,128)S(1)}, u32[]{:S(2)}, u32[]{:S(2)}) %collective-permute-start.2) | collective-permute-done | bytes 73760 | tf_op jit(solution)/shard_map/while/body/eval_jaxpr/ppermute | solution.py:19
  177.0 9.0 %collective-permute-done = f32[3,4,48,128]{3,2,1,0:T(8,128)} collective-permute-done((f32[3,4,48,128]{3,2,1,0:T(8,128)}, f32[3,4,48,128]{3,2,1,0:T(8,128)}, u32[]{:S(2)}, u32[]{:S(2)}) %collective-permute-start) | collective-permute-done | bytes 294944 | tf_op jit(solution)/shard_map/while/body/eval_jaxpr/ppermute | solution.py:30
  189.9 5.5 %collective-permute-done.2 = f32[3,1,48,128]{3,2,1,0:T(8,128)S(1)} collective-permute-done((f32[3,1,48,128]{3,2,1,0:T(8,128)S(1)}, f32[3,1,48,128]{3,2,1,0:T(8,128)S(1)}, u32[]{:S(2)}, u32[]{:S(2)}) %collective-permute-start.2) | collective-permute-done | bytes 73760 | tf_op jit(solution)/shard_map/while/body/eval_jaxpr/ppermute | solution.py:19
  199.0 9.0 %collective-permute-done = f32[3,4,48,128]{3,2,1,0:T(8,128)} collective-permute-done((f32[3,4,48,128]{3,2,1,0:T(8,128)}, f32[3,4,48,128]{3,2,1,0:T(8,128)}, u32[]{:S(2)}, u32[]{:S(2)}) %collective-permute-start) | collective-permute-done | bytes 294944 | tf_op jit(solution)/shard_map/while/body/eval_jaxpr/ppermute | solution.py:30
  212.0 5.5 %collective-permute-done.2 = f32[3,1,48,128]{3,2,1,0:T(8,128)S(1)} collective-permute-done((f32[3,1,48,128]{3,2,1,0:T(8,128)S(1)}, f32[3,1,48,128]{3,2,1,0:T(8,128)S(1)}, u32[]{:S(2)}, u32[]{:S(2)}) %collective-permute-start.2) | collective-permute-done | bytes 73760 | tf_op jit(solution)/shard_map/while/body/eval_jaxpr/ppermute | solution.py:19
  221.1 9.0 %collective-permute-done = f32[3,4,48,128]{3,2,1,0:T(8,128)} collective-permute-done((f32[3,4,48,128]{3,2,1,0:T(8,128)}, f32[3,4,48,128]{3,2,1,0:T(8,128)}, u32[]{:S(2)}, u32[]{:S(2)}) %collective-permute-start) | collective-permute-done | bytes 294944 | tf_op jit(solution)/shard_map/while/body/eval_jaxpr/ppermute | solution.py:30
  234.1 5.5 %collective-permute-done.2 = f32[3,1,48,128]{3,2,1,0:T(8,128)S(1)} collective-permute-done((f32[3,1,48,128]{3,2,1,0:T(8,128)S(1)}, f32[3,1,48,128]{3,2,1,0:T(8,128)S(1)}, u32[]{:S(2)}, u32[]{:S(2)}) %collective-permute-start.2) | collective-permute-done | bytes 73760 | tf_op jit(solution)/shard_map/while/body/eval_jaxpr/ppermute | solution.py:19
  250.6 4.9 collective-permute-start.19
  258.1 5.4 %collective-permute-start.21 = (f32[3,1,96,256]{3,2,1,0:T(8,128)S(1)}, f32[3,1,96,256]{3,2,1,0:T(8,128)S(1)}, u32[]{:S(2)}, u32[]{:S(2)}) collective-permute-start(f32[3,1,96,256]{3,2,1,0:T(8,128)S(1)} %get-tuple-element.221), channel_id=1, source_target_pairs={{1,0},{2,1},{3,2},{4,3},{5,4},{6,5},{7,6},{8,7},{9,8},{10,9},{11,1... | collective-permute-start | bytes 884744 | tf_op jit(solution)/shard_map/ppermute | solution.py:22
  264.9 2.2 collective-permute-start.14
  268.6 4.7 collective-permute-done.22
  277.1 19.3 %collective-permute-done.14 = f32[3,4,96,256]{3,2,1,0:T(8,128)S(1)} collective-permute-done((f32[3,4,96,256]{3,2,1,0:T(8,128)S(1)}, f32[3,4,96,256]{3,2,1,0:T(8,128)S(1)}, u32[]{:S(2)}, u32[]{:S(2)}) %collective-permute-start.14) | collective-permute-done | bytes 1179680 | tf_op jit(solution)/shard_map/ppermute | solution.py:30
  299.4 4.7 collective-permute-start.15
  305.0 3.3 collective-permute-done.15
  308.3 6.0 %collective-permute-done.16 = f32[3,1,96,256]{3,2,1,0:T(8,128)S(1)} collective-permute-done((f32[3,1,96,256]{3,2,1,0:T(8,128)S(1)}, f32[3,1,96,256]{3,2,1,0:T(8,128)S(1)}, u32[]{:S(2)}, u32[]{:S(2)}) %collective-permute-start.16) | collective-permute-done | bytes 294944 | tf_op jit(solution)/shard_map/ppermute | solution.py:19
  316.9 2.2 add_divide_fusion.1
  322.0 5.0 collective-permute-start.27
  327.3 4.1 collective-permute-done.24
  332.7 2.2 add_divide_fusion
  339.5 3.5 collective-permute-done.25
  342.9 5.7 %collective-permute-done.26 = f32[3,1,96,256]{3,2,1,0:T(8,128)S(1)} collective-permute-done((f32[3,1,96,256]{3,2,1,0:T(8,128)S(1)}, f32[3,1,96,256]{3,2,1,0:T(8,128)S(1)}, u32[]{:S(2)}, u32[]{:S(2)}) %collective-permute-start.26) | collective-permute-done | bytes 294944 | tf_op jit(solution)/shard_map/ppermute | solution.py:19
  352.2 160.3 %while.23 = (s32[]{:T(128)}, f32[3,4,48,128]{3,2,1,0:T(8,128)S(1)}, f32[]{:T(128)}, f32[3,4,48,128]{3,2,1,0:T(8,128)S(1)}, f32[48,128]{1,0:T(8,128)S(1)}, /*inde...) while((s32[]{:T(128)}, f32[3,4,48,128]{3,2,1,0:T(8,128)S(1)}, ...), condition=%wide.region_3.4_spmd, body=%wide.region_2.3_spmd.sunk | while | flops 312963072 | bytes 6588909 | solution.py:166
  352.2 2.0 collective-permute-start.3
  354.3 8.9 %collective-permute-done.3 = f32[3,4,48,128]{3,2,1,0:T(8,128)S(1)} collective-permute-done((f32[3,4,48,128]{3,2,1,0:T(8,128)S(1)}, f32[3,4,48,128]{3,2,1,0:T(8,128)S(1)}, u32[]{:S(2)}, u32[]{:S(2)}) %collective-permute-start.3) | collective-permute-done | bytes 294944 | tf_op jit(solution)/shard_map/while/body/eval_jaxpr/ppermute | solution.py:30
  366.1 5.5 %collective-permute-done.5 = f32[3,1,48,128]{3,2,1,0:T(8,128)S(1)} collective-permute-done((f32[3,1,48,128]{3,2,1,0:T(8,128)S(1)}, f32[3,1,48,128]{3,2,1,0:T(8,128)S(1)}, u32[]{:S(2)}, u32[]{:S(2)}) %collective-permute-start.5) | collective-permute-done | bytes 73760 | tf_op jit(solution)/shard_map/while/body/eval_jaxpr/ppermute | solution.py:19
  372.5 1.9 collective-permute-start.3
  374.5 8.7 %collective-permute-done.3 = f32[3,4,48,128]{3,2,1,0:T(8,128)S(1)} collective-permute-done((f32[3,4,48,128]{3,2,1,0:T(8,128)S(1)}, f32[3,4,48,128]{3,2,1,0:T(8,128)S(1)}, u32[]{:S(2)}, u32[]{:S(2)}) %collective-permute-start.3) | collective-permute-done | bytes 294944 | tf_op jit(solution)/shard_map/while/body/eval_jaxpr/ppermute | solution.py:30
  386.1 5.5 %collective-permute-done.5 = f32[3,1,48,128]{3,2,1,0:T(8,128)S(1)} collective-permute-done((f32[3,1,48,128]{3,2,1,0:T(8,128)S(1)}, f32[3,1,48,128]{3,2,1,0:T(8,128)S(1)}, u32[]{:S(2)}, u32[]{:S(2)}) %collective-permute-start.5) | collective-permute-done | bytes 73760 | tf_op jit(solution)/shard_map/while/body/eval_jaxpr/ppermute | solution.py:19
  392.5 1.9 collective-permute-start.3
  394.5 8.7 %collective-permute-done.3 = f32[3,4,48,128]{3,2,1,0:T(8,128)S(1)} collective-permute-done((f32[3,4,48,128]{3,2,1,0:T(8,128)S(1)}, f32[3,4,48,128]{3,2,1,0:T(8,128)S(1)}, u32[]{:S(2)}, u32[]{:S(2)}) %collective-permute-start.3) | collective-permute-done | bytes 294944 | tf_op jit(solution)/shard_map/while/body/eval_jaxpr/ppermute | solution.py:30
  406.1 5.5 %collective-permute-done.5 = f32[3,1,48,128]{3,2,1,0:T(8,128)S(1)} collective-permute-done((f32[3,1,48,128]{3,2,1,0:T(8,128)S(1)}, f32[3,1,48,128]{3,2,1,0:T(8,128)S(1)}, u32[]{:S(2)}, u32[]{:S(2)}) %collective-permute-start.5) | collective-permute-done | bytes 73760 | tf_op jit(solution)/shard_map/while/body/eval_jaxpr/ppermute | solution.py:19
  412.5 1.9 collective-permute-start.3
  414.5 8.7 %collective-permute-done.3 = f32[3,4,48,128]{3,2,1,0:T(8,128)S(1)} collective-permute-done((f32[3,4,48,128]{3,2,1,0:T(8,128)S(1)}, f32[3,4,48,128]{3,2,1,0:T(8,128)S(1)}, u32[]{:S(2)}, u32[]{:S(2)}) %collective-permute-start.3) | collective-permute-done | bytes 294944 | tf_op jit(solution)/shard_map/while/body/eval_jaxpr/ppermute | solution.py:30
  426.1 5.5 %collective-permute-done.5 = f32[3,1,48,128]{3,2,1,0:T(8,128)S(1)} collective-permute-done((f32[3,1,48,128]{3,2,1,0:T(8,128)S(1)}, f32[3,1,48,128]{3,2,1,0:T(8,128)S(1)}, u32[]{:S(2)}, u32[]{:S(2)}) %collective-permute-start.5) | collective-permute-done | bytes 73760 | tf_op jit(solution)/shard_map/while/body/eval_jaxpr/ppermute | solution.py:19
  432.5 1.9 collective-permute-start.3
  434.5 8.7 %collective-permute-done.3 = f32[3,4,48,128]{3,2,1,0:T(8,128)S(1)} collective-permute-done((f32[3,4,48,128]{3,2,1,0:T(8,128)S(1)}, f32[3,4,48,128]{3,2,1,0:T(8,128)S(1)}, u32[]{:S(2)}, u32[]{:S(2)}) %collective-permute-start.3) | collective-permute-done | bytes 294944 | tf_op jit(solution)/shard_map/while/body/eval_jaxpr/ppermute | solution.py:30
  446.1 5.5 %collective-permute-done.5 = f32[3,1,48,128]{3,2,1,0:T(8,128)S(1)} collective-permute-done((f32[3,1,48,128]{3,2,1,0:T(8,128)S(1)}, f32[3,1,48,128]{3,2,1,0:T(8,128)S(1)}, u32[]{:S(2)}, u32[]{:S(2)}) %collective-permute-start.5) | collective-permute-done | bytes 73760 | tf_op jit(solution)/shard_map/while/body/eval_jaxpr/ppermute | solution.py:19
  454.5 8.7 %collective-permute-done.3 = f32[3,4,48,128]{3,2,1,0:T(8,128)S(1)} collective-permute-done((f32[3,4,48,128]{3,2,1,0:T(8,128)S(1)}, f32[3,4,48,128]{3,2,1,0:T(8,128)S(1)}, u32[]{:S(2)}, u32[]{:S(2)}) %collective-permute-start.3) | collective-permute-done | bytes 294944 | tf_op jit(solution)/shard_map/while/body/eval_jaxpr/ppermute | solution.py:30
  466.1 5.5 %collective-permute-done.5 = f32[3,1,48,128]{3,2,1,0:T(8,128)S(1)} collective-permute-done((f32[3,1,48,128]{3,2,1,0:T(8,128)S(1)}, f32[3,1,48,128]{3,2,1,0:T(8,128)S(1)}, u32[]{:S(2)}, u32[]{:S(2)}) %collective-permute-start.5) | collective-permute-done | bytes 73760 | tf_op jit(solution)/shard_map/while/body/eval_jaxpr/ppermute | solution.py:19
  472.5 1.9 collective-permute-start.3
  474.5 8.7 %collective-permute-done.3 = f32[3,4,48,128]{3,2,1,0:T(8,128)S(1)} collective-permute-done((f32[3,4,48,128]{3,2,1,0:T(8,128)S(1)}, f32[3,4,48,128]{3,2,1,0:T(8,128)S(1)}, u32[]{:S(2)}, u32[]{:S(2)}) %collective-permute-start.3) | collective-permute-done | bytes 294944 | tf_op jit(solution)/shard_map/while/body/eval_jaxpr/ppermute | solution.py:30
  486.1 5.5 %collective-permute-done.5 = f32[3,1,48,128]{3,2,1,0:T(8,128)S(1)} collective-permute-done((f32[3,1,48,128]{3,2,1,0:T(8,128)S(1)}, f32[3,1,48,128]{3,2,1,0:T(8,128)S(1)}, u32[]{:S(2)}, u32[]{:S(2)}) %collective-permute-start.5) | collective-permute-done | bytes 73760 | tf_op jit(solution)/shard_map/while/body/eval_jaxpr/ppermute | solution.py:19
  494.5 8.7 %collective-permute-done.3 = f32[3,4,48,128]{3,2,1,0:T(8,128)S(1)} collective-permute-done((f32[3,4,48,128]{3,2,1,0:T(8,128)S(1)}, f32[3,4,48,128]{3,2,1,0:T(8,128)S(1)}, u32[]{:S(2)}, u32[]{:S(2)}) %collective-permute-start.3) | collective-permute-done | bytes 294944 | tf_op jit(solution)/shard_map/while/body/eval_jaxpr/ppermute | solution.py:30
  506.1 5.5 %collective-permute-done.5 = f32[3,1,48,128]{3,2,1,0:T(8,128)S(1)} collective-permute-done((f32[3,1,48,128]{3,2,1,0:T(8,128)S(1)}, f32[3,1,48,128]{3,2,1,0:T(8,128)S(1)}, u32[]{:S(2)}, u32[]{:S(2)}) %collective-permute-start.5) | collective-permute-done | bytes 73760 | tf_op jit(solution)/shard_map/while/body/eval_jaxpr/ppermute | solution.py:19
  (462 shorter events, 156.8 us)
Async XLA Ops:
  3.8 14.1 %collective-permute-start.6 = (f32[3,1,96,256]{3,2,1,0:T(8,128)S(1)}, f32[3,1,96,256]{3,2,1,0:T(8,128)S(1)}, u32[]{:S(2)}, u32[]{:S(2)}) collective-permute-start(f32[3,1,96,256]{3,2,1,0:T(8,128)S(1)} %get-tuple-element.233), channel_id=1, source_target_pairs={{1,0},{2,1},{3,2},{4,3},{5,4},{6,5},{7,6},{8,7},{9,8},{10,9},{11,1... | collective-permute-start | bytes 884744 | tf_op jit(solution)/shard_map/ppermute | solution.py:22
  8.8 9.8 %collective-permute-start.7 = (f32[3,1,96,256]{3,2,1,0:T(8,128)S(1)}, f32[3,1,96,256]{3,2,1,0:T(8,128)S(1)}, u32[]{:S(2)}, u32[]{:S(2)}) collective-permute-start(f32[3,1,96,256]{3,2,1,0:T(8,128)S(1)} %get-tuple-element.232), channel_id=1, source_target_pairs={{0,1},{1,2},{2,3},{3,4},{4,5},{5,6},{6,7},{7,8},{8,9},{9,10},{10,1... | collective-permute-start | bytes 884744 | tf_op jit(solution)/shard_map/ppermute | solution.py:19
  10.3 39.9 %collective-permute-start.12 = (f32[3,1,48,128]{3,2,1,0:T(8,128)}, f32[3,1,48,128]{3,2,1,0:T(8,128)}, u32[]{:S(2)}, u32[]{:S(2)}) collective-permute-start(f32[3,1,48,128]{3,2,1,0:T(8,128)} %get-tuple-element.241), channel_id=1, source_target_pairs={{1,0},{2,1},{3,2},{4,3},{5,4},{6,5},{7,6},{8,7},{9,8},{10,9},{11,1... | collective-permute-start | bytes 221192 | tf_op jit(solution)/shard_map/ppermute | solution.py:22
  15.7 34.5 %collective-permute-start.13 = (f32[3,1,48,128]{3,2,1,0:T(8,128)}, f32[3,1,48,128]{3,2,1,0:T(8,128)}, u32[]{:S(2)}, u32[]{:S(2)}) collective-permute-start(f32[3,1,48,128]{3,2,1,0:T(8,128)} %get-tuple-element.240), channel_id=1, source_target_pairs={{0,1},{1,2},{2,3},{3,4},{4,5},{5,6},{6,7},{7,8},{8,9},{9,10},{10,1... | collective-permute-start | bytes 221192 | tf_op jit(solution)/shard_map/ppermute | solution.py:19
  27.1 9.4 %collective-permute-start.8 = (f32[3,1,96,256]{3,2,1,0:T(8,128)}, f32[3,1,96,256]{3,2,1,0:T(8,128)}, u32[]{:S(2)}, u32[]{:S(2)}) collective-permute-start(f32[3,1,96,256]{3,2,1,0:T(8,128)} %get-tuple-element.229), channel_id=1, source_target_pairs={{1,0},{2,1},{3,2},{4,3},{5,4},{6,5},{7,6},{8,7},{9,8},{10,9},{11,1... | collective-permute-start | bytes 884744 | tf_op jit(solution)/shard_map/ppermute | solution.py:22
  31.9 10.6 %collective-permute-start.9 = (f32[3,1,96,256]{3,2,1,0:T(8,128)}, f32[3,1,96,256]{3,2,1,0:T(8,128)}, u32[]{:S(2)}, u32[]{:S(2)}) collective-permute-start(f32[3,1,96,256]{3,2,1,0:T(8,128)} %get-tuple-element.228), channel_id=1, source_target_pairs={{0,1},{1,2},{2,3},{3,4},{4,5},{5,6},{6,7},{7,8},{8,9},{9,10},{10,1... | collective-permute-start | bytes 884744 | tf_op jit(solution)/shard_map/ppermute | solution.py:19
  49.5 4.3 collective-permute-start.10
  49.6 10.0 %collective-permute-start.11 = (f32[3,1,96,256]{3,2,1,0:T(8,128)S(1)}, f32[3,1,96,256]{3,2,1,0:T(8,128)S(1)}, u32[]{:S(2)}, u32[]{:S(2)}) collective-permute-start(f32[3,1,96,256]{3,2,1,0:T(8,128)S(1)} %get-tuple-element.224), channel_id=1, source_target_pairs={{0,1},{1,2},{2,3},{3,4},{4,5},{5,6},{6,7},{7,8},{8,9},{9,10},{10,1... | collective-permute-start | bytes 884744 | tf_op jit(solution)/shard_map/ppermute | solution.py:19
  63.5 11.8 %collective-permute-start = (f32[3,4,48,128]{3,2,1,0:T(8,128)}, f32[3,4,48,128]{3,2,1,0:T(8,128)}, u32[]{:S(2)}, u32[]{:S(2)}) collective-permute-start(f32[3,4,48,128]{3,2,1,0:T(8,128)} %get-tuple-element.444), channel_id=1, source_target_pairs={{0,16},{16,32},{32,48},{48,64},{64,80},{80,96},{96,112},{1,17},{17... | collective-permute-start | bytes 884744 | tf_op jit(solution)/shard_map/while/body/eval_jaxpr/ppermute | solution.py:30
  77.3 7.5 %collective-permute-start.2 = (f32[3,1,48,128]{3,2,1,0:T(8,128)S(1)}, f32[3,1,48,128]{3,2,1,0:T(8,128)S(1)}, u32[]{:S(2)}, u32[]{:S(2)}) collective-permute-start(f32[3,1,48,128]{3,2,1,0:T(8,128)S(1)} %get-tuple-element.410), channel_id=1, source_target_pairs={{0,1},{1,2},{2,3},{3,4},{4,5},{5,6},{6,7},{7,8},{8,9},{9,10},{10,1... | collective-permute-start | bytes 221192 | tf_op jit(solution)/shard_map/while/body/eval_jaxpr/ppermute | solution.py:19
  86.4 11.1 %collective-permute-start = (f32[3,4,48,128]{3,2,1,0:T(8,128)}, f32[3,4,48,128]{3,2,1,0:T(8,128)}, u32[]{:S(2)}, u32[]{:S(2)}) collective-permute-start(f32[3,4,48,128]{3,2,1,0:T(8,128)} %get-tuple-element.444), channel_id=1, source_target_pairs={{0,16},{16,32},{32,48},{48,64},{64,80},{80,96},{96,112},{1,17},{17... | collective-permute-start | bytes 884744 | tf_op jit(solution)/shard_map/while/body/eval_jaxpr/ppermute | solution.py:30
  99.4 2.1 collective-permute-start.1
  99.5 7.5 %collective-permute-start.2 = (f32[3,1,48,128]{3,2,1,0:T(8,128)S(1)}, f32[3,1,48,128]{3,2,1,0:T(8,128)S(1)}, u32[]{:S(2)}, u32[]{:S(2)}) collective-permute-start(f32[3,1,48,128]{3,2,1,0:T(8,128)S(1)} %get-tuple-element.410), channel_id=1, source_target_pairs={{0,1},{1,2},{2,3},{3,4},{4,5},{5,6},{6,7},{7,8},{8,9},{9,10},{10,1... | collective-permute-start | bytes 221192 | tf_op jit(solution)/shard_map/while/body/eval_jaxpr/ppermute | solution.py:19
  108.6 11.1 %collective-permute-start = (f32[3,4,48,128]{3,2,1,0:T(8,128)}, f32[3,4,48,128]{3,2,1,0:T(8,128)}, u32[]{:S(2)}, u32[]{:S(2)}) collective-permute-start(f32[3,4,48,128]{3,2,1,0:T(8,128)} %get-tuple-element.444), channel_id=1, source_target_pairs={{0,16},{16,32},{32,48},{48,64},{64,80},{80,96},{96,112},{1,17},{17... | collective-permute-start | bytes 884744 | tf_op jit(solution)/shard_map/while/body/eval_jaxpr/ppermute | solution.py:30
  121.6 2.1 collective-permute-start.1
  121.7 7.5 %collective-permute-start.2 = (f32[3,1,48,128]{3,2,1,0:T(8,128)S(1)}, f32[3,1,48,128]{3,2,1,0:T(8,128)S(1)}, u32[]{:S(2)}, u32[]{:S(2)}) collective-permute-start(f32[3,1,48,128]{3,2,1,0:T(8,128)S(1)} %get-tuple-element.410), channel_id=1, source_target_pairs={{0,1},{1,2},{2,3},{3,4},{4,5},{5,6},{6,7},{7,8},{8,9},{9,10},{10,1... | collective-permute-start | bytes 221192 | tf_op jit(solution)/shard_map/while/body/eval_jaxpr/ppermute | solution.py:19
  130.8 11.0 %collective-permute-start = (f32[3,4,48,128]{3,2,1,0:T(8,128)}, f32[3,4,48,128]{3,2,1,0:T(8,128)}, u32[]{:S(2)}, u32[]{:S(2)}) collective-permute-start(f32[3,4,48,128]{3,2,1,0:T(8,128)} %get-tuple-element.444), channel_id=1, source_target_pairs={{0,16},{16,32},{32,48},{48,64},{64,80},{80,96},{96,112},{1,17},{17... | collective-permute-start | bytes 884744 | tf_op jit(solution)/shard_map/while/body/eval_jaxpr/ppermute | solution.py:30
  143.7 2.1 collective-permute-start.1
  143.8 7.5 %collective-permute-start.2 = (f32[3,1,48,128]{3,2,1,0:T(8,128)S(1)}, f32[3,1,48,128]{3,2,1,0:T(8,128)S(1)}, u32[]{:S(2)}, u32[]{:S(2)}) collective-permute-start(f32[3,1,48,128]{3,2,1,0:T(8,128)S(1)} %get-tuple-element.410), channel_id=1, source_target_pairs={{0,1},{1,2},{2,3},{3,4},{4,5},{5,6},{6,7},{7,8},{8,9},{9,10},{10,1... | collective-permute-start | bytes 221192 | tf_op jit(solution)/shard_map/while/body/eval_jaxpr/ppermute | solution.py:19
  152.9 11.0 %collective-permute-start = (f32[3,4,48,128]{3,2,1,0:T(8,128)}, f32[3,4,48,128]{3,2,1,0:T(8,128)}, u32[]{:S(2)}, u32[]{:S(2)}) collective-permute-start(f32[3,4,48,128]{3,2,1,0:T(8,128)} %get-tuple-element.444), channel_id=1, source_target_pairs={{0,16},{16,32},{32,48},{48,64},{64,80},{80,96},{96,112},{1,17},{17... | collective-permute-start | bytes 884744 | tf_op jit(solution)/shard_map/while/body/eval_jaxpr/ppermute | solution.py:30
  165.8 2.1 collective-permute-start.1
  165.9 7.5 %collective-permute-start.2 = (f32[3,1,48,128]{3,2,1,0:T(8,128)S(1)}, f32[3,1,48,128]{3,2,1,0:T(8,128)S(1)}, u32[]{:S(2)}, u32[]{:S(2)}) collective-permute-start(f32[3,1,48,128]{3,2,1,0:T(8,128)S(1)} %get-tuple-element.410), channel_id=1, source_target_pairs={{0,1},{1,2},{2,3},{3,4},{4,5},{5,6},{6,7},{7,8},{8,9},{9,10},{10,1... | collective-permute-start | bytes 221192 | tf_op jit(solution)/shard_map/while/body/eval_jaxpr/ppermute | solution.py:19
  175.0 11.0 %collective-permute-start = (f32[3,4,48,128]{3,2,1,0:T(8,128)}, f32[3,4,48,128]{3,2,1,0:T(8,128)}, u32[]{:S(2)}, u32[]{:S(2)}) collective-permute-start(f32[3,4,48,128]{3,2,1,0:T(8,128)} %get-tuple-element.444), channel_id=1, source_target_pairs={{0,16},{16,32},{32,48},{48,64},{64,80},{80,96},{96,112},{1,17},{17... | collective-permute-start | bytes 884744 | tf_op jit(solution)/shard_map/while/body/eval_jaxpr/ppermute | solution.py:30
  188.0 7.5 %collective-permute-start.2 = (f32[3,1,48,128]{3,2,1,0:T(8,128)S(1)}, f32[3,1,48,128]{3,2,1,0:T(8,128)S(1)}, u32[]{:S(2)}, u32[]{:S(2)}) collective-permute-start(f32[3,1,48,128]{3,2,1,0:T(8,128)S(1)} %get-tuple-element.410), channel_id=1, source_target_pairs={{0,1},{1,2},{2,3},{3,4},{4,5},{5,6},{6,7},{7,8},{8,9},{9,10},{10,1... | collective-permute-start | bytes 221192 | tf_op jit(solution)/shard_map/while/body/eval_jaxpr/ppermute | solution.py:19
  197.0 11.0 %collective-permute-start = (f32[3,4,48,128]{3,2,1,0:T(8,128)}, f32[3,4,48,128]{3,2,1,0:T(8,128)}, u32[]{:S(2)}, u32[]{:S(2)}) collective-permute-start(f32[3,4,48,128]{3,2,1,0:T(8,128)} %get-tuple-element.444), channel_id=1, source_target_pairs={{0,16},{16,32},{32,48},{48,64},{64,80},{80,96},{96,112},{1,17},{17... | collective-permute-start | bytes 884744 | tf_op jit(solution)/shard_map/while/body/eval_jaxpr/ppermute | solution.py:30
  210.0 2.1 collective-permute-start.1
  210.0 7.5 %collective-permute-start.2 = (f32[3,1,48,128]{3,2,1,0:T(8,128)S(1)}, f32[3,1,48,128]{3,2,1,0:T(8,128)S(1)}, u32[]{:S(2)}, u32[]{:S(2)}) collective-permute-start(f32[3,1,48,128]{3,2,1,0:T(8,128)S(1)} %get-tuple-element.410), channel_id=1, source_target_pairs={{0,1},{1,2},{2,3},{3,4},{4,5},{5,6},{6,7},{7,8},{8,9},{9,10},{10,1... | collective-permute-start | bytes 221192 | tf_op jit(solution)/shard_map/while/body/eval_jaxpr/ppermute | solution.py:19
  219.1 11.0 %collective-permute-start = (f32[3,4,48,128]{3,2,1,0:T(8,128)}, f32[3,4,48,128]{3,2,1,0:T(8,128)}, u32[]{:S(2)}, u32[]{:S(2)}) collective-permute-start(f32[3,4,48,128]{3,2,1,0:T(8,128)} %get-tuple-element.444), channel_id=1, source_target_pairs={{0,16},{16,32},{32,48},{48,64},{64,80},{80,96},{96,112},{1,17},{17... | collective-permute-start | bytes 884744 | tf_op jit(solution)/shard_map/while/body/eval_jaxpr/ppermute | solution.py:30
  232.1 2.1 collective-permute-start.1
  232.1 7.5 %collective-permute-start.2 = (f32[3,1,48,128]{3,2,1,0:T(8,128)S(1)}, f32[3,1,48,128]{3,2,1,0:T(8,128)S(1)}, u32[]{:S(2)}, u32[]{:S(2)}) collective-permute-start(f32[3,1,48,128]{3,2,1,0:T(8,128)S(1)} %get-tuple-element.410), channel_id=1, source_target_pairs={{0,1},{1,2},{2,3},{3,4},{4,5},{5,6},{6,7},{7,8},{8,9},{9,10},{10,1... | collective-permute-start | bytes 221192 | tf_op jit(solution)/shard_map/while/body/eval_jaxpr/ppermute | solution.py:19
  249.9 13.6 %collective-permute-start.17 = (f32[3,1,96,256]{3,2,1,0:T(8,128)S(1)}, f32[3,1,96,256]{3,2,1,0:T(8,128)S(1)}, u32[]{:S(2)}, u32[]{:S(2)}) collective-permute-start(f32[3,1,96,256]{3,2,1,0:T(8,128)S(1)} %get-tuple-element.213), channel_id=1, source_target_pairs={{1,0},{2,1},{3,2},{4,3},{5,4},{6,5},{7,6},{8,7},{9,8},{10,9},{11,1... | collective-permute-start | bytes 884744 | tf_op jit(solution)/shard_map/ppermute | solution.py:22
  249.9 13.6 %collective-permute-start.18 = (f32[3,1,96,256]{3,2,1,0:T(8,128)S(1)}, f32[3,1,96,256]{3,2,1,0:T(8,128)S(1)}, u32[]{:S(2)}, u32[]{:S(2)}) collective-permute-start(f32[3,1,96,256]{3,2,1,0:T(8,128)S(1)} %get-tuple-element.212), channel_id=1, source_target_pairs={{0,1},{1,2},{2,3},{3,4},{4,5},{5,6},{6,7},{7,8},{8,9},{9,10},{10,1... | collective-permute-start | bytes 884744 | tf_op jit(solution)/shard_map/ppermute | solution.py:19
  250.6 16.5 %collective-permute-start.19 = (f32[3,1,96,256]{3,2,1,0:T(8,128)S(1)}, f32[3,1,96,256]{3,2,1,0:T(8,128)S(1)}, u32[]{:S(2)}, u32[]{:S(2)}) collective-permute-start(f32[3,1,96,256]{3,2,1,0:T(8,128)S(1)} %get-tuple-element.209), channel_id=1, source_target_pairs={{1,0},{2,1},{3,2},{4,3},{5,4},{6,5},{7,6},{8,7},{9,8},{10,9},{11,1... | collective-permute-start | bytes 884744 | tf_op jit(solution)/shard_map/ppermute | solution.py:22
  255.6 11.6 %collective-permute-start.20 = (f32[3,1,96,256]{3,2,1,0:T(8,128)S(1)}, f32[3,1,96,256]{3,2,1,0:T(8,128)S(1)}, u32[]{:S(2)}, u32[]{:S(2)}) collective-permute-start(f32[3,1,96,256]{3,2,1,0:T(8,128)S(1)} %get-tuple-element.208), channel_id=1, source_target_pairs={{0,1},{1,2},{2,3},{3,4},{4,5},{5,6},{6,7},{7,8},{8,9},{9,10},{10,1... | collective-permute-start | bytes 884744 | tf_op jit(solution)/shard_map/ppermute | solution.py:19
  258.1 10.5 %collective-permute-start.21 = (f32[3,1,96,256]{3,2,1,0:T(8,128)S(1)}, f32[3,1,96,256]{3,2,1,0:T(8,128)S(1)}, u32[]{:S(2)}, u32[]{:S(2)}) collective-permute-start(f32[3,1,96,256]{3,2,1,0:T(8,128)S(1)} %get-tuple-element.221), channel_id=1, source_target_pairs={{1,0},{2,1},{3,2},{4,3},{5,4},{6,5},{7,6},{8,7},{9,8},{10,9},{11,1... | collective-permute-start | bytes 884744 | tf_op jit(solution)/shard_map/ppermute | solution.py:22
  263.5 9.8 %collective-permute-start.22 = (f32[3,1,96,256]{3,2,1,0:T(8,128)S(1)}, f32[3,1,96,256]{3,2,1,0:T(8,128)S(1)}, u32[]{:S(2)}, u32[]{:S(2)}) collective-permute-start(f32[3,1,96,256]{3,2,1,0:T(8,128)S(1)} %get-tuple-element.220), channel_id=1, source_target_pairs={{0,1},{1,2},{2,3},{3,4},{4,5},{5,6},{6,7},{7,8},{8,9},{9,10},{10,1... | collective-permute-start | bytes 884744 | tf_op jit(solution)/shard_map/ppermute | solution.py:19
  264.9 31.4 %collective-permute-start.14 = (f32[3,4,96,256]{3,2,1,0:T(8,128)S(1)}, f32[3,4,96,256]{3,2,1,0:T(8,128)S(1)}, u32[]{:S(2)}, u32[]{:S(2)}) collective-permute-start(f32[3,4,96,256]{3,2,1,0:T(8,128)S(1)} %pad_add_fusion.2), channel_id=1, source_target_pairs={{0,16},{16,32},{32,48},{48,64},{64,80},{80,96},{96,112},{1,17},{17... | collective-permute-start | bytes 3538952 | tf_op jit(solution)/shard_map/ppermute | solution.py:30
  299.4 8.9 %collective-permute-start.15 = (f32[3,1,96,256]{3,2,1,0:T(8,128)S(1)}, f32[3,1,96,256]{3,2,1,0:T(8,128)S(1)}, u32[]{:S(2)}, u32[]{:S(2)}) collective-permute-start(f32[3,1,96,256]{3,2,1,0:T(8,128)S(1)} %get-tuple-element.217), channel_id=1, source_target_pairs={{1,0},{2,1},{3,2},{4,3},{5,4},{6,5},{7,6},{8,7},{9,8},{10,9},{11,1... | collective-permute-start | bytes 884744 | tf_op jit(solution)/shard_map/ppermute | solution.py:22
  304.0 10.2 %collective-permute-start.16 = (f32[3,1,96,256]{3,2,1,0:T(8,128)S(1)}, f32[3,1,96,256]{3,2,1,0:T(8,128)S(1)}, u32[]{:S(2)}, u32[]{:S(2)}) collective-permute-start(f32[3,1,96,256]{3,2,1,0:T(8,128)S(1)} %get-tuple-element.216), channel_id=1, source_target_pairs={{0,1},{1,2},{2,3},{3,4},{4,5},{5,6},{6,7},{7,8},{8,9},{9,10},{10,1... | collective-permute-start | bytes 884744 | tf_op jit(solution)/shard_map/ppermute | solution.py:19
  321.4 5.8 %collective-permute-start.23 = (f32[3,1,96,256]{3,2,1,0:T(8,128)S(1)}, f32[3,1,96,256]{3,2,1,0:T(8,128)S(1)}, u32[]{:S(2)}, u32[]{:S(2)}) collective-permute-start(f32[3,1,96,256]{3,2,1,0:T(8,128)S(1)} %get-tuple-element.205), channel_id=1, source_target_pairs={{1,0},{2,1},{3,2},{4,3},{5,4},{6,5},{7,6},{8,7},{9,8},{10,9},{11,1... | collective-permute-start | bytes 884744 | tf_op jit(solution)/shard_map/ppermute | solution.py:22
  321.5 9.8 %collective-permute-start.24 = (f32[3,1,96,256]{3,2,1,0:T(8,128)S(1)}, f32[3,1,96,256]{3,2,1,0:T(8,128)S(1)}, u32[]{:S(2)}, u32[]{:S(2)}) collective-permute-start(f32[3,1,96,256]{3,2,1,0:T(8,128)S(1)} %get-tuple-element.204), channel_id=1, source_target_pairs={{0,1},{1,2},{2,3},{3,4},{4,5},{5,6},{6,7},{7,8},{8,9},{9,10},{10,1... | collective-permute-start | bytes 884744 | tf_op jit(solution)/shard_map/ppermute | solution.py:19
  322.0 16.9 %collective-permute-start.27 = (f32[3,1,48,128]{3,2,1,0:T(8,128)S(1)}, f32[3,1,48,128]{3,2,1,0:T(8,128)S(1)}, u32[]{:S(2)}, u32[]{:S(2)}) collective-permute-start(f32[3,1,48,128]{3,2,1,0:T(8,128)S(1)} %get-tuple-element.237), channel_id=1, source_target_pairs={{1,0},{2,1},{3,2},{4,3},{5,4},{6,5},{7,6},{8,7},{9,8},{10,9},{11,1... | collective-permute-start | bytes 221192 | tf_op jit(solution)/shard_map/ppermute | solution.py:22
  327.0 11.9 %collective-permute-start.28 = (f32[3,1,48,128]{3,2,1,0:T(8,128)S(1)}, f32[3,1,48,128]{3,2,1,0:T(8,128)S(1)}, u32[]{:S(2)}, u32[]{:S(2)}) collective-permute-start(f32[3,1,48,128]{3,2,1,0:T(8,128)S(1)} %get-tuple-element.236), channel_id=1, source_target_pairs={{0,1},{1,2},{2,3},{3,4},{4,5},{5,6},{6,7},{7,8},{8,9},{9,10},{10,1... | collective-permute-start | bytes 221192 | tf_op jit(solution)/shard_map/ppermute | solution.py:19
  337.3 5.6 %collective-permute-start.25 = (f32[3,1,96,256]{3,2,1,0:T(8,128)S(1)}, f32[3,1,96,256]{3,2,1,0:T(8,128)S(1)}, u32[]{:S(2)}, u32[]{:S(2)}) collective-permute-start(f32[3,1,96,256]{3,2,1,0:T(8,128)S(1)} %get-tuple-element.201), channel_id=1, source_target_pairs={{1,0},{2,1},{3,2},{4,3},{5,4},{6,5},{7,6},{8,7},{9,8},{10,9},{11,1... | collective-permute-start | bytes 884744 | tf_op jit(solution)/shard_map/ppermute | solution.py:22
  338.7 10.0 %collective-permute-start.26 = (f32[3,1,96,256]{3,2,1,0:T(8,128)S(1)}, f32[3,1,96,256]{3,2,1,0:T(8,128)S(1)}, u32[]{:S(2)}, u32[]{:S(2)}) collective-permute-start(f32[3,1,96,256]{3,2,1,0:T(8,128)S(1)} %get-tuple-element.200), channel_id=1, source_target_pairs={{0,1},{1,2},{2,3},{3,4},{4,5},{5,6},{6,7},{7,8},{8,9},{9,10},{10,1... | collective-permute-start | bytes 884744 | tf_op jit(solution)/shard_map/ppermute | solution.py:19
  352.2 11.0 %collective-permute-start.3 = (f32[3,4,48,128]{3,2,1,0:T(8,128)S(1)}, f32[3,4,48,128]{3,2,1,0:T(8,128)S(1)}, u32[]{:S(2)}, u32[]{:S(2)}) collective-permute-start(f32[3,4,48,128]{3,2,1,0:T(8,128)S(1)} %get-tuple-element.491), channel_id=1, source_target_pairs={{0,16},{16,32},{32,48},{48,64},{64,80},{80,96},{96,112},{1,17},{17... | collective-permute-start | bytes 884744 | tf_op jit(solution)/shard_map/while/body/eval_jaxpr/ppermute | solution.py:30
  364.1 7.5 %collective-permute-start.5 = (f32[3,1,48,128]{3,2,1,0:T(8,128)S(1)}, f32[3,1,48,128]{3,2,1,0:T(8,128)S(1)}, u32[]{:S(2)}, u32[]{:S(2)}) collective-permute-start(f32[3,1,48,128]{3,2,1,0:T(8,128)S(1)} %get-tuple-element.426), channel_id=1, source_target_pairs={{0,1},{1,2},{2,3},{3,4},{4,5},{5,6},{6,7},{7,8},{8,9},{9,10},{10,1... | collective-permute-start | bytes 221192 | tf_op jit(solution)/shard_map/while/body/eval_jaxpr/ppermute | solution.py:19
  372.5 10.7 %collective-permute-start.3 = (f32[3,4,48,128]{3,2,1,0:T(8,128)S(1)}, f32[3,4,48,128]{3,2,1,0:T(8,128)S(1)}, u32[]{:S(2)}, u32[]{:S(2)}) collective-permute-start(f32[3,4,48,128]{3,2,1,0:T(8,128)S(1)} %get-tuple-element.491), channel_id=1, source_target_pairs={{0,16},{16,32},{32,48},{48,64},{64,80},{80,96},{96,112},{1,17},{17... | collective-permute-start | bytes 884744 | tf_op jit(solution)/shard_map/while/body/eval_jaxpr/ppermute | solution.py:30
  384.0 2.1 collective-permute-start.4
  384.1 7.5 %collective-permute-start.5 = (f32[3,1,48,128]{3,2,1,0:T(8,128)S(1)}, f32[3,1,48,128]{3,2,1,0:T(8,128)S(1)}, u32[]{:S(2)}, u32[]{:S(2)}) collective-permute-start(f32[3,1,48,128]{3,2,1,0:T(8,128)S(1)} %get-tuple-element.426), channel_id=1, source_target_pairs={{0,1},{1,2},{2,3},{3,4},{4,5},{5,6},{6,7},{7,8},{8,9},{9,10},{10,1... | collective-permute-start | bytes 221192 | tf_op jit(solution)/shard_map/while/body/eval_jaxpr/ppermute | solution.py:19
  392.5 10.7 %collective-permute-start.3 = (f32[3,4,48,128]{3,2,1,0:T(8,128)S(1)}, f32[3,4,48,128]{3,2,1,0:T(8,128)S(1)}, u32[]{:S(2)}, u32[]{:S(2)}) collective-permute-start(f32[3,4,48,128]{3,2,1,0:T(8,128)S(1)} %get-tuple-element.491), channel_id=1, source_target_pairs={{0,16},{16,32},{32,48},{48,64},{64,80},{80,96},{96,112},{1,17},{17... | collective-permute-start | bytes 884744 | tf_op jit(solution)/shard_map/while/body/eval_jaxpr/ppermute | solution.py:30
  404.0 2.1 collective-permute-start.4
  404.1 7.5 %collective-permute-start.5 = (f32[3,1,48,128]{3,2,1,0:T(8,128)S(1)}, f32[3,1,48,128]{3,2,1,0:T(8,128)S(1)}, u32[]{:S(2)}, u32[]{:S(2)}) collective-permute-start(f32[3,1,48,128]{3,2,1,0:T(8,128)S(1)} %get-tuple-element.426), channel_id=1, source_target_pairs={{0,1},{1,2},{2,3},{3,4},{4,5},{5,6},{6,7},{7,8},{8,9},{9,10},{10,1... | collective-permute-start | bytes 221192 | tf_op jit(solution)/shard_map/while/body/eval_jaxpr/ppermute | solution.py:19
  412.5 10.7 %collective-permute-start.3 = (f32[3,4,48,128]{3,2,1,0:T(8,128)S(1)}, f32[3,4,48,128]{3,2,1,0:T(8,128)S(1)}, u32[]{:S(2)}, u32[]{:S(2)}) collective-permute-start(f32[3,4,48,128]{3,2,1,0:T(8,128)S(1)} %get-tuple-element.491), channel_id=1, source_target_pairs={{0,16},{16,32},{32,48},{48,64},{64,80},{80,96},{96,112},{1,17},{17... | collective-permute-start | bytes 884744 | tf_op jit(solution)/shard_map/while/body/eval_jaxpr/ppermute | solution.py:30
  424.0 2.1 collective-permute-start.4
  424.1 7.5 %collective-permute-start.5 = (f32[3,1,48,128]{3,2,1,0:T(8,128)S(1)}, f32[3,1,48,128]{3,2,1,0:T(8,128)S(1)}, u32[]{:S(2)}, u32[]{:S(2)}) collective-permute-start(f32[3,1,48,128]{3,2,1,0:T(8,128)S(1)} %get-tuple-element.426), channel_id=1, source_target_pairs={{0,1},{1,2},{2,3},{3,4},{4,5},{5,6},{6,7},{7,8},{8,9},{9,10},{10,1... | collective-permute-start | bytes 221192 | tf_op jit(solution)/shard_map/while/body/eval_jaxpr/ppermute | solution.py:19
  432.5 10.7 %collective-permute-start.3 = (f32[3,4,48,128]{3,2,1,0:T(8,128)S(1)}, f32[3,4,48,128]{3,2,1,0:T(8,128)S(1)}, u32[]{:S(2)}, u32[]{:S(2)}) collective-permute-start(f32[3,4,48,128]{3,2,1,0:T(8,128)S(1)} %get-tuple-element.491), channel_id=1, source_target_pairs={{0,16},{16,32},{32,48},{48,64},{64,80},{80,96},{96,112},{1,17},{17... | collective-permute-start | bytes 884744 | tf_op jit(solution)/shard_map/while/body/eval_jaxpr/ppermute | solution.py:30
  444.1 7.5 %collective-permute-start.5 = (f32[3,1,48,128]{3,2,1,0:T(8,128)S(1)}, f32[3,1,48,128]{3,2,1,0:T(8,128)S(1)}, u32[]{:S(2)}, u32[]{:S(2)}) collective-permute-start(f32[3,1,48,128]{3,2,1,0:T(8,128)S(1)} %get-tuple-element.426), channel_id=1, source_target_pairs={{0,1},{1,2},{2,3},{3,4},{4,5},{5,6},{6,7},{7,8},{8,9},{9,10},{10,1... | collective-permute-start | bytes 221192 | tf_op jit(solution)/shard_map/while/body/eval_jaxpr/ppermute | solution.py:19
  452.5 10.7 %collective-permute-start.3 = (f32[3,4,48,128]{3,2,1,0:T(8,128)S(1)}, f32[3,4,48,128]{3,2,1,0:T(8,128)S(1)}, u32[]{:S(2)}, u32[]{:S(2)}) collective-permute-start(f32[3,4,48,128]{3,2,1,0:T(8,128)S(1)} %get-tuple-element.491), channel_id=1, source_target_pairs={{0,16},{16,32},{32,48},{48,64},{64,80},{80,96},{96,112},{1,17},{17... | collective-permute-start | bytes 884744 | tf_op jit(solution)/shard_map/while/body/eval_jaxpr/ppermute | solution.py:30
  464.1 7.5 %collective-permute-start.5 = (f32[3,1,48,128]{3,2,1,0:T(8,128)S(1)}, f32[3,1,48,128]{3,2,1,0:T(8,128)S(1)}, u32[]{:S(2)}, u32[]{:S(2)}) collective-permute-start(f32[3,1,48,128]{3,2,1,0:T(8,128)S(1)} %get-tuple-element.426), channel_id=1, source_target_pairs={{0,1},{1,2},{2,3},{3,4},{4,5},{5,6},{6,7},{7,8},{8,9},{9,10},{10,1... | collective-permute-start | bytes 221192 | tf_op jit(solution)/shard_map/while/body/eval_jaxpr/ppermute | solution.py:19
  472.5 10.7 %collective-permute-start.3 = (f32[3,4,48,128]{3,2,1,0:T(8,128)S(1)}, f32[3,4,48,128]{3,2,1,0:T(8,128)S(1)}, u32[]{:S(2)}, u32[]{:S(2)}) collective-permute-start(f32[3,4,48,128]{3,2,1,0:T(8,128)S(1)} %get-tuple-element.491), channel_id=1, source_target_pairs={{0,16},{16,32},{32,48},{48,64},{64,80},{80,96},{96,112},{1,17},{17... | collective-permute-start | bytes 884744 | tf_op jit(solution)/shard_map/while/body/eval_jaxpr/ppermute | solution.py:30
  484.1 7.5 %collective-permute-start.5 = (f32[3,1,48,128]{3,2,1,0:T(8,128)S(1)}, f32[3,1,48,128]{3,2,1,0:T(8,128)S(1)}, u32[]{:S(2)}, u32[]{:S(2)}) collective-permute-start(f32[3,1,48,128]{3,2,1,0:T(8,128)S(1)} %get-tuple-element.426), channel_id=1, source_target_pairs={{0,1},{1,2},{2,3},{3,4},{4,5},{5,6},{6,7},{7,8},{8,9},{9,10},{10,1... | collective-permute-start | bytes 221192 | tf_op jit(solution)/shard_map/while/body/eval_jaxpr/ppermute | solution.py:19
  492.5 10.7 %collective-permute-start.3 = (f32[3,4,48,128]{3,2,1,0:T(8,128)S(1)}, f32[3,4,48,128]{3,2,1,0:T(8,128)S(1)}, u32[]{:S(2)}, u32[]{:S(2)}) collective-permute-start(f32[3,4,48,128]{3,2,1,0:T(8,128)S(1)} %get-tuple-element.491), channel_id=1, source_target_pairs={{0,16},{16,32},{32,48},{48,64},{64,80},{80,96},{96,112},{1,17},{17... | collective-permute-start | bytes 884744 | tf_op jit(solution)/shard_map/while/body/eval_jaxpr/ppermute | solution.py:30
  504.1 7.5 %collective-permute-start.5 = (f32[3,1,48,128]{3,2,1,0:T(8,128)S(1)}, f32[3,1,48,128]{3,2,1,0:T(8,128)S(1)}, u32[]{:S(2)}, u32[]{:S(2)}) collective-permute-start(f32[3,1,48,128]{3,2,1,0:T(8,128)S(1)} %get-tuple-element.426), channel_id=1, source_target_pairs={{0,1},{1,2},{2,3},{3,4},{4,5},{5,6},{6,7},{7,8},{8,9},{9,10},{10,1... | collective-permute-start | bytes 221192 | tf_op jit(solution)/shard_map/while/body/eval_jaxpr/ppermute | solution.py:19
  (89 other events, 689.3 us)
where the time goes:
time: 523 us; the launch traced here: 514 us
  waiting for transfers between devices  314 us (60%)
  matrix products  87.9 us (17%)
  starting transfers between devices  83.4 us (16%)
  other arithmetic  15.1 us (3%)
  local copies, waits for them, and re-layouts  10.5 us (2%)
    ppermute x17, waiting for transfers between devices, shifted(): return lax.ppermute(block, axis, route)  161 us
    ppermute x27, waiting for transfers between devices, with_halo(): lax.ppermute(lax.slice_in_dim(block, block.shape[dim] - width, None, axis...  121 us
    ppermute x27, starting transfers between devices, with_halo(): lax.ppermute(lax.slice_in_dim(block, 0, width, axis=dim), axis, backward)  37.9 us
    ppermute x17, starting transfers between devices, shifted(): return lax.ppermute(block, axis, route)  34.4 us
    ppermute x27, waiting for transfers between devices, with_halo(): lax.ppermute(lax.slice_in_dim(block, 0, width, axis=dim), axis, backward)  32.6 us
    dot_general x27, matrix products, to_modal(): return jnp.einsum('ir,...rj->...ij', forward_r, inner, precision=HI)  28.5 us
    dot_general x27, matrix products, to_modal(): inner = jnp.einsum('...rz,jz->...rj', field, forward_z, precision=HI)  22.9 us
    dot_general x27, matrix products, to_phys(): inner = jnp.einsum('...ij,zj->...iz', modes, backward_z, precision=HI)  18.9 us
  transfers between devices with their start and end apart: 71, of which 60 were waited for; matrix products, arithmetic and copies ran while one was open for 8% of the time, Pallas kernels for 0%

commit v1 on v0

v1 whole, which is shorter than its diff:
```python
import ml_dtypes
import numpy as np
import jax
import jax.numpy as jnp
from jax import lax
from jax.experimental import pallas as pl
from jax.experimental.pallas import tpu as pltpu
from jax.sharding import PartitionSpec as P

SLICES = 8
AZIMUTH = 64
RADIAL, AXIAL = 96, 256
RADIAL_C, AXIAL_C = 48, 128
BLOCKS = 16
UNITS = 96
STEP = 0.1
HALF = 0.05
F32 = jnp.float32
BF16 = jnp.bfloat16


def azimuth_transform():
    points = np.arange(AZIMUTH)
    rows = np.zeros((2, UNITS, 3, AZIMUTH))
    scalars = np.zeros((128, 4))
    for k in range(64):
        angle = 2.0 * np.pi * k / AZIMUTH
        cos, sin = np.cos(angle * points) / 8.0, np.sin(angle * points) / 8.0
        rows[0, k, 0], rows[0, k, 1] = cos, sin
        rows[1, k, 1], rows[1, k, 0] = cos, -sin
        second = 2.0 * np.cos(angle) - 2.0
        scalars[k] = (second, second, 2.0 * np.sin(angle), -2.0)
    rows[0, 64, 2] = 1.0 / 8.0
    rows[1, 64, 2] = (-1.0) ** points / 8.0
    scalars[64] = (0.0, -4.0, 0.0, 0.0)
    for k in range(1, 32):
        angle = 2.0 * np.pi * k / AZIMUTH
        rows[0, 64 + k, 2] = np.sqrt(2.0) * np.cos(angle * points) / 8.0
        rows[1, 64 + k, 2] = -np.sqrt(2.0) * np.sin(angle * points) / 8.0
        second = 2.0 * np.cos(angle) - 2.0
        scalars[64 + k] = (second, second, 2.0 * np.sin(angle), 0.0)
    matrix = rows.reshape(192, 3, BLOCKS, 4).transpose(0, 2, 1, 3).reshape(192, 192)
    return matrix, scalars.astype(np.float32)


def split_constant(matrix):
    single = matrix.astype(np.float32)
    high = single.astype(ml_dtypes.bfloat16)
    low = (single - high.astype(np.float32)).astype(ml_dtypes.bfloat16)
    return np.concatenate([high, high, low], axis=1)


TRANSFORM, SCALARS = azimuth_transform()
TO_UNITS = split_constant(TRANSFORM)
FROM_UNITS = split_constant(TRANSFORM.T.copy())


def split(value):
    high = value.astype(BF16)
    return high, (value - high.astype(F32)).astype(BF16)


def dot(left, right):
    return jnp.dot(left, right, preferred_element_type=F32)


def axial(value, weights):
    high, low = split(value)
    return dot(jnp.concatenate([high, low, high], axis=1), weights)


def radial(weights, value):
    high, low = split(value)
    return dot(weights, jnp.concatenate([high, low, high], axis=0))


def gather_kernel(initial_ref, forcing_ref, send_ref, block_ref, sem):
    tm = lax.axis_index("tm")
    rows = pl.ds(pl.multiple_of((tm % 4) * 24, 8), 24)

    @pl.when(tm < 4)
    def _():
        copy = pltpu.make_async_copy(initial_ref.at[:, rows, :], block_ref, sem)
        copy.start()
        copy.wait()

    @pl.when(tm >= 4)
    def _():
        copy = pltpu.make_async_copy(forcing_ref.at[:, rows, :], block_ref, sem)
        copy.start()
        copy.wait()

    for plane in range(12):
        for piece in range(6):
            half, row = piece // 3, (piece % 3) * 8
            values = block_ref[plane, row : row + 8, half * 128 : half * 128 + 128]
            group, first = piece // 2, (piece % 2) * 8
            send_ref[pl.ds(first * 40 + plane * 3 + group, 8, stride=40), :] = values


def to_units_kernel(transform_ref, received_ref, send_ref):
    columns = [received_ref[pl.ds(group, 192, stride=3), :] for group in range(3)]
    send_ref[UNITS * 8 :, :] = jnp.zeros((32 * 8, 128), F32)
    zero = jnp.zeros((UNITS, 128), F32)
    send_ref[pl.ds(6, UNITS, stride=8), :] = zero
    send_ref[pl.ds(7, UNITS, stride=8), :] = zero
    for group in range(3):
        units = radial(transform_ref[...], columns[group])
        for part in range(2):
            send_ref[pl.ds(part * 3 + group, UNITS, stride=8), :] = units[part * UNITS : (part + 1) * UNITS]


def column_of(row, size):
    at = lax.broadcasted_iota(jnp.int32, (size, size), 0) == lax.broadcasted_iota(jnp.int32, (size, size), 1)
    return jnp.sum(jnp.where(at, row, 0.0), axis=1, keepdims=True)


def identity_plus(value):
    size = value.shape[0]
    at = lax.broadcasted_iota(jnp.int32, (size, size), 0) == lax.broadcasted_iota(jnp.int32, (size, size), 1)
    return jnp.where(at, 1.0, 0.0) + value


def axial_weights(value):
    high, low = split(jnp.transpose(identity_plus(value)))
    return jnp.concatenate([high, high, low], axis=0)


def radial_weights(value):
    high, low = split(value)
    return jnp.concatenate([high, high, low], axis=1)


def units_kernel(
    scalars_ref,
    received_ref,
    forward_radial_ref,
    backward_radial_ref,
    forward_axial_ref,
    backward_axial_ref,
    forward_radial_c_ref,
    backward_radial_c_ref,
    forward_axial_c_ref,
    backward_axial_c_ref,
    decay_radial_ref,
    decay_axial_ref,
    advection_ref,
    diffusion_ref,
    out_ref,
    bz_ref,
    fz_ref,
    br_ref,
    fr_ref,
    bz_narrow_ref,
    br_narrow_ref,
    fz_narrow_ref,
    fr_narrow_ref,
    bzc_ref,
    fzc_ref,
    brc_ref,
    frc_ref,
    cross_ref,
    first_ref,
    second_ref,
    cross_c_ref,
    first_c_ref,
    second_c_ref,
    spectrum_ref,
    inverse_ref,
    inverse_c_ref,
    field_ref,
    coarse_ref,
    push_ref,
    ahead_ref,
    behind_ref,
    known_ref,
    const_ref,
    gain_ref,
):
    unit = lax.axis_index("tm") * BLOCKS + lax.axis_index("azim")
    scalar = [scalars_ref[unit, n] for n in range(4)]

    bz_ref[...] = axial_weights(backward_axial_ref[...])
    fz_ref[...] = axial_weights(forward_axial_ref[...])
    br_ref[...] = radial_weights(identity_plus(backward_radial_ref[...]))
    fr_ref[...] = radial_weights(identity_plus(forward_radial_ref[...]))
    bzc_ref[...] = axial_weights(backward_axial_c_ref[...])
    fzc_ref[...] = axial_weights(forward_axial_c_ref[...])
    brc_ref[...] = radial_weights(identity_plus(backward_radial_c_ref[...]))
    frc_ref[...] = radial_weights(identity_plus(forward_radial_c_ref[...]))
    for n in range(3):
        bz_narrow_ref[n * 128 : n * 128 + 128, :] = bz_ref[n * 256 : n * 256 + 128, :]
    fz_narrow_ref[...] = fz_ref[:, :128]
    fr_narrow_ref[...] = fr_ref[:48, :]
    br_narrow_ref[...] = radial_weights(identity_plus(backward_radial_ref[...])[:, :48])

    diffusion = column_of(diffusion_ref[...], RADIAL)
    cross_ref[...] = scalar[2] * advection_ref[...] + scalar[3]
    first_ref[...] = jnp.broadcast_to(scalar[0] * diffusion, (RADIAL, AXIAL))
    second_ref[...] = jnp.broadcast_to(scalar[1] * diffusion, (RADIAL, AXIAL))
    pick_lane = jnp.where(
        lax.broadcasted_iota(jnp.int32, (AXIAL, AXIAL_C), 0)
        == 2 * lax.broadcasted_iota(jnp.int32, (AXIAL, AXIAL_C), 1),
        1.0,
        0.0,
    )
    pick_row = jnp.where(
        lax.broadcasted_iota(jnp.int32, (RADIAL_C, RADIAL), 1)
        == 2 * lax.broadcasted_iota(jnp.int32, (RADIAL_C, RADIAL), 0),
        1.0,
        0.0,
    )
    exact = lax.Precision.HIGHEST
    advection_c = jnp.dot(
        jnp.dot(pick_row, advection_ref[...], precision=exact, preferred_element_type=F32),
        pick_lane,
        precision=exact,
        preferred_element_type=F32,
    )
    diffusion_c = jnp.sum(pick_row * diffusion_ref[...], axis=1, keepdims=True)
    cross_c_ref[...] = scalar[2] * advection_c + scalar[3]
    first_c_ref[...] = jnp.broadcast_to(scalar[0] * diffusion_c, (RADIAL_C, AXIAL_C))
    second_c_ref[...] = jnp.broadcast_to(scalar[1] * diffusion_c, (RADIAL_C, AXIAL_C))
    spectrum = -(column_of(decay_radial_ref[...], RADIAL) + decay_axial_ref[...])
    spectrum_ref[...] = spectrum
    inverse_ref[...] = 1.0 / (1.0 - HALF * spectrum)
    inverse_c_ref[...] = 1.0 / (1.0 - STEP * spectrum[:RADIAL_C, :AXIAL_C])

    for field in range(2):
        for part in range(2):
            for rows in range(4):
                source = (field * 4 + rows) * 16 * 8 + part * 3
                for piece in range(6):
                    half, row = piece // 3, (piece % 3) * 8
                    group, first = piece // 2, (piece % 2) * 8
                    field_ref[field, part, rows * 24 + row : rows * 24 + row + 8, half * 128 : half * 128 + 128] = (
                        received_ref[pl.ds(source + first * 8 + group, 8, stride=8), :]
                    )

    def forces(re, im, cross, first, second):
        return first * re - cross * im, second * im + cross * re

    def to_points(modes):
        inner = axial(modes.reshape(2 * RADIAL, AXIAL), bz_ref[...])
        return radial(br_ref[...], inner[:RADIAL]), radial(br_ref[...], inner[RADIAL:])

    def fine_forces(re, im):
        return forces(re, im, cross_ref[...], first_ref[...], second_ref[...])

    def to_modes(re, im):
        inner = axial(jnp.concatenate([re, im], axis=0), fz_ref[...])
        return jnp.stack([radial(fr_ref[...], inner[:RADIAL]), radial(fr_ref[...], inner[RADIAL:])])

    def explicit(modes):
        return to_modes(*fine_forces(*to_points(modes)))

    def explicit_of_coarse(modes):
        inner = axial(modes.reshape(2 * RADIAL_C, AXIAL_C), bz_narrow_ref[...])
        re, im = radial(br_narrow_ref[...], inner[:RADIAL_C]), radial(br_narrow_ref[...], inner[RADIAL_C:])
        return to_modes(*fine_forces(re, im))

    def restricted_explicit(modes):
        re, im = fine_forces(*to_points(modes))
        inner = jnp.concatenate([radial(fr_narrow_ref[...], re), radial(fr_narrow_ref[...], im)], axis=0)
        return axial(inner, fz_narrow_ref[...]).reshape(2, RADIAL_C, AXIAL_C)

    def coarse_explicit(modes):
        inner = axial(modes.reshape(2 * RADIAL_C, AXIAL_C), bzc_ref[...])
        both = radial(brc_ref[...], jnp.concatenate([inner[:RADIAL_C], inner[RADIAL_C:]], axis=1))
        re, im = forces(
            both[:, :AXIAL_C], both[:, AXIAL_C:], cross_c_ref[...], first_c_ref[...], second_c_ref[...]
        )
        both = radial(frc_ref[...], jnp.concatenate([re, im], axis=1))
        inner = jnp.concatenate([both[:, :AXIAL_C], both[:, AXIAL_C:]], axis=0)
        return axial(inner, fzc_ref[...]).reshape(2, RADIAL_C, AXIAL_C)

    def corner(value):
        return value[:, :RADIAL_C, :AXIAL_C]

    known_ref[0] = explicit(field_ref[0])
    spectrum = spectrum_ref[...]
    total0 = known_ref[0] + field_ref[1] + spectrum * field_ref[0]
    known_ref[3] = inverse_ref[...] * (field_ref[0] - HALF * spectrum * field_ref[0] + (0.5 * STEP) * total0)
    known_ref[1] = explicit(known_ref[3])
    known_ref[4] = inverse_ref[...] * (
        known_ref[3]
        + HALF * (known_ref[1] - known_ref[0])
        - HALF * spectrum_ref[...] * field_ref[0]
        + (0.5 * STEP) * (known_ref[0] + field_ref[1] + spectrum_ref[...] * field_ref[0])
    )
    known_ref[2] = explicit(known_ref[4])
    spectrum_c = spectrum_ref[:RADIAL_C, :AXIAL_C]
    coarse_known = [known_ref[n, :, :RADIAL_C, :AXIAL_C] for n in range(5)]
    start_c = field_ref[0, :, :RADIAL_C, :AXIAL_C]
    forcing_c = field_ref[1, :, :RADIAL_C, :AXIAL_C]
    gain_ref[0] = (
        STEP
        * (
            (coarse_known[0] + spectrum_c * start_c) / 6.0
            + (2.0 / 3.0) * (coarse_known[1] + spectrum_c * coarse_known[3])
            + (coarse_known[2] + spectrum_c * coarse_known[4]) / 6.0
            + forcing_c
        )
        - STEP * spectrum_c * coarse_known[4]
    )
    coarse_ref[0] = start_c
    coarse_ref[9] = coarse_known[4]
    coarse_ref[1] = inverse_c_ref[...] * (gain_ref[0] + start_c)

    def chain(n, carry):
        latest = coarse_ref[n]
        coarse_ref[n + 1] = inverse_c_ref[...] * (
            gain_ref[0] + latest + STEP * coarse_explicit(latest - coarse_ref[0])
        )
        return carry

    lax.fori_loop(1, SLICES, chain, 0)

    def spread(n, carry):
        state = coarse_ref[n]
        push = explicit_of_coarse(state)
        push_ref[n] = push[:, :RADIAL_C, :AXIAL_C]
        behind_ref[n] = (0.25 * HALF) * push
        ahead_ref[n] = (0.75 * HALF) * push
        damped = (0.25 * HALF) * spectrum_ref[:RADIAL_C, :AXIAL_C] * state
        behind_ref[n, :, :RADIAL_C, :AXIAL_C] = behind_ref[n, :, :RADIAL_C, :AXIAL_C] - damped
        ahead_ref[n, :, :RADIAL_C, :AXIAL_C] = ahead_ref[n, :, :RADIAL_C, :AXIAL_C] + damped + state
        return carry

    lax.fori_loop(0, SLICES + 2, spread, 0)

    def padded(value):
        return jnp.pad(value, ((0, 0), (0, RADIAL - RADIAL_C), (0, AXIAL - AXIAL_C)))

    spectrum = spectrum_ref[...]
    wide_start = padded(coarse_ref[0])
    wide_end = padded(coarse_ref[9])
    push_start = (ahead_ref[0] + behind_ref[0] - wide_start) * (1.0 / HALF)
    push_end = (ahead_ref[9] + behind_ref[9] - wide_end) * (1.0 / HALF)
    rhs_start = push_start + spectrum * wide_start
    rhs_end = push_end + spectrum * wide_end
    total0 = known_ref[0] + field_ref[1] + spectrum * field_ref[0]
    total1 = known_ref[1] + field_ref[1] + spectrum * known_ref[3]
    total2 = known_ref[2] + field_ref[1] + spectrum * known_ref[4]
    shared = -HALF * spectrum * (known_ref[3] - 0.5 * (wide_start + wide_end)) + STEP * (
        (5.0 / 24.0) * total0 + (1.0 / 3.0) * total1 - (1.0 / 24.0) * total2 - 0.375 * rhs_start - 0.125 * rhs_end
    )
    const_ref[0] = field_ref[0] - wide_start + shared
    const_ref[1] = known_ref[4] - wide_end + HALF * (known_ref[2] - push_end - known_ref[0] + push_start) + shared
    const_ref[2] = (
        -HALF * (known_ref[1] - 0.5 * (push_start + push_end))
        - HALF * spectrum * (known_ref[4] - wide_end)
        + STEP
        * (
            (-1.0 / 24.0) * total0
            + (1.0 / 3.0) * total1
            + (5.0 / 24.0) * total2
            - 0.125 * rhs_start
            - 0.375 * rhs_end
        )
    )
    gain_ref[8] = STEP * (forcing_c + (coarse_known[0] - push_ref[0]) / 6.0)
    gain_ref[9] = STEP * (forcing_c + (coarse_known[2] - push_ref[9]) / 6.0)

    def sweep(n, carry):
        later = jnp.minimum(n, 1)
        middle = inverse_ref[...] * (const_ref[later] + ahead_ref[n] + behind_ref[n + 1])
        middle_push = explicit(middle)
        ending = inverse_ref[...] * (middle + HALF * middle_push + const_ref[2] + behind_ref[n + 1] - behind_ref[n])
        ending_push = restricted_explicit(ending)
        spectrum_c = spectrum_ref[:RADIAL_C, :AXIAL_C]
        gain_ref[n] = (
            gain_ref[8 + later]
            + (STEP / 6.0) * (push_ref[n] + spectrum_c * coarse_ref[n])
            + (STEP * 2.0 / 3.0) * (corner(middle_push) + spectrum_c * corner(middle))
            + (STEP / 6.0) * ending_push
            - (STEP * 5.0 / 6.0) * spectrum_c * corner(ending)
        )
        for part in range(2):
            for half in range(2):
                for j in range(0 if half else 3, 6):
                    out_ref[n, pl.ds(part * 12 + half * 6 + j, 16, stride=24), :] = ending[
                        part, 16 * j : 16 * j + 16, half * 128 : half * 128 + 128
                    ]
        return carry

    lax.fori_loop(0, SLICES, sweep, 0)

    def place(n, state):
        for part in range(2):
            for j in range(3):
                out_ref[n, pl.ds(part * 12 + j, 16, stride=24), :] = state[part, 16 * j : 16 * j + 16, :]

    state = inverse_c_ref[...] * (gain_ref[0] + coarse_ref[0])
    place(0, state)

    def chain_again(n, state):
        after = inverse_c_ref[...] * (gain_ref[n] + state + STEP * coarse_explicit(state - coarse_ref[n]))
        place(n, after)
        return after

    lax.fori_loop(1, SLICES, chain_again, state)


def from_units_kernel(transform_ref, received_ref, send_ref):
    for pair in range(6):
        parts = []
        for part in range(2):
            parts.append(
                jnp.concatenate(
                    [received_ref[pl.ds(part * 12 + 2 * pair + n, UNITS, stride=24), :] for n in range(2)], axis=1
                )
            )
        planes = radial(transform_ref[...], jnp.concatenate(parts, axis=0))
        for n in range(2):
            send_ref[pl.ds(2 * pair + n, 192, stride=12), :] = planes[:, n * 128 : n * 128 + 128]


def place_kernel(received_ref, out_ref):
    for plane in range(12):
        for half in range(2):
            for j in range(6):
                out_ref[plane, 16 * j : 16 * j + 16, half * 128 : half * 128 + 128] = received_ref[
                    pl.ds(plane * 12 + half * 6 + j, 16, stride=144), :
                ]


VMEM = pl.BlockSpec(memory_space=pltpu.VMEM)
ANY = pl.BlockSpec(memory_space=pl.ANY)
SMEM = pl.BlockSpec(memory_space=pltpu.SMEM)
PARAMS = pltpu.CompilerParams(vmem_limit_bytes=48 << 20)


def array(*shape):
    return jax.ShapeDtypeStruct(shape, F32)


def exchange(value, axes, peers):
    rows = value.shape[0] // peers
    moved = lax.all_to_all(value.reshape(peers, rows, 128), axes, 0, 0)
    return moved.reshape(value.shape)


def per_device(
    initial_state,
    forcing,
    forward_radial,
    backward_radial,
    forward_axial,
    backward_axial,
    forward_radial_coarse,
    backward_radial_coarse,
    forward_axial_coarse,
    backward_axial_coarse,
    decay_radial,
    decay_axial,
    advection,
    diffusion,
):
    send = pl.pallas_call(
        gather_kernel,
        out_shape=array(BLOCKS * 40, 128),
        in_specs=[ANY, ANY],
        out_specs=VMEM,
        scratch_shapes=[pltpu.VMEM((12, 24, AXIAL), F32), pltpu.SemaphoreType.DMA],
        compiler_params=PARAMS,
        name="gather_points",
    )(initial_state.reshape(12, RADIAL, AXIAL), forcing.reshape(12, RADIAL, AXIAL))
    received = exchange(send, "azim", BLOCKS)
    received = received.reshape(BLOCKS, 40, 128)[:, :36].reshape(BLOCKS * 36, 128)
    send = pl.pallas_call(
        to_units_kernel,
        out_shape=array(128 * 8, 128),
        in_specs=[VMEM, VMEM],
        out_specs=VMEM,
        compiler_params=PARAMS,
        name="to_units",
    )(jnp.asarray(TO_UNITS), received)
    received = exchange(send, ("tm", "azim"), 128)

    def wide(rows, columns):
        return pltpu.VMEM((rows, columns), BF16)

    fine, coarse = (2, RADIAL, AXIAL), (2, RADIAL_C, AXIAL_C)
    send = pl.pallas_call(
        units_kernel,
        out_shape=array(SLICES, 16 * 24, 128),
        in_specs=[SMEM] + [VMEM] * 13,
        out_specs=VMEM,
        scratch_shapes=[
            wide(3 * AXIAL, AXIAL),
            wide(3 * AXIAL, AXIAL),
            wide(RADIAL, 3 * RADIAL),
            wide(RADIAL, 3 * RADIAL),
            wide(3 * AXIAL_C, AXIAL),
            wide(RADIAL, 3 * RADIAL_C),
            wide(3 * AXIAL, AXIAL_C),
            wide(RADIAL_C, 3 * RADIAL),
            wide(3 * AXIAL_C, AXIAL_C),
            wide(3 * AXIAL_C, AXIAL_C),
            wide(RADIAL_C, 3 * RADIAL_C),
            wide(RADIAL_C, 3 * RADIAL_C),
        ]
        + [pltpu.VMEM((RADIAL, AXIAL), F32)] * 3
        + [pltpu.VMEM((RADIAL_C, AXIAL_C), F32)] * 3
        + [
            pltpu.VMEM((RADIAL, AXIAL), F32),
            pltpu.VMEM((RADIAL, AXIAL), F32),
            pltpu.VMEM((RADIAL_C, AXIAL_C), F32),
            pltpu.VMEM((2,) + fine, F32),
            pltpu.VMEM((10,) + coarse, F32),
            pltpu.VMEM((10,) + coarse, F32),
            pltpu.VMEM((10,) + fine, F32),
            pltpu.VMEM((10,) + fine, F32),
            pltpu.VMEM((5,) + fine, F32),
            pltpu.VMEM((3,) + fine, F32),
            pltpu.VMEM((10,) + coarse, F32),
        ],
        compiler_params=PARAMS,
        name="units",
    )(
        jnp.asarray(SCALARS),
        received,
        forward_radial,
        backward_radial,
        forward_axial,
        backward_axial,
        forward_radial_coarse,
        backward_radial_coarse,
        forward_axial_coarse,
        backward_axial_coarse,
        decay_radial.reshape(1, RADIAL),
        decay_axial.reshape(1, AXIAL),
        advection,
        diffusion.reshape(1, RADIAL),
    )
    received = exchange(send.reshape(128 * 24, 128), ("tm", "azim"), 128)
    send = pl.pallas_call(
        from_units_kernel,
        out_shape=array(BLOCKS * 144, 128),
        in_specs=[VMEM, VMEM],
        out_specs=VMEM,
        compiler_params=PARAMS,
        name="from_units",
    )(jnp.asarray(FROM_UNITS), received)
    received = exchange(send, "azim", BLOCKS)
    planes = pl.pallas_call(
        place_kernel,
        out_shape=array(12, RADIAL, AXIAL),
        in_specs=[VMEM],
        out_specs=VMEM,
        compiler_params=PARAMS,
        name="place",
    )(received)
    return planes.reshape(1, 3, 4, RADIAL, AXIAL)


def solution(mesh):
    split_planes = P(None, "azim", None, None)
    return jax.shard_map(
        per_device,
        mesh=mesh,
        in_specs=(split_planes, split_planes) + (P(),) * 12,
        out_specs=P("tm", None, "azim", None, None),
        check_vma=False,
    )
```

time: 523 us -> 131 us (0.25)
  the two profiles are of different devices: /device:TPU:32 before, /device:TPU:1 now
where the time goes in v1:
time: 131 us
  blocking collectives  89.5 us (68%)
  Pallas kernels  38.7 us (30%)
  local copies, waits for them, and re-layouts  2.66 us (2%)
    all_to_all x4, blocking collectives, exchange(): moved = lax.all_to_all(value.reshape(peers, rows, 128), axes, 0, 0)  89.5 us
    pallas_call x1, Pallas kernels, per_device(): pl.pallas_call(units_kernel, out_shape=array(SLICES, 16 * 24, 128), in_sp...  36.1 us
    unnamed x34, local copies, waits for them, and re-layouts  2.64 us

profile of v1, /device:TPU:1, one launch (start us, length us, event | category | flops | bytes accessed | tf_op | source)
XLA Modules:
  0.0 131.1 jit_solution(16902319615705468797)
XLA Ops:
  0.0 0.0 copy-start
  0.0 1.3 copy-done
  1.3 0.0 copy-start.1
  1.3 1.3 copy-done.1
  2.5 0.1 gather_points.1
  2.6 0.0 copy-start.4
  2.7 18.7 %all_to_all.20 = f32[16,40,128]{2,1,0:T(8,128)S(1)} all-to-all(f32[16,40,128]{2,1,0:T(8,128)S(1)} %bitcast.20), channel_id=1, replica_groups=mesh['tm'=8,'azim'=16] {'azim'}, dimensions={0} | all-to-all | bytes 655360 | tf_op jit(solution)/shard_map/all_to_all | solution.py:440
  21.4 0.0 copy-done.4
  21.4 0.0 copy-start.2
  21.5 0.0 copy-start.3
  21.5 0.0 copy-start.6
  21.5 0.0 copy-start.7
  21.5 0.0 copy-start.8
  21.5 0.0 copy-start.9
  21.5 0.0 copy-start.10
  21.5 0.0 copy-start.11
  21.5 0.0 copy-start.12
  21.6 0.0 copy-start.13
  21.6 0.0 copy-start.14
  21.6 0.0 copy-start.15
  21.6 0.0 copy-start.16
  21.6 0.4 to_units.1
  22.0 18.7 %all_to_all.21 = f32[128,8,128]{2,1,0:T(8,128)S(1)} all-to-all(f32[128,8,128]{2,1,0:T(8,128)S(1)} %bitcast.18), channel_id=1, replica_groups=mesh['tm'=8,'azim'=16] {'tm','azim'}, dimensions={0} | all-to-all | bytes 1048576 | tf_op jit(solution)/shard_map/all_to_all | solution.py:440
  40.7 0.0 copy-done.2
  40.7 0.0 copy-done.3
  40.7 0.0 copy-done.6
  40.7 0.0 copy-done.7
  40.7 0.0 copy-done.8
  40.7 0.0 copy-done.9
  40.8 0.0 copy-done.10
  40.8 0.0 copy-done.11
  40.8 0.0 copy-done.12
  40.8 0.0 copy-done.13
  40.8 0.0 copy-done.14
  40.8 0.0 copy-done.15
  40.8 0.0 copy-done.16
  40.8 36.1 %units.1 = f32[8,384,128]{2,1,0:T(8,128)S(1)} custom-call(f32[128,4]{1,0:T(8,128)S(1)} %copy-done.9, f32[1024,128]{1,0:T(8,128)S(1)} %bitcast.19, f32[96,96]{1,0:T(8,128)S(1)} %copy-done.10, f32[96,96]{1,0:T(8,128)S(1)} %copy-done.11, f32[256,256]{1,0:T(8,128)S(1)} %copy-done.2, f32[256,256]{1,0:T(8,128)S(1)} %copy-done.3, f32[48,48]{1,0:T(8,128)S(1)} %copy-done.12, ...), custom_call_target="tpu_custom_call" | custom-call | tf_op jit(solution)/shard_map/units/pallas_call | solution.py:485
  76.9 0.0 copy-start.5
  77.0 29.1 %all_to_all.22 = f32[128,24,128]{2,1,0:T(8,128)S(1)} all-to-all(f32[128,24,128]{2,1,0:T(8,128)S(1)} %bitcast.15), channel_id=1, replica_groups=mesh['tm'=8,'azim'=16] {'tm','azim'}, dimensions={0} | all-to-all | bytes 3145728 | tf_op jit(solution)/shard_map/all_to_all | solution.py:440
  106.1 0.0 copy-done.5
  106.1 0.7 from_units.1
  106.8 22.9 %all_to_all.23 = f32[16,144,128]{2,1,0:T(8,128)S(1)} all-to-all(f32[16,144,128]{2,1,0:T(8,128)S(1)} %bitcast.17), channel_id=1, replica_groups=mesh['tm'=8,'azim'=16] {'azim'}, dimensions={0} | all-to-all | bytes 2359296 | tf_op jit(solution)/shard_map/all_to_all | solution.py:440
  129.7 1.4 %place.1 = f32[12,96,256]{2,1,0:T(8,128)} custom-call(f32[2304,128]{1,0:T(8,128)S(1)} %bitcast.16), custom_call_target="tpu_custom_call" | custom-call | tf_op jit(solution)/shard_map/place/pallas_call | solution.py:547
  (1 shorter events, 0.0 us)
Async XLA Ops:
  0.0 1.3 copy-start
  1.3 1.3 copy-start.1
  2.6 18.8 %copy-start.4 = (bf16[192,576]{1,0:T(8,128)(2,1)S(1)}, bf16[192,576]{1,0:T(8,128)(2,1)}, u32[]{:S(2)}) copy-start(bf16[192,576]{1,0:T(8,128)(2,1)} %constant.6.clone.transform_ref) | copy-start | bytes 663556
  21.4 19.3 %copy-start.2 = (f32[256,256]{1,0:T(8,128)S(1)}, f32[256,256]{1,0:T(8,128)}, u32[]{:S(2)}) copy-start(f32[256,256]{1,0:T(8,128)} %forward_axial_ref.1) | copy-start | bytes 786436
  21.5 19.3 %copy-start.3 = (f32[256,256]{1,0:T(8,128)S(1)}, f32[256,256]{1,0:T(8,128)}, u32[]{:S(2)}) copy-start(f32[256,256]{1,0:T(8,128)} %backward_axial_ref.1) | copy-start | bytes 786436
  21.5 19.3 %copy-start.6 = (f32[96,256]{1,0:T(8,128)S(1)}, f32[96,256]{1,0:T(8,128)}, u32[]{:S(2)}) copy-start(f32[96,256]{1,0:T(8,128)} %advection_ref.1) | copy-start | bytes 294916
  21.5 19.2 %copy-start.7 = (f32[128,128]{1,0:T(8,128)S(1)}, f32[128,128]{1,0:T(8,128)}, u32[]{:S(2)}) copy-start(f32[128,128]{1,0:T(8,128)} %forward_axial_c_ref.1) | copy-start | bytes 196612
  21.5 19.2 %copy-start.8 = (f32[128,128]{1,0:T(8,128)S(1)}, f32[128,128]{1,0:T(8,128)}, u32[]{:S(2)}) copy-start(f32[128,128]{1,0:T(8,128)} %backward_axial_c_ref.1) | copy-start | bytes 196612
  21.5 19.2 %copy-start.9 = (f32[128,4]{1,0:T(8,128)S(1)}, f32[128,4]{1,0:T(8,128)}, u32[]{:S(2)}) copy-start(f32[128,4]{1,0:T(8,128)} %constant.7.clone.scalars_ref) | copy-start | bytes 6148
  21.5 19.2 %copy-start.10 = (f32[96,96]{1,0:T(8,128)S(1)}, f32[96,96]{1,0:T(8,128)}, u32[]{:S(2)}) copy-start(f32[96,96]{1,0:T(8,128)} %forward_radial_ref.1) | copy-start | bytes 110596
  21.5 19.2 %copy-start.11 = (f32[96,96]{1,0:T(8,128)S(1)}, f32[96,96]{1,0:T(8,128)}, u32[]{:S(2)}) copy-start(f32[96,96]{1,0:T(8,128)} %backward_radial_ref.1) | copy-start | bytes 110596
  21.5 19.2 %copy-start.12 = (f32[48,48]{1,0:T(8,128)S(1)}, f32[48,48]{1,0:T(8,128)}, u32[]{:S(2)}) copy-start(f32[48,48]{1,0:T(8,128)} %forward_radial_c_ref.1) | copy-start | bytes 27652
  21.6 19.2 %copy-start.13 = (f32[48,48]{1,0:T(8,128)S(1)}, f32[48,48]{1,0:T(8,128)}, u32[]{:S(2)}) copy-start(f32[48,48]{1,0:T(8,128)} %backward_radial_c_ref.1) | copy-start | bytes 27652
  21.6 19.2 %copy-start.14 = (f32[256]{0:T(256)S(1)}, f32[256]{0:T(256)}, u32[]{:S(2)}) copy-start(f32[256]{0:T(256)} %param.28) | copy-start | bytes 3076
  21.6 19.2 %copy-start.15 = (f32[96]{0:T(128)S(1)}, f32[96]{0:T(128)}, u32[]{:S(2)}) copy-start(f32[96]{0:T(128)} %param.27) | copy-start | bytes 1156
  21.6 19.2 %copy-start.16 = (f32[96]{0:T(128)S(1)}, f32[96]{0:T(128)}, u32[]{:S(2)}) copy-start(f32[96]{0:T(128)} %param.30) | copy-start | bytes 1156
  76.9 29.1 %copy-start.5 = (bf16[192,576]{1,0:T(8,128)(2,1)S(1)}, bf16[192,576]{1,0:T(8,128)(2,1)}, u32[]{:S(2)}) copy-start(bf16[192,576]{1,0:T(8,128)(2,1)} %constant.8.clone.transform_ref) | copy-start | bytes 663556

commit v2 on v1

--- a/solution.py
+++ b/solution.py
@@ -131,9 +131,33 @@
     return jnp.concatenate([high, high, low], axis=1)
 
 
-def units_kernel(
+OPERATORS = (
+    ("axial", (6 * AXIAL, AXIAL), BF16),
+    ("radial", (2 * RADIAL, 3 * RADIAL), BF16),
+    ("axial_c", (6 * AXIAL_C, AXIAL_C), BF16),
+    ("radial_c", (RADIAL + 2 * RADIAL_C, 3 * RADIAL_C), BF16),
+    ("point", (5 * RADIAL, AXIAL), F32),
+    ("point_c", (4 * RADIAL_C, AXIAL_C), F32),
+)
+
+
+def views(axial_ref, radial_ref, axial_c_ref, radial_c_ref, point_ref, point_c_ref):
+    def parts(ref, *sizes):
+        ends = np.cumsum(sizes)
+        return [ref.at[int(end - size) : int(end), :] for size, end in zip(sizes, ends)]
+
+    return (
+        parts(axial_ref, *[3 * AXIAL] * 2)
+        + parts(radial_ref, *[RADIAL] * 2)
+        + parts(axial_c_ref, *[3 * AXIAL_C] * 2)
+        + parts(radial_c_ref, RADIAL, RADIAL_C, RADIAL_C)
+        + parts(point_ref, *[RADIAL] * 5)
+        + parts(point_c_ref, *[RADIAL_C] * 4)
+    )
+
+
+def operators_kernel(
     scalars_ref,
-    received_ref,
     forward_radial_ref,
     backward_radial_ref,
     forward_axial_ref,
@@ -146,37 +170,12 @@
     decay_axial_ref,
     advection_ref,
     diffusion_ref,
-    out_ref,
-    bz_ref,
-    fz_ref,
-    br_ref,
-    fr_ref,
-    bz_narrow_ref,
-    br_narrow_ref,
-    fz_narrow_ref,
-    fr_narrow_ref,
-    bzc_ref,
-    fzc_ref,
-    brc_ref,
-    frc_ref,
-    cross_ref,
-    first_ref,
-    second_ref,
-    cross_c_ref,
-    first_c_ref,
-    second_c_ref,
-    spectrum_ref,
-    inverse_ref,
-    inverse_c_ref,
-    field_ref,
-    coarse_ref,
-    push_ref,
-    ahead_ref,
-    behind_ref,
-    known_ref,
-    const_ref,
-    gain_ref,
+    *operator_refs,
 ):
+    all_views = views(*operator_refs)
+    (bz_ref, fz_ref, br_ref, fr_ref, bzc_ref, fzc_ref, br_narrow_ref, brc_ref, frc_ref) = all_views[:9]
+    (cross_ref, first_ref, second_ref, spectrum_ref, inverse_ref) = all_views[9:14]
+    (cross_c_ref, first_c_ref, second_c_ref, inverse_c_ref) = all_views[14:]
     unit = lax.axis_index("tm") * BLOCKS + lax.axis_index("azim")
     scalar = [scalars_ref[unit, n] for n in range(4)]
 
@@ -188,10 +187,6 @@
     fzc_ref[...] = axial_weights(forward_axial_c_ref[...])
     brc_ref[...] = radial_weights(identity_plus(backward_radial_c_ref[...]))
     frc_ref[...] = radial_weights(identity_plus(forward_radial_c_ref[...]))
-    for n in range(3):
-        bz_narrow_ref[n * 128 : n * 128 + 128, :] = bz_ref[n * 256 : n * 256 + 128, :]
-    fz_narrow_ref[...] = fz_ref[:, :128]
-    fr_narrow_ref[...] = fr_ref[:48, :]
     br_narrow_ref[...] = radial_weights(identity_plus(backward_radial_ref[...])[:, :48])
 
     diffusion = column_of(diffusion_ref[...], RADIAL)
@@ -225,6 +220,31 @@
     spectrum_ref[...] = spectrum
     inverse_ref[...] = 1.0 / (1.0 - HALF * spectrum)
     inverse_c_ref[...] = 1.0 / (1.0 - STEP * spectrum[:RADIAL_C, :AXIAL_C])
+
+
+def units_kernel(
+    received_ref,
+    axial_ref,
+    radial_ref,
+    axial_c_ref,
+    radial_c_ref,
+    point_ref,
+    point_c_ref,
+    out_ref,
+    field_ref,
+    coarse_ref,
+    push_ref,
+    ahead_ref,
+    behind_ref,
+    known_ref,
+    const_ref,
+    gain_ref,
+    state_ref,
+):
+    all_views = views(axial_ref, radial_ref, axial_c_ref, radial_c_ref, point_ref, point_c_ref)
+    (bz_ref, fz_ref, br_ref, fr_ref, bzc_ref, fzc_ref, br_narrow_ref, brc_ref, frc_ref) = all_views[:9]
+    (cross_ref, first_ref, second_ref, spectrum_ref, inverse_ref) = all_views[9:14]
+    (cross_c_ref, first_c_ref, second_c_ref, inverse_c_ref) = all_views[14:]
 
     for field in range(2):
         for part in range(2):
@@ -240,29 +260,41 @@
     def forces(re, im, cross, first, second):
         return first * re - cross * im, second * im + cross * re
 
-    def to_points(modes):
-        inner = axial(modes.reshape(2 * RADIAL, AXIAL), bz_ref[...])
-        return radial(br_ref[...], inner[:RADIAL]), radial(br_ref[...], inner[RADIAL:])
-
-    def fine_forces(re, im):
-        return forces(re, im, cross_ref[...], first_ref[...], second_ref[...])
-
-    def to_modes(re, im):
-        inner = axial(jnp.concatenate([re, im], axis=0), fz_ref[...])
-        return jnp.stack([radial(fr_ref[...], inner[:RADIAL]), radial(fr_ref[...], inner[RADIAL:])])
-
-    def explicit(modes):
-        return to_modes(*fine_forces(*to_points(modes)))
-
-    def explicit_of_coarse(modes):
-        inner = axial(modes.reshape(2 * RADIAL_C, AXIAL_C), bz_narrow_ref[...])
-        re, im = radial(br_narrow_ref[...], inner[:RADIAL_C]), radial(br_narrow_ref[...], inner[RADIAL_C:])
-        return to_modes(*fine_forces(re, im))
-
-    def restricted_explicit(modes):
-        re, im = fine_forces(*to_points(modes))
-        inner = jnp.concatenate([radial(fr_narrow_ref[...], re), radial(fr_narrow_ref[...], im)], axis=0)
-        return axial(inner, fz_narrow_ref[...]).reshape(2, RADIAL_C, AXIAL_C)
+    def radial_each(weights, rows, size):
+        return [radial(weights, rows[n * size : n * size + size]) for n in range(rows.shape[0] // size)]
+
+    def fine_forces(planes):
+        moved = []
+        for n in range(0, len(planes), 2):
+            moved += forces(planes[n], planes[n + 1], cross_ref[...], first_ref[...], second_ref[...])
+        return moved
+
+    def flat(states):
+        return jnp.concatenate([state.reshape(-1, state.shape[-1]) for state in states], axis=0)
+
+    def pairs(planes):
+        return [jnp.stack(planes[n : n + 2]) for n in range(0, len(planes), 2)]
+
+    def to_points(states):
+        return radial_each(br_ref[...], axial(flat(states), bz_ref[...]), RADIAL)
+
+    def to_modes(planes):
+        inner = axial(jnp.concatenate(planes, axis=0), fz_ref[...])
+        return pairs(radial_each(fr_ref[...], inner, RADIAL))
+
+    def explicit(states):
+        return to_modes(fine_forces(to_points(states)))
+
+    def explicit_of_coarse(states):
+        narrow = jnp.concatenate([bz_ref[n * AXIAL : n * AXIAL + AXIAL_C, :] for n in range(3)], axis=0)
+        inner = axial(flat(states), narrow)
+        return to_modes(fine_forces(radial_each(br_narrow_ref[...], inner, RADIAL_C)))
+
+    def restricted_explicit(states):
+        planes = fine_forces(to_points(states))
+        planes = [radial(fr_ref[:RADIAL_C, :], plane) for plane in planes]
+        inner = axial(jnp.concatenate(planes, axis=0), fz_ref[:, :AXIAL_C])
+        return pairs([inner[n * RADIAL_C : (n + 1) * RADIAL_C] for n in range(len(planes))])
 
     def coarse_explicit(modes):
         inner = axial(modes.reshape(2 * RADIAL_C, AXIAL_C), bzc_ref[...])
@@ -277,18 +309,18 @@
     def corner(value):
         return value[:, :RADIAL_C, :AXIAL_C]
 
-    known_ref[0] = explicit(field_ref[0])
+    known_ref[0] = explicit([field_ref[0]])[0]
     spectrum = spectrum_ref[...]
     total0 = known_ref[0] + field_ref[1] + spectrum * field_ref[0]
     known_ref[3] = inverse_ref[...] * (field_ref[0] - HALF * spectrum * field_ref[0] + (0.5 * STEP) * total0)
-    known_ref[1] = explicit(known_ref[3])
+    known_ref[1] = explicit([known_ref[3]])[0]
     known_ref[4] = inverse_ref[...] * (
         known_ref[3]
         + HALF * (known_ref[1] - known_ref[0])
         - HALF * spectrum_ref[...] * field_ref[0]
         + (0.5 * STEP) * (known_ref[0] + field_ref[1] + spectrum_ref[...] * field_ref[0])
     )
-    known_ref[2] = explicit(known_ref[4])
+    known_ref[2] = explicit([known_ref[4]])[0]
     spectrum_c = spectrum_ref[:RADIAL_C, :AXIAL_C]
     coarse_known = [known_ref[n, :, :RADIAL_C, :AXIAL_C] for n in range(5)]
     start_c = field_ref[0, :, :RADIAL_C, :AXIAL_C]
@@ -307,27 +339,37 @@
     coarse_ref[9] = coarse_known[4]
     coarse_ref[1] = inverse_c_ref[...] * (gain_ref[0] + start_c)
 
-    def chain(n, carry):
-        latest = coarse_ref[n]
-        coarse_ref[n + 1] = inverse_c_ref[...] * (
+    def chain(latest):
+        return inverse_c_ref[...] * (
             gain_ref[0] + latest + STEP * coarse_explicit(latest - coarse_ref[0])
         )
+
+    def spread(places):
+        states = [coarse_ref[n] for n in places]
+        pushes = explicit_of_coarse(states)
+        damping = (0.25 * HALF) * spectrum_ref[:RADIAL_C, :AXIAL_C]
+        for n, state, push in zip(places, states, pushes):
+            push_ref[n] = corner(push)
+            behind_ref[n] = (0.25 * HALF) * push
+            ahead_ref[n] = (0.75 * HALF) * push
+            damped = damping * state
+            behind_ref[n, :, :RADIAL_C, :AXIAL_C] = (0.25 * HALF) * corner(push) - damped
+            ahead_ref[n, :, :RADIAL_C, :AXIAL_C] = (0.75 * HALF) * corner(push) + damped + state
+
+    def chain_and_spread(n, carry):
+        at = 2 * n
+        after = chain(coarse_ref[at + 1])
+        last = chain(after)
+        spread([at, at + 1])
+        coarse_ref[at + 2] = after
+        coarse_ref[at + 3] = last
         return carry
 
-    lax.fori_loop(1, SLICES, chain, 0)
-
-    def spread(n, carry):
-        state = coarse_ref[n]
-        push = explicit_of_coarse(state)
-        push_ref[n] = push[:, :RADIAL_C, :AXIAL_C]
-        behind_ref[n] = (0.25 * HALF) * push
-        ahead_ref[n] = (0.75 * HALF) * push
-        damped = (0.25 * HALF) * spectrum_ref[:RADIAL_C, :AXIAL_C] * state
-        behind_ref[n, :, :RADIAL_C, :AXIAL_C] = behind_ref[n, :, :RADIAL_C, :AXIAL_C] - damped
-        ahead_ref[n, :, :RADIAL_C, :AXIAL_C] = ahead_ref[n, :, :RADIAL_C, :AXIAL_C] + damped + state
-        return carry
-
-    lax.fori_loop(0, SLICES + 2, spread, 0)
+    lax.fori_loop(0, 3, chain_and_spread, 0)
+    last = chain(coarse_ref[7])
+    spread([6, 7, 9])
+    coarse_ref[8] = last
+    spread([8])
 
     def padded(value):
         return jnp.pad(value, ((0, 0), (0, RADIAL - RADIAL_C), (0, AXIAL - AXIAL_C)))
@@ -362,44 +404,52 @@
     gain_ref[8] = STEP * (forcing_c + (coarse_known[0] - push_ref[0]) / 6.0)
     gain_ref[9] = STEP * (forcing_c + (coarse_known[2] - push_ref[9]) / 6.0)
 
-    def sweep(n, carry):
-        later = jnp.minimum(n, 1)
-        middle = inverse_ref[...] * (const_ref[later] + ahead_ref[n] + behind_ref[n + 1])
-        middle_push = explicit(middle)
-        ending = inverse_ref[...] * (middle + HALF * middle_push + const_ref[2] + behind_ref[n + 1] - behind_ref[n])
-        ending_push = restricted_explicit(ending)
+    def sweep(places, kinds):
+        middles = [
+            inverse_ref[...] * (const_ref[kind] + ahead_ref[n] + behind_ref[n + 1])
+            for n, kind in zip(places, kinds)
+        ]
+        middle_pushes = explicit(middles)
+        endings = [
+            inverse_ref[...] * (middle + HALF * push + const_ref[2] + behind_ref[n + 1] - behind_ref[n])
+            for n, middle, push in zip(places, middles, middle_pushes)
+        ]
+        ending_pushes = restricted_explicit(endings)
         spectrum_c = spectrum_ref[:RADIAL_C, :AXIAL_C]
-        gain_ref[n] = (
-            gain_ref[8 + later]
-            + (STEP / 6.0) * (push_ref[n] + spectrum_c * coarse_ref[n])
-            + (STEP * 2.0 / 3.0) * (corner(middle_push) + spectrum_c * corner(middle))
-            + (STEP / 6.0) * ending_push
-            - (STEP * 5.0 / 6.0) * spectrum_c * corner(ending)
-        )
-        for part in range(2):
-            for half in range(2):
-                for j in range(0 if half else 3, 6):
-                    out_ref[n, pl.ds(part * 12 + half * 6 + j, 16, stride=24), :] = ending[
-                        part, 16 * j : 16 * j + 16, half * 128 : half * 128 + 128
-                    ]
-        return carry
-
-    lax.fori_loop(0, SLICES, sweep, 0)
-
-    def place(n, state):
+        for at, n in enumerate(places):
+            middle, ending = middles[at], endings[at]
+            gain_ref[n] = (
+                gain_ref[8 + kinds[at]]
+                + (STEP / 6.0) * (push_ref[n] + spectrum_c * coarse_ref[n])
+                + (STEP * 2.0 / 3.0) * (corner(middle_pushes[at]) + spectrum_c * corner(middle))
+                + (STEP / 6.0) * ending_pushes[at]
+                - (STEP * 5.0 / 6.0) * spectrum_c * corner(ending)
+            )
+            for part in range(2):
+                for half in range(2):
+                    for j in range(0 if half else 3, 6):
+                        out_ref[n, pl.ds(part * 12 + half * 6 + j, 16, stride=24), :] = ending[
+                            part, 16 * j : 16 * j + 16, half * 128 : half * 128 + 128
+                        ]
+
+    def chain_again(n, state):
+        after = inverse_c_ref[...] * (gain_ref[n] + state + STEP * coarse_explicit(state - coarse_ref[n]))
         for part in range(2):
             for j in range(3):
-                out_ref[n, pl.ds(part * 12 + j, 16, stride=24), :] = state[part, 16 * j : 16 * j + 16, :]
-
-    state = inverse_c_ref[...] * (gain_ref[0] + coarse_ref[0])
-    place(0, state)
-
-    def chain_again(n, state):
-        after = inverse_c_ref[...] * (gain_ref[n] + state + STEP * coarse_explicit(state - coarse_ref[n]))
-        place(n, after)
+                out_ref[n, pl.ds(part * 12 + j, 16, stride=24), :] = after[part, 16 * j : 16 * j + 16, :]
         return after
 
-    lax.fori_loop(1, SLICES, chain_again, state)
+    sweep([0, 1], [0, 1])
+    state_ref[...] = coarse_ref[0]
+
+    def sweep_and_chain(n, carry):
+        at = 2 * n
+        state_ref[...] = chain_again(at - 1, chain_again(at - 2, state_ref[...]))
+        sweep([at, at + 1], [1, 1])
+        return carry
+
+    lax.fori_loop(1, 4, sweep_and_chain, 0)
+    chain_again(7, chain_again(6, state_ref[...]))
 
 
 def from_units_kernel(transform_ref, received_ref, send_ref):
@@ -426,9 +476,12 @@
 
 
 VMEM = pl.BlockSpec(memory_space=pltpu.VMEM)
-ANY = pl.BlockSpec(memory_space=pl.ANY)
+HBM = pl.BlockSpec(memory_space=pltpu.HBM)
 SMEM = pl.BlockSpec(memory_space=pltpu.SMEM)
-PARAMS = pltpu.CompilerParams(vmem_limit_bytes=48 << 20)
+
+
+def params(mib):
+    return pltpu.CompilerParams(vmem_limit_bytes=mib << 20)
 
 
 def array(*shape):
@@ -457,70 +510,15 @@
     advection,
     diffusion,
 ):
-    send = pl.pallas_call(
-        gather_kernel,
-        out_shape=array(BLOCKS * 40, 128),
-        in_specs=[ANY, ANY],
-        out_specs=VMEM,
-        scratch_shapes=[pltpu.VMEM((12, 24, AXIAL), F32), pltpu.SemaphoreType.DMA],
-        compiler_params=PARAMS,
-        name="gather_points",
-    )(initial_state.reshape(12, RADIAL, AXIAL), forcing.reshape(12, RADIAL, AXIAL))
-    received = exchange(send, "azim", BLOCKS)
-    received = received.reshape(BLOCKS, 40, 128)[:, :36].reshape(BLOCKS * 36, 128)
-    send = pl.pallas_call(
-        to_units_kernel,
-        out_shape=array(128 * 8, 128),
-        in_specs=[VMEM, VMEM],
-        out_specs=VMEM,
-        compiler_params=PARAMS,
-        name="to_units",
-    )(jnp.asarray(TO_UNITS), received)
-    received = exchange(send, ("tm", "azim"), 128)
-
-    def wide(rows, columns):
-        return pltpu.VMEM((rows, columns), BF16)
-
-    fine, coarse = (2, RADIAL, AXIAL), (2, RADIAL_C, AXIAL_C)
-    send = pl.pallas_call(
-        units_kernel,
-        out_shape=array(SLICES, 16 * 24, 128),
-        in_specs=[SMEM] + [VMEM] * 13,
-        out_specs=VMEM,
-        scratch_shapes=[
-            wide(3 * AXIAL, AXIAL),
-            wide(3 * AXIAL, AXIAL),
-            wide(RADIAL, 3 * RADIAL),
-            wide(RADIAL, 3 * RADIAL),
-            wide(3 * AXIAL_C, AXIAL),
-            wide(RADIAL, 3 * RADIAL_C),
-            wide(3 * AXIAL, AXIAL_C),
-            wide(RADIAL_C, 3 * RADIAL),
-            wide(3 * AXIAL_C, AXIAL_C),
-            wide(3 * AXIAL_C, AXIAL_C),
-            wide(RADIAL_C, 3 * RADIAL_C),
-            wide(RADIAL_C, 3 * RADIAL_C),
-        ]
-        + [pltpu.VMEM((RADIAL, AXIAL), F32)] * 3
-        + [pltpu.VMEM((RADIAL_C, AXIAL_C), F32)] * 3
-        + [
-            pltpu.VMEM((RADIAL, AXIAL), F32),
-            pltpu.VMEM((RADIAL, AXIAL), F32),
-            pltpu.VMEM((RADIAL_C, AXIAL_C), F32),
-            pltpu.VMEM((2,) + fine, F32),
-            pltpu.VMEM((10,) + coarse, F32),
-            pltpu.VMEM((10,) + coarse, F32),
-            pltpu.VMEM((10,) + fine, F32),
-            pltpu.VMEM((10,) + fine, F32),
-            pltpu.VMEM((5,) + fine, F32),
-            pltpu.VMEM((3,) + fine, F32),
-            pltpu.VMEM((10,) + coarse, F32),
-        ],
-        compiler_params=PARAMS,
-        name="units",
+    operators = pl.pallas_call(
+        operators_kernel,
+        out_shape=[jax.ShapeDtypeStruct(shape, kind) for _, shape, kind in OPERATORS],
+        in_specs=[SMEM] + [VMEM] * 12,
+        out_specs=[VMEM] * len(OPERATORS),
+        compiler_params=params(8),
+        name="operators",
     )(
         jnp.asarray(SCALARS),
-        received,
         forward_radial,
         backward_radial,
         forward_axial,
@@ -534,13 +532,59 @@
         advection,
         diffusion.reshape(1, RADIAL),
     )
+    send = pl.pallas_call(
+        gather_kernel,
+        out_shape=array(BLOCKS * 40, 128),
+        in_specs=[HBM, HBM],
+        out_specs=VMEM,
+        scratch_shapes=[pltpu.VMEM((12, 24, AXIAL), F32), pltpu.SemaphoreType.DMA],
+        compiler_params=params(4),
+        name="gather_points",
+    )(
+        *[
+            pltpu.with_memory_space_constraint(field.reshape(12, RADIAL, AXIAL), pltpu.HBM)
+            for field in (initial_state, forcing)
+        ]
+    )
+    received = exchange(send, "azim", BLOCKS)
+    received = received.reshape(BLOCKS, 40, 128)[:, :36].reshape(BLOCKS * 36, 128)
+    send = pl.pallas_call(
+        to_units_kernel,
+        out_shape=array(128 * 8, 128),
+        in_specs=[VMEM, VMEM],
+        out_specs=VMEM,
+        compiler_params=params(4),
+        name="to_units",
+    )(jnp.asarray(TO_UNITS), received)
+    received = exchange(send, ("tm", "azim"), 128)
+
+    fine, coarse = (2, RADIAL, AXIAL), (2, RADIAL_C, AXIAL_C)
+    send = pl.pallas_call(
+        units_kernel,
+        out_shape=array(SLICES, 16 * 24, 128),
+        in_specs=[VMEM] * (1 + len(OPERATORS)),
+        out_specs=VMEM,
+        scratch_shapes=[
+            pltpu.VMEM((2,) + fine, F32),
+            pltpu.VMEM((10,) + coarse, F32),
+            pltpu.VMEM((10,) + coarse, F32),
+            pltpu.VMEM((10,) + fine, F32),
+            pltpu.VMEM((10,) + fine, F32),
+            pltpu.VMEM((5,) + fine, F32),
+            pltpu.VMEM((3,) + fine, F32),
+            pltpu.VMEM((10,) + coarse, F32),
+            pltpu.VMEM(coarse, F32),
+        ],
+        compiler_params=params(28),
+        name="units",
+    )(received, *operators)
     received = exchange(send.reshape(128 * 24, 128), ("tm", "azim"), 128)
     send = pl.pallas_call(
         from_units_kernel,
         out_shape=array(BLOCKS * 144, 128),
         in_specs=[VMEM, VMEM],
         out_specs=VMEM,
-        compiler_params=PARAMS,
+        compiler_params=params(8),
         name="from_units",
     )(jnp.asarray(FROM_UNITS), received)
     received = exchange(send, "azim", BLOCKS)
@@ -549,7 +593,7 @@
         out_shape=array(12, RADIAL, AXIAL),
         in_specs=[VMEM],
         out_specs=VMEM,
-        compiler_params=PARAMS,
+        compiler_params=params(6),
         name="place",
     )(received)
     return planes.reshape(1, 3, 4, RADIAL, AXIAL)

time: 131 us -> 120 us (0.916)
  blocking collectives: 89.5 us -> 70.7 us
  waiting for transfers between devices: 0 us -> 11.3 us
  Pallas kernels: 38.7 us -> 31.5 us
  starting transfers between devices: 0 us -> 5.48 us
  local copies, waits for them, and re-layouts: 2.66 us -> 0.12 us
    all_to_all x4 -> x3, blocking collectives: 89.5 us -> 70.7 us  [exchange(): moved = lax.all_to_all(value.reshape(peers, rows, 128), axes, 0, 0)]
    all_to_all x0 -> x1, waiting for transfers between devices: none -> 11.3 us  [exchange(): moved = lax.all_to_all(value.reshape(peers, rows, 128), axes, 0, 0)]
    pallas_call x1, Pallas kernels: 36.1 us -> 25.2 us  [per_device(): pl.pallas_call(units_kernel, out_shape=array(SLICES, 16 * 24, 128), in_sp...]
    all_to_all x0 -> x1, starting transfers between devices: none -> 5.48 us  [exchange(): moved = lax.all_to_all(value.reshape(peers, rows, 128), axes, 0, 0)]
    unnamed x34 -> x30, local copies, waits for them, and re-layouts: 2.64 us -> 0.1 us
    pallas_call x0 -> x1, Pallas kernels: none -> 2.05 us  [per_device(): pl.pallas_call(operators_kernel, out_shape=[jax.ShapeDtypeStruct(shape, k...]
  transfers between devices with their start and end apart: 0 -> 1, of which waited for: 0 -> 1; matrix products, arithmetic and copies ran while one was open for 0% -> 0% of each run, Pallas kernels for 0% -> 2%
where the time goes in v2:
time: 120 us; the launch traced here: 119 us
  blocking collectives  70.7 us (59%)
  Pallas kernels  31.5 us (26%)
  waiting for transfers between devices  11.3 us (9%)
  starting transfers between devices  5.48 us (5%)
    all_to_all x3, blocking collectives, exchange(): moved = lax.all_to_all(value.reshape(peers, rows, 128), axes, 0, 0)  70.7 us
    pallas_call x1, Pallas kernels, per_device(): pl.pallas_call(units_kernel, out_shape=array(SLICES, 16 * 24, 128), in_sp...  25.2 us
    all_to_all x1, waiting for transfers between devices, exchange(): moved = lax.all_to_all(value.reshape(peers, rows, 128), axes, 0, 0)  11.3 us
    all_to_all x1, starting transfers between devices, exchange(): moved = lax.all_to_all(value.reshape(peers, rows, 128), axes, 0, 0)  5.48 us
  transfers between devices with their start and end apart: 1, of which 1 were waited for; matrix products, arithmetic and copies ran while one was open for 0% of the time, Pallas kernels for 2%

profile of v2, /device:TPU:1, one launch (start us, length us, event | category | flops | bytes accessed | tf_op | source)
XLA Modules:
  0.0 119.4 jit_solution(3378501021970648010)
XLA Ops:
  0.0 1.0 gather_points.1
  1.0 0.0 copy-start.3
  1.0 18.7 %all_to_all.20 = f32[16,40,128]{2,1,0:T(8,128)S(1)} all-to-all(f32[16,40,128]{2,1,0:T(8,128)S(1)} %bitcast.19), channel_id=1, replica_groups=mesh['tm'=8,'azim'=16] {'azim'}, dimensions={0} | all-to-all | bytes 655360 | tf_op jit(solution)/shard_map/all_to_all | solution.py:493
  19.8 0.0 copy-done.3
  19.8 0.0 copy-start
  19.8 0.0 copy-start.1
  19.8 0.0 copy-start.4
  19.9 0.0 copy-start.5
  19.9 0.0 copy-start.6
  19.9 0.0 copy-start.7
  19.9 0.0 copy-start.8
  19.9 0.0 copy-start.9
  19.9 0.0 copy-start.10
  19.9 0.0 copy-start.11
  19.9 0.0 copy-start.12
  19.9 0.0 copy-start.13
  20.0 0.0 copy-start.14
  20.0 1.2 to_units.1
  21.1 5.5 %all-to-all-start.1 = ((f32[128,8,128]{2,1,0:T(8,128)}), f32[128,8,128]{2,1,0:T(8,128)S(1)}, u32[]{:S(2)}, u32[]{:S(2)}) async-start(f32[128,8,128]{2,1,0:T(8,128)} %bitcast.3), calls=%async_computation.1 | async-start | bytes 1048576 | tf_op jit(solution)/shard_map/all_to_all | solution.py:493
  26.6 0.0 copy-done
  26.6 0.0 copy-done.1
  26.6 0.0 copy-done.4
  26.6 0.0 copy-done.5
  26.7 0.0 copy-done.6
  26.7 0.0 copy-done.7
  26.7 0.0 copy-done.8
  26.7 0.0 copy-done.9
  26.7 0.0 copy-done.10
  26.7 0.0 copy-done.11
  26.7 0.0 copy-done.12
  26.7 0.0 copy-done.13
  26.7 0.0 copy-done.14
  26.7 2.1 %operators.1 = (bf16[1536,256]{1,0:T(8,128)(2,1)S(1)}, bf16[192,288]{1,0:T(8,128)(2,1)S(1)}, bf16[768,128]{1,0:T(8,128)(2,1)S(1)}, bf16[192,144]{1,0:T(8,128)(2,...) custom-call(f32[128,4]{1,0:T(8,128)S(1)} %copy-done.7, f32[96,96]{1,0:T(8,128)S(1)} %copy-done.8, ...), custom_call_target="tpu_custom_call" | custom-call | tf_op jit(solution)/shard_map/operators/pallas_call | solution.py:513
  28.8 11.3 %all-to-all-done.1 = f32[128,8,128]{2,1,0:T(8,128)S(1)} async-done(((f32[128,8,128]{2,1,0:T(8,128)}), f32[128,8,128]{2,1,0:T(8,128)S(1)}, u32[]{:S(2)}, u32[]{:S(2)}) %all-to-all-start.1) | async-done | bytes 524320 | tf_op jit(solution)/shard_map/all_to_all | solution.py:493
  40.1 25.2 %units.1 = f32[8,384,128]{2,1,0:T(8,128)S(1)} custom-call(f32[1024,128]{1,0:T(8,128)S(1)} %bitcast.18, bf16[1536,256]{1,0:T(8,128)(2,1)S(1)} %get-tuple-element.11.axial_ref, bf16[192,288]{1,0:T(8,128)(2,1)S(1)} %get-tuple-element.12.radial_ref, bf16[768,128]{1,0:T(8,128)(2,1)S(1)} %get-tuple-element.13.axial_c_ref, ...), custom_call_target="tpu_custom_call" | custom-call | tf_op jit(solution)/shard_map/units/pallas_call | solution.py:562
  65.3 0.0 copy-start.2
  65.3 29.1 %all_to_all.21 = f32[128,24,128]{2,1,0:T(8,128)S(1)} all-to-all(f32[128,24,128]{2,1,0:T(8,128)S(1)} %bitcast.15), channel_id=1, replica_groups=mesh['tm'=8,'azim'=16] {'tm','azim'}, dimensions={0} | all-to-all | bytes 3145728 | tf_op jit(solution)/shard_map/all_to_all | solution.py:493
  94.4 0.0 copy-done.2
  94.4 0.7 from_units.1
  95.2 22.9 %all_to_all.22 = f32[16,144,128]{2,1,0:T(8,128)S(1)} all-to-all(f32[16,144,128]{2,1,0:T(8,128)S(1)} %bitcast.17), channel_id=1, replica_groups=mesh['tm'=8,'azim'=16] {'azim'}, dimensions={0} | all-to-all | bytes 2359296 | tf_op jit(solution)/shard_map/all_to_all | solution.py:493
  118.0 1.4 %place.1 = f32[12,96,256]{2,1,0:T(8,128)} custom-call(f32[2304,128]{1,0:T(8,128)S(1)} %bitcast.16), custom_call_target="tpu_custom_call" | custom-call | tf_op jit(solution)/shard_map/place/pallas_call | solution.py:591
  (1 shorter events, 0.0 us)
Async XLA Ops:
  1.0 18.8 %copy-start.3 = (bf16[192,576]{1,0:T(8,128)(2,1)S(1)}, bf16[192,576]{1,0:T(8,128)(2,1)}, u32[]{:S(2)}) copy-start(bf16[192,576]{1,0:T(8,128)(2,1)} %constant.7.clone.transform_ref) | copy-start | bytes 663556
  19.8 6.8 %copy-start = (f32[256,256]{1,0:T(8,128)S(1)}, f32[256,256]{1,0:T(8,128)}, u32[]{:S(2)}) copy-start(f32[256,256]{1,0:T(8,128)} %forward_axial_ref.1) | copy-start | bytes 786436
  19.8 6.8 %copy-start.1 = (f32[256,256]{1,0:T(8,128)S(1)}, f32[256,256]{1,0:T(8,128)}, u32[]{:S(2)}) copy-start(f32[256,256]{1,0:T(8,128)} %backward_axial_ref.1) | copy-start | bytes 786436
  19.8 6.8 %copy-start.4 = (f32[96,256]{1,0:T(8,128)S(1)}, f32[96,256]{1,0:T(8,128)}, u32[]{:S(2)}) copy-start(f32[96,256]{1,0:T(8,128)} %advection_ref.1) | copy-start | bytes 294916
  19.9 6.8 %copy-start.5 = (f32[128,128]{1,0:T(8,128)S(1)}, f32[128,128]{1,0:T(8,128)}, u32[]{:S(2)}) copy-start(f32[128,128]{1,0:T(8,128)} %forward_axial_c_ref.1) | copy-start | bytes 196612
  19.9 6.8 %copy-start.6 = (f32[128,128]{1,0:T(8,128)S(1)}, f32[128,128]{1,0:T(8,128)}, u32[]{:S(2)}) copy-start(f32[128,128]{1,0:T(8,128)} %backward_axial_c_ref.1) | copy-start | bytes 196612
  19.9 6.8 %copy-start.7 = (f32[128,4]{1,0:T(8,128)S(1)}, f32[128,4]{1,0:T(8,128)}, u32[]{:S(2)}) copy-start(f32[128,4]{1,0:T(8,128)} %constant.6.clone.scalars_ref) | copy-start | bytes 6148
  19.9 6.8 %copy-start.8 = (f32[96,96]{1,0:T(8,128)S(1)}, f32[96,96]{1,0:T(8,128)}, u32[]{:S(2)}) copy-start(f32[96,96]{1,0:T(8,128)} %forward_radial_ref.1) | copy-start | bytes 110596
  19.9 6.8 %copy-start.9 = (f32[96,96]{1,0:T(8,128)S(1)}, f32[96,96]{1,0:T(8,128)}, u32[]{:S(2)}) copy-start(f32[96,96]{1,0:T(8,128)} %backward_radial_ref.1) | copy-start | bytes 110596
  19.9 6.8 %copy-start.10 = (f32[48,48]{1,0:T(8,128)S(1)}, f32[48,48]{1,0:T(8,128)}, u32[]{:S(2)}) copy-start(f32[48,48]{1,0:T(8,128)} %forward_radial_c_ref.1) | copy-start | bytes 27652
  19.9 6.8 %copy-start.11 = (f32[48,48]{1,0:T(8,128)S(1)}, f32[48,48]{1,0:T(8,128)}, u32[]{:S(2)}) copy-start(f32[48,48]{1,0:T(8,128)} %backward_radial_c_ref.1) | copy-start | bytes 27652
  19.9 6.8 %copy-start.12 = (f32[256]{0:T(256)S(1)}, f32[256]{0:T(256)}, u32[]{:S(2)}) copy-start(f32[256]{0:T(256)} %param.28) | copy-start | bytes 3076
  19.9 6.8 %copy-start.13 = (f32[96]{0:T(128)S(1)}, f32[96]{0:T(128)}, u32[]{:S(2)}) copy-start(f32[96]{0:T(128)} %param.27) | copy-start | bytes 1156
  20.0 6.8 %copy-start.14 = (f32[96]{0:T(128)S(1)}, f32[96]{0:T(128)}, u32[]{:S(2)}) copy-start(f32[96]{0:T(128)} %param.30) | copy-start | bytes 1156
  21.1 18.9 %all-to-all-start.1 = ((f32[128,8,128]{2,1,0:T(8,128)}), f32[128,8,128]{2,1,0:T(8,128)S(1)}, u32[]{:S(2)}, u32[]{:S(2)}) async-start(f32[128,8,128]{2,1,0:T(8,128)} %bitcast.3), calls=%async_computation.1 | async-start | bytes 1048576 | tf_op jit(solution)/shard_map/all_to_all | solution.py:493
  65.3 29.1 %copy-start.2 = (bf16[192,576]{1,0:T(8,128)(2,1)S(1)}, bf16[192,576]{1,0:T(8,128)(2,1)}, u32[]{:S(2)}) copy-start(bf16[192,576]{1,0:T(8,128)(2,1)} %constant.8.clone.transform_ref) | copy-start | bytes 663556

commit v3 on v2

--- a/solution.py
+++ b/solution.py
@@ -74,6 +74,12 @@
     return dot(weights, jnp.concatenate([high, low, high], axis=0))
 
 
+def radial_stacked(weights, value):
+    products = dot(weights, jnp.concatenate(split(value), axis=0))
+    half = weights.shape[0] // 2
+    return products[:half] + products[half:]
+
+
 def gather_kernel(initial_ref, forcing_ref, send_ref, block_ref, sem):
     tm = lax.axis_index("tm")
     rows = pl.ds(pl.multiple_of((tm % 4) * 24, 8), 24)
@@ -131,9 +137,16 @@
     return jnp.concatenate([high, high, low], axis=1)
 
 
+def stacked_weights(value):
+    high, low = split(value)
+    return jnp.concatenate(
+        [jnp.concatenate([high, high], axis=1), jnp.concatenate([low, jnp.zeros_like(low)], axis=1)], axis=0
+    )
+
+
 OPERATORS = (
     ("axial", (6 * AXIAL, AXIAL), BF16),
-    ("radial", (2 * RADIAL, 3 * RADIAL), BF16),
+    ("radial", (4 * RADIAL, 2 * RADIAL), BF16),
     ("axial_c", (6 * AXIAL_C, AXIAL_C), BF16),
     ("radial_c", (RADIAL + 2 * RADIAL_C, 3 * RADIAL_C), BF16),
     ("point", (5 * RADIAL, AXIAL), F32),
@@ -148,7 +161,7 @@
 
     return (
         parts(axial_ref, *[3 * AXIAL] * 2)
-        + parts(radial_ref, *[RADIAL] * 2)
+        + parts(radial_ref, *[2 * RADIAL] * 2)
         + parts(axial_c_ref, *[3 * AXIAL_C] * 2)
         + parts(radial_c_ref, RADIAL, RADIAL_C, RADIAL_C)
         + parts(point_ref, *[RADIAL] * 5)
@@ -181,13 +194,13 @@
 
     bz_ref[...] = axial_weights(backward_axial_ref[...])
     fz_ref[...] = axial_weights(forward_axial_ref[...])
-    br_ref[...] = radial_weights(identity_plus(backward_radial_ref[...]))
-    fr_ref[...] = radial_weights(identity_plus(forward_radial_ref[...]))
+    br_ref[...] = stacked_weights(identity_plus(backward_radial_ref[...]))
+    fr_ref[...] = stacked_weights(identity_plus(forward_radial_ref[...]))
     bzc_ref[...] = axial_weights(backward_axial_c_ref[...])
     fzc_ref[...] = axial_weights(forward_axial_c_ref[...])
     brc_ref[...] = radial_weights(identity_plus(backward_radial_c_ref[...]))
     frc_ref[...] = radial_weights(identity_plus(forward_radial_c_ref[...]))
-    br_narrow_ref[...] = radial_weights(identity_plus(backward_radial_ref[...])[:, :48])
+    br_narrow_ref[...] = radial_weights(identity_plus(backward_radial_ref[...])[:, :RADIAL_C])
 
     diffusion = column_of(diffusion_ref[...], RADIAL)
     cross_ref[...] = scalar[2] * advection_ref[...] + scalar[3]
@@ -260,8 +273,8 @@
     def forces(re, im, cross, first, second):
         return first * re - cross * im, second * im + cross * re
 
-    def radial_each(weights, rows, size):
-        return [radial(weights, rows[n * size : n * size + size]) for n in range(rows.shape[0] // size)]
+    def blocks(rows, size):
+        return [rows[n : n + size] for n in range(0, rows.shape[0], size)]
 
     def fine_forces(planes):
         moved = []
@@ -276,51 +289,91 @@
         return [jnp.stack(planes[n : n + 2]) for n in range(0, len(planes), 2)]
 
     def to_points(states):
-        return radial_each(br_ref[...], axial(flat(states), bz_ref[...]), RADIAL)
+        inner = axial(flat(states), bz_ref[...])
+        yield
+        planes = []
+        for plane in blocks(inner, RADIAL):
+            planes.append(radial_stacked(br_ref[...], plane))
+            yield
+        return planes
 
     def to_modes(planes):
         inner = axial(jnp.concatenate(planes, axis=0), fz_ref[...])
-        return pairs(radial_each(fr_ref[...], inner, RADIAL))
+        yield
+        planes = []
+        for plane in blocks(inner, RADIAL):
+            planes.append(radial_stacked(fr_ref[...], plane))
+            yield
+        return pairs(planes)
 
     def explicit(states):
-        return to_modes(fine_forces(to_points(states)))
+        planes = yield from to_points(states)
+        return (yield from to_modes(fine_forces(planes)))
 
     def explicit_of_coarse(states):
         narrow = jnp.concatenate([bz_ref[n * AXIAL : n * AXIAL + AXIAL_C, :] for n in range(3)], axis=0)
         inner = axial(flat(states), narrow)
-        return to_modes(fine_forces(radial_each(br_narrow_ref[...], inner, RADIAL_C)))
+        yield
+        planes = []
+        for plane in blocks(inner, RADIAL_C):
+            planes.append(radial(br_narrow_ref[...], plane))
+            yield
+        return (yield from to_modes(fine_forces(planes)))
 
     def restricted_explicit(states):
-        planes = fine_forces(to_points(states))
-        planes = [radial(fr_ref[:RADIAL_C, :], plane) for plane in planes]
-        inner = axial(jnp.concatenate(planes, axis=0), fz_ref[:, :AXIAL_C])
-        return pairs([inner[n * RADIAL_C : (n + 1) * RADIAL_C] for n in range(len(planes))])
+        planes = fine_forces((yield from to_points(states)))
+        rows = jnp.concatenate([fr_ref[:RADIAL_C, :], fr_ref[RADIAL : RADIAL + RADIAL_C, :]], axis=0)
+        narrow = []
+        for plane in planes:
+            narrow.append(radial_stacked(rows, plane))
+            yield
+        inner = axial(jnp.concatenate(narrow, axis=0), fz_ref[:, :AXIAL_C])
+        yield
+        return pairs(blocks(inner, RADIAL_C))
 
     def coarse_explicit(modes):
         inner = axial(modes.reshape(2 * RADIAL_C, AXIAL_C), bzc_ref[...])
+        yield
         both = radial(brc_ref[...], jnp.concatenate([inner[:RADIAL_C], inner[RADIAL_C:]], axis=1))
+        yield
         re, im = forces(
             both[:, :AXIAL_C], both[:, AXIAL_C:], cross_c_ref[...], first_c_ref[...], second_c_ref[...]
         )
         both = radial(frc_ref[...], jnp.concatenate([re, im], axis=1))
-        inner = jnp.concatenate([both[:, :AXIAL_C], both[:, AXIAL_C:]], axis=0)
-        return axial(inner, fzc_ref[...]).reshape(2, RADIAL_C, AXIAL_C)
+        yield
+        inner = axial(jnp.concatenate([both[:, :AXIAL_C], both[:, AXIAL_C:]], axis=0), fzc_ref[...])
+        yield
+        return inner.reshape(2, RADIAL_C, AXIAL_C)
+
+    def side_by_side(*streams):
+        left = [[stream, 0, count, None] for stream, count in streams]
+        while any(entry[0] is not None for entry in left):
+            entry = min((e for e in left if e[0] is not None), key=lambda e: e[1] / e[2])
+            try:
+                next(entry[0])
+                entry[1] += 1
+            except StopIteration as end:
+                entry[0], entry[3] = None, end.value
+        return [entry[3] for entry in left]
+
+    def alone(stream):
+        return side_by_side((stream, 1))[0]
 
     def corner(value):
         return value[:, :RADIAL_C, :AXIAL_C]
 
-    known_ref[0] = explicit([field_ref[0]])[0]
+    known_ref[0] = alone(explicit([field_ref[0]]))[0]
     spectrum = spectrum_ref[...]
     total0 = known_ref[0] + field_ref[1] + spectrum * field_ref[0]
     known_ref[3] = inverse_ref[...] * (field_ref[0] - HALF * spectrum * field_ref[0] + (0.5 * STEP) * total0)
-    known_ref[1] = explicit([known_ref[3]])[0]
+    known_ref[1] = alone(explicit([known_ref[3]]))[0]
     known_ref[4] = inverse_ref[...] * (
         known_ref[3]
         + HALF * (known_ref[1] - known_ref[0])
         - HALF * spectrum_ref[...] * field_ref[0]
         + (0.5 * STEP) * (known_ref[0] + field_ref[1] + spectrum_ref[...] * field_ref[0])
     )
-    known_ref[2] = explicit([known_ref[4]])[0]
+    known_ref[2] = alone(explicit([known_ref[4]]))[0]
     spectrum_c = spectrum_ref[:RADIAL_C, :AXIAL_C]
     coarse_known = [known_ref[n, :, :RADIAL_C, :AXIAL_C] for n in range(5)]
     start_c = field_ref[0, :, :RADIAL_C, :AXIAL_C]
@@ -339,14 +392,15 @@
     coarse_ref[9] = coarse_known[4]
     coarse_ref[1] = inverse_c_ref[...] * (gain_ref[0] + start_c)
 
-    def chain(latest):
-        return inverse_c_ref[...] * (
-            gain_ref[0] + latest + STEP * coarse_explicit(latest - coarse_ref[0])
-        )
+    def chain(*places):
+        for n in places:
+            latest = coarse_ref[n - 1]
+            push = yield from coarse_explicit(latest - coarse_ref[0])
+            coarse_ref[n] = inverse_c_ref[...] * (gain_ref[0] + latest + STEP * push)
 
     def spread(places):
         states = [coarse_ref[n] for n in places]
-        pushes = explicit_of_coarse(states)
+        pushes = yield from explicit_of_coarse(states)
         damping = (0.25 * HALF) * spectrum_ref[:RADIAL_C, :AXIAL_C]
         for n, state, push in zip(places, states, pushes):
             push_ref[n] = corner(push)
@@ -356,20 +410,14 @@
             behind_ref[n, :, :RADIAL_C, :AXIAL_C] = (0.25 * HALF) * corner(push) - damped
             ahead_ref[n, :, :RADIAL_C, :AXIAL_C] = (0.75 * HALF) * corner(push) + damped + state
 
-    def chain_and_spread(n, carry):
-        at = 2 * n
-        after = chain(coarse_ref[at + 1])
-        last = chain(after)
-        spread([at, at + 1])
-        coarse_ref[at + 2] = after
-        coarse_ref[at + 3] = last
-        return carry
-
-    lax.fori_loop(0, 3, chain_and_spread, 0)
-    last = chain(coarse_ref[7])
-    spread([6, 7, 9])
-    coarse_ref[8] = last
-    spread([8])
+    def chaining(*places):
+        return chain(*places), 4 * len(places)
+
+    def spreading(*places):
+        return spread(places), 2 + 4 * len(places)
+
+    side_by_side(chaining(2, 3, 4), spreading(0, 1, 9))
+    side_by_side(chaining(5, 6), spreading(2, 3, 4))
 
     def padded(value):
         return jnp.pad(value, ((0, 0), (0, RADIAL - RADIAL_C), (0, AXIAL - AXIAL_C)))
@@ -409,12 +457,12 @@
             inverse_ref[...] * (const_ref[kind] + ahead_ref[n] + behind_ref[n + 1])
             for n, kind in zip(places, kinds)
         ]
-        middle_pushes = explicit(middles)
+        middle_pushes = yield from explicit(middles)
         endings = [
             inverse_ref[...] * (middle + HALF * push + const_ref[2] + behind_ref[n + 1] - behind_ref[n])
             for n, middle, push in zip(places, middles, middle_pushes)
         ]
-        ending_pushes = restricted_explicit(endings)
+        ending_pushes = yield from restricted_explicit(endings)
         spectrum_c = spectrum_ref[:RADIAL_C, :AXIAL_C]
         for at, n in enumerate(places):
             middle, ending = middles[at], endings[at]
@@ -432,24 +480,27 @@
                             part, 16 * j : 16 * j + 16, half * 128 : half * 128 + 128
                         ]
 
-    def chain_again(n, state):
-        after = inverse_c_ref[...] * (gain_ref[n] + state + STEP * coarse_explicit(state - coarse_ref[n]))
-        for part in range(2):
-            for j in range(3):
-                out_ref[n, pl.ds(part * 12 + j, 16, stride=24), :] = after[part, 16 * j : 16 * j + 16, :]
-        return after
-
-    sweep([0, 1], [0, 1])
+    def chain_again(places):
+        for n in places:
+            state = state_ref[...]
+            push = yield from coarse_explicit(state - coarse_ref[n])
+            after = inverse_c_ref[...] * (gain_ref[n] + state + STEP * push)
+            state_ref[...] = after
+            for part in range(2):
+                for j in range(3):
+                    out_ref[n, pl.ds(part * 12 + j, 16, stride=24), :] = after[part, 16 * j : 16 * j + 16, :]
+
+    def sweeping(*places):
+        return sweep(places, [min(n, 1) for n in places]), 4 + 8 * len(places)
+
+    def chaining_again(*places):
+        return chain_again(places), 4 * len(places)
+
     state_ref[...] = coarse_ref[0]
-
-    def sweep_and_chain(n, carry):
-        at = 2 * n
-        state_ref[...] = chain_again(at - 1, chain_again(at - 2, state_ref[...]))
-        sweep([at, at + 1], [1, 1])
-        return carry
-
-    lax.fori_loop(1, 4, sweep_and_chain, 0)
-    chain_again(7, chain_again(6, state_ref[...]))
+    side_by_side(chaining(7, 8), sweeping(0, 1, 2), spreading(5, 6))
+    side_by_side(sweeping(3, 4, 5), chaining_again(0, 1, 2), spreading(7, 8))
+    side_by_side(sweeping(6, 7), chaining_again(3, 4, 5))
+    side_by_side(chaining_again(6, 7))
 
 
 def from_units_kernel(transform_ref, received_ref, send_ref):

time: 120 us -> 110 us (0.917)
  Pallas kernels: 31.5 us -> 21.7 us
    pallas_call x1, Pallas kernels: 25.2 us -> 15.4 us  [per_device(): pl.pallas_call(units_kernel, out_shape=array(SLICES, 16 * 24, 128), in_sp...]
where the time goes in v3:
time: 110 us
  blocking collectives  70.7 us (64%)
  Pallas kernels  21.7 us (20%)
  waiting for transfers between devices  11.3 us (10%)
  starting transfers between devices  5.48 us (5%)
    all_to_all x3, blocking collectives, exchange(): moved = lax.all_to_all(value.reshape(peers, rows, 128), axes, 0, 0)  70.7 us
    pallas_call x1, Pallas kernels, per_device(): pl.pallas_call(units_kernel, out_shape=array(SLICES, 16 * 24, 128), in_sp...  15.4 us
    all_to_all x1, waiting for transfers between devices, exchange(): moved = lax.all_to_all(value.reshape(peers, rows, 128), axes, 0, 0)  11.3 us
    all_to_all x1, starting transfers between devices, exchange(): moved = lax.all_to_all(value.reshape(peers, rows, 128), axes, 0, 0)  5.48 us
  transfers between devices with their start and end apart: 1, of which 1 were waited for; matrix products, arithmetic and copies ran while one was open for 0% of the time, Pallas kernels for 2%

profile of v3, /device:TPU:1, one launch (start us, length us, event | category | flops | bytes accessed | tf_op | source)
XLA Modules:
  0.0 109.6 jit_solution(4522646232832369542)
XLA Ops:
  0.0 1.0 gather_points.1
  1.0 0.0 copy-start.3
  1.0 18.7 %all_to_all.20 = f32[16,40,128]{2,1,0:T(8,128)S(1)} all-to-all(f32[16,40,128]{2,1,0:T(8,128)S(1)} %bitcast.19), channel_id=1, replica_groups=mesh['tm'=8,'azim'=16] {'azim'}, dimensions={0} | all-to-all | bytes 655360 | tf_op jit(solution)/shard_map/all_to_all | solution.py:544
  19.8 0.0 copy-done.3
  19.8 0.0 copy-start
  19.8 0.0 copy-start.1
  19.8 0.0 copy-start.4
  19.9 0.0 copy-start.5
  19.9 0.0 copy-start.6
  19.9 0.0 copy-start.7
  19.9 0.0 copy-start.8
  19.9 0.0 copy-start.9
  19.9 0.0 copy-start.10
  19.9 0.0 copy-start.11
  19.9 0.0 copy-start.12
  19.9 0.0 copy-start.13
  20.0 0.0 copy-start.14
  20.0 1.2 %to_units.1 = f32[1024,128]{1,0:T(8,128)} custom-call(bf16[192,576]{1,0:T(8,128)(2,1)S(1)} %copy-done.3, f32[576,128]{1,0:T(8,128)S(1)} %reshape.42.received_ref), custom_call_target="tpu_custom_call" | custom-call | tf_op jit(solution)/shard_map/to_units/pallas_call | solution.py:602
  21.1 5.5 %all-to-all-start.1 = ((f32[128,8,128]{2,1,0:T(8,128)}), f32[128,8,128]{2,1,0:T(8,128)S(1)}, u32[]{:S(2)}, u32[]{:S(2)}) async-start(f32[128,8,128]{2,1,0:T(8,128)} %bitcast.3), calls=%async_computation.1 | async-start | bytes 1048576 | tf_op jit(solution)/shard_map/all_to_all | solution.py:544
  26.6 0.0 copy-done
  26.6 0.0 copy-done.1
  26.6 0.0 copy-done.4
  26.6 0.0 copy-done.5
  26.7 0.0 copy-done.6
  26.7 0.0 copy-done.7
  26.7 0.0 copy-done.8
  26.7 0.0 copy-done.9
  26.7 0.0 copy-done.10
  26.7 0.0 copy-done.11
  26.7 0.0 copy-done.12
  26.7 0.0 copy-done.13
  26.7 0.0 copy-done.14
  26.7 2.1 %operators.1 = (bf16[1536,256]{1,0:T(8,128)(2,1)S(1)}, bf16[384,192]{1,0:T(8,128)(2,1)S(1)}, bf16[768,128]{1,0:T(8,128)(2,1)S(1)}, bf16[192,144]{1,0:T(8,128)(2,...) custom-call(f32[128,4]{1,0:T(8,128)S(1)} %copy-done.7, f32[96,96]{1,0:T(8,128)S(1)} %copy-done.8, ...), custom_call_target="tpu_custom_call" | custom-call | tf_op jit(solution)/shard_map/operators/pallas_call | solution.py:564
  28.8 11.3 %all-to-all-done.1 = f32[128,8,128]{2,1,0:T(8,128)S(1)} async-done(((f32[128,8,128]{2,1,0:T(8,128)}), f32[128,8,128]{2,1,0:T(8,128)S(1)}, u32[]{:S(2)}, u32[]{:S(2)}) %all-to-all-start.1) | async-done | bytes 524320 | tf_op jit(solution)/shard_map/all_to_all | solution.py:544
  40.1 15.4 %units.1 = f32[8,384,128]{2,1,0:T(8,128)S(1)} custom-call(f32[1024,128]{1,0:T(8,128)S(1)} %bitcast.18, bf16[1536,256]{1,0:T(8,128)(2,1)S(1)} %get-tuple-element.11.axial_ref, bf16[384,192]{1,0:T(8,128)(2,1)S(1)} %get-tuple-element.12.radial_ref, bf16[768,128]{1,0:T(8,128)(2,1)S(1)} %get-tuple-element.13.axial_c_ref, ...), custom_call_target="tpu_custom_call" | custom-call | tf_op jit(solution)/shard_map/units/pallas_call | solution.py:613
  55.5 0.0 copy-start.2
  55.5 29.1 %all_to_all.21 = f32[128,24,128]{2,1,0:T(8,128)S(1)} all-to-all(f32[128,24,128]{2,1,0:T(8,128)S(1)} %bitcast.15), channel_id=1, replica_groups=mesh['tm'=8,'azim'=16] {'tm','azim'}, dimensions={0} | all-to-all | bytes 3145728 | tf_op jit(solution)/shard_map/all_to_all | solution.py:544
  84.6 0.0 copy-done.2
  84.6 0.7 from_units.1
  85.4 22.9 %all_to_all.22 = f32[16,144,128]{2,1,0:T(8,128)S(1)} all-to-all(f32[16,144,128]{2,1,0:T(8,128)S(1)} %bitcast.17), channel_id=1, replica_groups=mesh['tm'=8,'azim'=16] {'azim'}, dimensions={0} | all-to-all | bytes 2359296 | tf_op jit(solution)/shard_map/all_to_all | solution.py:544
  108.2 1.4 %place.1 = f32[12,96,256]{2,1,0:T(8,128)} custom-call(f32[2304,128]{1,0:T(8,128)S(1)} %bitcast.16), custom_call_target="tpu_custom_call" | custom-call | tf_op jit(solution)/shard_map/place/pallas_call | solution.py:642
  (1 shorter events, 0.0 us)
Async XLA Ops:
  1.0 18.8 %copy-start.3 = (bf16[192,576]{1,0:T(8,128)(2,1)S(1)}, bf16[192,576]{1,0:T(8,128)(2,1)}, u32[]{:S(2)}) copy-start(bf16[192,576]{1,0:T(8,128)(2,1)} %constant.7.clone.transform_ref) | copy-start | bytes 663556
  19.8 6.8 %copy-start = (f32[256,256]{1,0:T(8,128)S(1)}, f32[256,256]{1,0:T(8,128)}, u32[]{:S(2)}) copy-start(f32[256,256]{1,0:T(8,128)} %forward_axial_ref.1) | copy-start | bytes 786436
  19.8 6.8 %copy-start.1 = (f32[256,256]{1,0:T(8,128)S(1)}, f32[256,256]{1,0:T(8,128)}, u32[]{:S(2)}) copy-start(f32[256,256]{1,0:T(8,128)} %backward_axial_ref.1) | copy-start | bytes 786436
  19.8 6.8 %copy-start.4 = (f32[96,256]{1,0:T(8,128)S(1)}, f32[96,256]{1,0:T(8,128)}, u32[]{:S(2)}) copy-start(f32[96,256]{1,0:T(8,128)} %advection_ref.1) | copy-start | bytes 294916
  19.9 6.8 %copy-start.5 = (f32[128,128]{1,0:T(8,128)S(1)}, f32[128,128]{1,0:T(8,128)}, u32[]{:S(2)}) copy-start(f32[128,128]{1,0:T(8,128)} %forward_axial_c_ref.1) | copy-start | bytes 196612
  19.9 6.8 %copy-start.6 = (f32[128,128]{1,0:T(8,128)S(1)}, f32[128,128]{1,0:T(8,128)}, u32[]{:S(2)}) copy-start(f32[128,128]{1,0:T(8,128)} %backward_axial_c_ref.1) | copy-start | bytes 196612
  19.9 6.8 %copy-start.7 = (f32[128,4]{1,0:T(8,128)S(1)}, f32[128,4]{1,0:T(8,128)}, u32[]{:S(2)}) copy-start(f32[128,4]{1,0:T(8,128)} %constant.6.clone.scalars_ref) | copy-start | bytes 6148
  19.9 6.8 %copy-start.8 = (f32[96,96]{1,0:T(8,128)S(1)}, f32[96,96]{1,0:T(8,128)}, u32[]{:S(2)}) copy-start(f32[96,96]{1,0:T(8,128)} %forward_radial_ref.1) | copy-start | bytes 110596
  19.9 6.8 %copy-start.9 = (f32[96,96]{1,0:T(8,128)S(1)}, f32[96,96]{1,0:T(8,128)}, u32[]{:S(2)}) copy-start(f32[96,96]{1,0:T(8,128)} %backward_radial_ref.1) | copy-start | bytes 110596
  19.9 6.8 %copy-start.10 = (f32[48,48]{1,0:T(8,128)S(1)}, f32[48,48]{1,0:T(8,128)}, u32[]{:S(2)}) copy-start(f32[48,48]{1,0:T(8,128)} %forward_radial_c_ref.1) | copy-start | bytes 27652
  19.9 6.8 %copy-start.11 = (f32[48,48]{1,0:T(8,128)S(1)}, f32[48,48]{1,0:T(8,128)}, u32[]{:S(2)}) copy-start(f32[48,48]{1,0:T(8,128)} %backward_radial_c_ref.1) | copy-start | bytes 27652
  19.9 6.8 %copy-start.12 = (f32[256]{0:T(256)S(1)}, f32[256]{0:T(256)}, u32[]{:S(2)}) copy-start(f32[256]{0:T(256)} %param.28) | copy-start | bytes 3076
  19.9 6.8 %copy-start.13 = (f32[96]{0:T(128)S(1)}, f32[96]{0:T(128)}, u32[]{:S(2)}) copy-start(f32[96]{0:T(128)} %param.27) | copy-start | bytes 1156
  20.0 6.8 %copy-start.14 = (f32[96]{0:T(128)S(1)}, f32[96]{0:T(128)}, u32[]{:S(2)}) copy-start(f32[96]{0:T(128)} %param.30) | copy-start | bytes 1156
  21.1 18.9 %all-to-all-start.1 = ((f32[128,8,128]{2,1,0:T(8,128)}), f32[128,8,128]{2,1,0:T(8,128)S(1)}, u32[]{:S(2)}, u32[]{:S(2)}) async-start(f32[128,8,128]{2,1,0:T(8,128)} %bitcast.3), calls=%async_computation.1 | async-start | bytes 1048576 | tf_op jit(solution)/shard_map/all_to_all | solution.py:544
  55.5 29.1 %copy-start.2 = (bf16[192,576]{1,0:T(8,128)(2,1)S(1)}, bf16[192,576]{1,0:T(8,128)(2,1)}, u32[]{:S(2)}) copy-start(bf16[192,576]{1,0:T(8,128)(2,1)} %constant.8.clone.transform_ref) | copy-start | bytes 663556

commit v4 on v3

--- a/solution.py
+++ b/solution.py
@@ -66,7 +66,9 @@
 
 def axial(value, weights):
     high, low = split(value)
-    return dot(jnp.concatenate([high, low, high], axis=1), weights)
+    depth = weights.shape[0] // 3
+    products = dot(jnp.concatenate([high, low], axis=0), weights[:depth])
+    return products[: value.shape[0]] + products[value.shape[0] :] + dot(high, weights[2 * depth :])
 
 
 def radial(weights, value):
@@ -80,23 +82,29 @@
     return products[:half] + products[half:]
 
 
-def gather_kernel(initial_ref, forcing_ref, send_ref, block_ref, sem):
+def gather_kernel(initial_ref, forcing_ref, send_ref, block_ref, sems):
     tm = lax.axis_index("tm")
     rows = pl.ds(pl.multiple_of((tm % 4) * 24, 8), 24)
 
+    def copies(source_ref):
+        for group in range(4):
+            own = pl.ds(3 * group, 3)
+            yield pltpu.make_async_copy(source_ref.at[own, rows, :], block_ref.at[own], sems.at[group])
+
     @pl.when(tm < 4)
     def _():
-        copy = pltpu.make_async_copy(initial_ref.at[:, rows, :], block_ref, sem)
-        copy.start()
-        copy.wait()
+        for copy in copies(initial_ref):
+            copy.start()
 
     @pl.when(tm >= 4)
     def _():
-        copy = pltpu.make_async_copy(forcing_ref.at[:, rows, :], block_ref, sem)
-        copy.start()
-        copy.wait()
-
+        for copy in copies(forcing_ref):
+            copy.start()
+
+    waits = list(copies(initial_ref))
     for plane in range(12):
+        if plane % 3 == 0:
+            waits[plane // 3].wait()
         for piece in range(6):
             half, row = piece // 3, (piece % 3) * 8
             values = block_ref[plane, row : row + 8, half * 128 : half * 128 + 128]
@@ -345,58 +353,62 @@
         yield
         return inner.reshape(2, RADIAL_C, AXIAL_C)
 
-    def side_by_side(*streams):
-        left = [[stream, 0, count, None] for stream, count in streams]
-        while any(entry[0] is not None for entry in left):
-            entry = min((e for e in left if e[0] is not None), key=lambda e: e[1] / e[2])
-            try:
-                next(entry[0])
-                entry[1] += 1
-            except StopIteration as end:
-                entry[0], entry[3] = None, end.value
-        return [entry[3] for entry in left]
-
-    def alone(stream):
-        return side_by_side((stream, 1))[0]
+    done = set()
+
+    def side_by_side(*tasks):
+        waiting = list(tasks)
+        while waiting:
+            ready = [task for task in waiting if all(need in done for need in task[0])]
+            for task in reversed(ready):
+                try:
+                    next(task[2])
+                except StopIteration:
+                    done.update(task[1])
+                    waiting.remove(task)
 
     def corner(value):
         return value[:, :RADIAL_C, :AXIAL_C]
 
-    known_ref[0] = alone(explicit([field_ref[0]]))[0]
-    spectrum = spectrum_ref[...]
-    total0 = known_ref[0] + field_ref[1] + spectrum * field_ref[0]
-    known_ref[3] = inverse_ref[...] * (field_ref[0] - HALF * spectrum * field_ref[0] + (0.5 * STEP) * total0)
-    known_ref[1] = alone(explicit([known_ref[3]]))[0]
-    known_ref[4] = inverse_ref[...] * (
-        known_ref[3]
-        + HALF * (known_ref[1] - known_ref[0])
-        - HALF * spectrum_ref[...] * field_ref[0]
-        + (0.5 * STEP) * (known_ref[0] + field_ref[1] + spectrum_ref[...] * field_ref[0])
-    )
-    known_ref[2] = alone(explicit([known_ref[4]]))[0]
     spectrum_c = spectrum_ref[:RADIAL_C, :AXIAL_C]
-    coarse_known = [known_ref[n, :, :RADIAL_C, :AXIAL_C] for n in range(5)]
     start_c = field_ref[0, :, :RADIAL_C, :AXIAL_C]
     forcing_c = field_ref[1, :, :RADIAL_C, :AXIAL_C]
-    gain_ref[0] = (
-        STEP
-        * (
-            (coarse_known[0] + spectrum_c * start_c) / 6.0
-            + (2.0 / 3.0) * (coarse_known[1] + spectrum_c * coarse_known[3])
-            + (coarse_known[2] + spectrum_c * coarse_known[4]) / 6.0
-            + forcing_c
+    coarse_ref[0] = start_c
+
+    def first_iteration():
+        known_ref[0] = (yield from explicit([field_ref[0]]))[0]
+        spectrum = spectrum_ref[...]
+        total0 = known_ref[0] + field_ref[1] + spectrum * field_ref[0]
+        known_ref[3] = inverse_ref[...] * (field_ref[0] - HALF * spectrum * field_ref[0] + (0.5 * STEP) * total0)
+        known_ref[1] = (yield from explicit([known_ref[3]]))[0]
+        known_ref[4] = inverse_ref[...] * (
+            known_ref[3]
+            + HALF * (known_ref[1] - known_ref[0])
+            - HALF * spectrum_ref[...] * field_ref[0]
+            + (0.5 * STEP) * (known_ref[0] + field_ref[1] + spectrum_ref[...] * field_ref[0])
         )
-        - STEP * spectrum_c * coarse_known[4]
-    )
-    coarse_ref[0] = start_c
-    coarse_ref[9] = coarse_known[4]
-    coarse_ref[1] = inverse_c_ref[...] * (gain_ref[0] + start_c)
+        coarse_ref[9] = known_ref[4, :, :RADIAL_C, :AXIAL_C]
+        done.add("S9")
+        known_ref[2] = (yield from explicit([known_ref[4]]))[0]
+        coarse_known = [known_ref[n, :, :RADIAL_C, :AXIAL_C] for n in range(5)]
+        gain_ref[0] = (
+            STEP
+            * (
+                (coarse_known[0] + spectrum_c * start_c) / 6.0
+                + (2.0 / 3.0) * (coarse_known[1] + spectrum_c * coarse_known[3])
+                + (coarse_known[2] + spectrum_c * coarse_known[4]) / 6.0
+                + forcing_c
+            )
+            - STEP * spectrum_c * coarse_known[4]
+        )
+        coarse_ref[1] = inverse_c_ref[...] * (gain_ref[0] + start_c)
+        gain_ref[10] = gain_ref[0]
+
 
     def chain(*places):
         for n in places:
             latest = coarse_ref[n - 1]
             push = yield from coarse_explicit(latest - coarse_ref[0])
-            coarse_ref[n] = inverse_c_ref[...] * (gain_ref[0] + latest + STEP * push)
+            coarse_ref[n] = inverse_c_ref[...] * (gain_ref[10] + latest + STEP * push)
 
     def spread(places):
         states = [coarse_ref[n] for n in places]
@@ -410,47 +422,42 @@
             behind_ref[n, :, :RADIAL_C, :AXIAL_C] = (0.25 * HALF) * corner(push) - damped
             ahead_ref[n, :, :RADIAL_C, :AXIAL_C] = (0.75 * HALF) * corner(push) + damped + state
 
-    def chaining(*places):
-        return chain(*places), 4 * len(places)
-
-    def spreading(*places):
-        return spread(places), 2 + 4 * len(places)
-
-    side_by_side(chaining(2, 3, 4), spreading(0, 1, 9))
-    side_by_side(chaining(5, 6), spreading(2, 3, 4))
-
     def padded(value):
         return jnp.pad(value, ((0, 0), (0, RADIAL - RADIAL_C), (0, AXIAL - AXIAL_C)))
 
-    spectrum = spectrum_ref[...]
-    wide_start = padded(coarse_ref[0])
-    wide_end = padded(coarse_ref[9])
-    push_start = (ahead_ref[0] + behind_ref[0] - wide_start) * (1.0 / HALF)
-    push_end = (ahead_ref[9] + behind_ref[9] - wide_end) * (1.0 / HALF)
-    rhs_start = push_start + spectrum * wide_start
-    rhs_end = push_end + spectrum * wide_end
-    total0 = known_ref[0] + field_ref[1] + spectrum * field_ref[0]
-    total1 = known_ref[1] + field_ref[1] + spectrum * known_ref[3]
-    total2 = known_ref[2] + field_ref[1] + spectrum * known_ref[4]
-    shared = -HALF * spectrum * (known_ref[3] - 0.5 * (wide_start + wide_end)) + STEP * (
-        (5.0 / 24.0) * total0 + (1.0 / 3.0) * total1 - (1.0 / 24.0) * total2 - 0.375 * rhs_start - 0.125 * rhs_end
-    )
-    const_ref[0] = field_ref[0] - wide_start + shared
-    const_ref[1] = known_ref[4] - wide_end + HALF * (known_ref[2] - push_end - known_ref[0] + push_start) + shared
-    const_ref[2] = (
-        -HALF * (known_ref[1] - 0.5 * (push_start + push_end))
-        - HALF * spectrum * (known_ref[4] - wide_end)
-        + STEP
-        * (
-            (-1.0 / 24.0) * total0
-            + (1.0 / 3.0) * total1
-            + (5.0 / 24.0) * total2
-            - 0.125 * rhs_start
-            - 0.375 * rhs_end
+    def constants():
+        spectrum = spectrum_ref[...]
+        wide_start = padded(coarse_ref[0])
+        wide_end = padded(coarse_ref[9])
+        push_start = (ahead_ref[0] + behind_ref[0] - wide_start) * (1.0 / HALF)
+        push_end = (ahead_ref[9] + behind_ref[9] - wide_end) * (1.0 / HALF)
+        rhs_start = push_start + spectrum * wide_start
+        rhs_end = push_end + spectrum * wide_end
+        total0 = known_ref[0] + field_ref[1] + spectrum * field_ref[0]
+        total1 = known_ref[1] + field_ref[1] + spectrum * known_ref[3]
+        total2 = known_ref[2] + field_ref[1] + spectrum * known_ref[4]
+        shared = -HALF * spectrum * (known_ref[3] - 0.5 * (wide_start + wide_end)) + STEP * (
+            (5.0 / 24.0) * total0 + (1.0 / 3.0) * total1 - (1.0 / 24.0) * total2 - 0.375 * rhs_start - 0.125 * rhs_end
         )
-    )
-    gain_ref[8] = STEP * (forcing_c + (coarse_known[0] - push_ref[0]) / 6.0)
-    gain_ref[9] = STEP * (forcing_c + (coarse_known[2] - push_ref[9]) / 6.0)
+        const_ref[0] = field_ref[0] - wide_start + shared
+        const_ref[1] = known_ref[4] - wide_end + HALF * (known_ref[2] - push_end - known_ref[0] + push_start) + shared
+        const_ref[2] = (
+            -HALF * (known_ref[1] - 0.5 * (push_start + push_end))
+            - HALF * spectrum * (known_ref[4] - wide_end)
+            + STEP
+            * (
+                (-1.0 / 24.0) * total0
+                + (1.0 / 3.0) * total1
+                + (5.0 / 24.0) * total2
+                - 0.125 * rhs_start
+                - 0.375 * rhs_end
+            )
+        )
+        coarse_known = [known_ref[n, :, :RADIAL_C, :AXIAL_C] for n in (0, 2)]
+        gain_ref[8] = STEP * (forcing_c + (coarse_known[0] - push_ref[0]) / 6.0)
+        gain_ref[9] = STEP * (forcing_c + (coarse_known[1] - push_ref[9]) / 6.0)
+        return
+        yield
 
     def sweep(places, kinds):
         middles = [
@@ -490,17 +497,31 @@
                 for j in range(3):
                     out_ref[n, pl.ds(part * 12 + j, 16, stride=24), :] = after[part, 16 * j : 16 * j + 16, :]
 
+    def chaining(n):
+        return ["S%d" % (n - 1)], ["S%d" % n], chain(n)
+
+    def spreading(*places):
+        return ["S%d" % n for n in places], ["E%d" % n for n in places], spread(places)
+
     def sweeping(*places):
-        return sweep(places, [min(n, 1) for n in places]), 4 + 8 * len(places)
-
-    def chaining_again(*places):
-        return chain_again(places), 4 * len(places)
+        needs = ["E%d" % n for n in range(places[0], places[-1] + 2)] + ["constants"]
+        return needs, ["J%d" % n for n in places], sweep(places, [min(n, 1) for n in places])
+
+    def chaining_again(n):
+        return ["J%d" % n, "T%d" % n], ["T%d" % (n + 1)], chain_again([n])
 
     state_ref[...] = coarse_ref[0]
-    side_by_side(chaining(7, 8), sweeping(0, 1, 2), spreading(5, 6))
-    side_by_side(sweeping(3, 4, 5), chaining_again(0, 1, 2), spreading(7, 8))
-    side_by_side(sweeping(6, 7), chaining_again(3, 4, 5))
-    side_by_side(chaining_again(6, 7))
+    done.update(["S0", "T0"])
+    side_by_side(
+        ([], ["first", "S1"], first_iteration()),
+        *[chaining(n) for n in range(2, 9)],
+        *[chaining_again(n) for n in range(8)],
+        spreading(0),
+        spreading(9),
+        (["first", "E0", "E9"], ["constants"], constants()),
+        *[spreading(n) for n in range(1, 9)],
+        *[sweeping(n) for n in range(8)],
+    )
 
 
 def from_units_kernel(transform_ref, received_ref, send_ref):
@@ -517,13 +538,21 @@
             send_ref[pl.ds(2 * pair + n, 192, stride=12), :] = planes[:, n * 128 : n * 128 + 128]
 
 
-def place_kernel(received_ref, out_ref):
+def place_kernel(received_ref, out_ref, planes_ref, sems):
+    def copy(group):
+        own = pl.ds(3 * group, 3)
+        return pltpu.make_async_copy(planes_ref.at[own], out_ref.at[own], sems.at[group])
+
     for plane in range(12):
         for half in range(2):
             for j in range(6):
-                out_ref[plane, 16 * j : 16 * j + 16, half * 128 : half * 128 + 128] = received_ref[
+                planes_ref[plane, 16 * j : 16 * j + 16, half * 128 : half * 128 + 128] = received_ref[
                     pl.ds(plane * 12 + half * 6 + j, 16, stride=144), :
                 ]
+        if plane % 3 == 2:
+            copy(plane // 3).start()
+    for group in range(4):
+        copy(group).wait()
 
 
 VMEM = pl.BlockSpec(memory_space=pltpu.VMEM)
@@ -588,7 +617,7 @@
         out_shape=array(BLOCKS * 40, 128),
         in_specs=[HBM, HBM],
         out_specs=VMEM,
-        scratch_shapes=[pltpu.VMEM((12, 24, AXIAL), F32), pltpu.SemaphoreType.DMA],
+        scratch_shapes=[pltpu.VMEM((12, 24, AXIAL), F32), pltpu.SemaphoreType.DMA((4,))],
         compiler_params=params(4),
         name="gather_points",
     )(
@@ -623,7 +652,7 @@
             pltpu.VMEM((10,) + fine, F32),
             pltpu.VMEM((5,) + fine, F32),
             pltpu.VMEM((3,) + fine, F32),
-            pltpu.VMEM((10,) + coarse, F32),
+            pltpu.VMEM((11,) + coarse, F32),
             pltpu.VMEM(coarse, F32),
         ],
         compiler_params=params(28),
@@ -643,7 +672,8 @@
         place_kernel,
         out_shape=array(12, RADIAL, AXIAL),
         in_specs=[VMEM],
-        out_specs=VMEM,
+        out_specs=HBM,
+        scratch_shapes=[pltpu.VMEM((12, RADIAL, AXIAL), F32), pltpu.SemaphoreType.DMA((4,))],
         compiler_params=params(6),
         name="place",
     )(received)

time: 110 us -> 108 us (0.982)
  Pallas kernels: 21.7 us -> 19.4 us
    pallas_call x1, Pallas kernels: 15.4 us -> 13.3 us  [per_device(): pl.pallas_call(units_kernel, out_shape=array(SLICES, 16 * 24, 128), in_sp...]
where the time goes in v4:
time: 108 us; the launch traced here: 107 us
  blocking collectives  70.7 us (65%)
  Pallas kernels  19.4 us (18%)
  waiting for transfers between devices  11.3 us (10%)
  starting transfers between devices  5.47 us (5%)
    all_to_all x3, blocking collectives, exchange(): moved = lax.all_to_all(value.reshape(peers, rows, 128), axes, 0, 0)  70.7 us
    pallas_call x1, Pallas kernels, per_device(): pl.pallas_call(units_kernel, out_shape=array(SLICES, 16 * 24, 128), in_sp...  13.3 us
    all_to_all x1, waiting for transfers between devices, exchange(): moved = lax.all_to_all(value.reshape(peers, rows, 128), axes, 0, 0)  11.3 us
    all_to_all x1, starting transfers between devices, exchange(): moved = lax.all_to_all(value.reshape(peers, rows, 128), axes, 0, 0)  5.47 us
  transfers between devices with their start and end apart: 1, of which 1 were waited for; matrix products, arithmetic and copies ran while one was open for 0% of the time, Pallas kernels for 2%

profile of v4, /device:TPU:1, one launch (start us, length us, event | category | flops | bytes accessed | tf_op | source)
XLA Modules:
  0.0 107.3 jit_solution(10922343807879702280)
XLA Ops:
  0.0 1.0 gather_points.1
  1.0 0.0 copy-start.3
  1.1 18.7 %all_to_all.20 = f32[16,40,128]{2,1,0:T(8,128)S(1)} all-to-all(f32[16,40,128]{2,1,0:T(8,128)S(1)} %bitcast.19), channel_id=1, replica_groups=mesh['tm'=8,'azim'=16] {'azim'}, dimensions={0} | all-to-all | bytes 655360 | tf_op jit(solution)/shard_map/all_to_all | solution.py:573
  19.8 0.0 copy-done.3
  19.8 0.0 copy-start
  19.9 0.0 copy-start.1
  19.9 0.0 copy-start.4
  19.9 0.0 copy-start.5
  19.9 0.0 copy-start.6
  19.9 0.0 copy-start.7
  19.9 0.0 copy-start.8
  19.9 0.0 copy-start.9
  19.9 0.0 copy-start.10
  19.9 0.0 copy-start.11
  20.0 0.0 copy-start.12
  20.0 0.0 copy-start.13
  20.0 0.0 copy-start.14
  20.0 1.2 %to_units.1 = f32[1024,128]{1,0:T(8,128)} custom-call(bf16[192,576]{1,0:T(8,128)(2,1)S(1)} %copy-done.3, f32[576,128]{1,0:T(8,128)S(1)} %reshape.42.received_ref), custom_call_target="tpu_custom_call" | custom-call | tf_op jit(solution)/shard_map/to_units/pallas_call | solution.py:631
  21.2 5.5 %all-to-all-start.1 = ((f32[128,8,128]{2,1,0:T(8,128)}), f32[128,8,128]{2,1,0:T(8,128)S(1)}, u32[]{:S(2)}, u32[]{:S(2)}) async-start(f32[128,8,128]{2,1,0:T(8,128)} %bitcast.3), calls=%async_computation.1 | async-start | bytes 1048576 | tf_op jit(solution)/shard_map/all_to_all | solution.py:573
  26.6 0.0 copy-done
  26.6 0.0 copy-done.1
  26.7 0.0 copy-done.4
  26.7 0.0 copy-done.5
  26.7 0.0 copy-done.6
  26.7 0.0 copy-done.7
  26.7 0.0 copy-done.8
  26.7 0.0 copy-done.9
  26.7 0.0 copy-done.10
  26.7 0.0 copy-done.11
  26.7 0.0 copy-done.12
  26.7 0.0 copy-done.13
  26.8 0.0 copy-done.14
  26.8 2.1 %operators.1 = (bf16[1536,256]{1,0:T(8,128)(2,1)S(1)}, bf16[384,192]{1,0:T(8,128)(2,1)S(1)}, bf16[768,128]{1,0:T(8,128)(2,1)S(1)}, bf16[192,144]{1,0:T(8,128)(2,...) custom-call(f32[128,4]{1,0:T(8,128)S(1)} %copy-done.7, f32[96,96]{1,0:T(8,128)S(1)} %copy-done.8, ...), custom_call_target="tpu_custom_call" | custom-call | tf_op jit(solution)/shard_map/operators/pallas_call | solution.py:593
  28.8 11.3 %all-to-all-done.1 = f32[128,8,128]{2,1,0:T(8,128)S(1)} async-done(((f32[128,8,128]{2,1,0:T(8,128)}), f32[128,8,128]{2,1,0:T(8,128)S(1)}, u32[]{:S(2)}, u32[]{:S(2)}) %all-to-all-start.1) | async-done | bytes 524320 | tf_op jit(solution)/shard_map/all_to_all | solution.py:573
  40.1 13.3 %units.1 = f32[8,384,128]{2,1,0:T(8,128)S(1)} custom-call(f32[1024,128]{1,0:T(8,128)S(1)} %bitcast.18, bf16[1536,256]{1,0:T(8,128)(2,1)S(1)} %get-tuple-element.11.axial_ref, bf16[384,192]{1,0:T(8,128)(2,1)S(1)} %get-tuple-element.12.radial_ref, bf16[768,128]{1,0:T(8,128)(2,1)S(1)} %get-tuple-element.13.axial_c_ref, ...), custom_call_target="tpu_custom_call" | custom-call | tf_op jit(solution)/shard_map/units/pallas_call | solution.py:642
  53.4 0.0 copy-start.2
  53.4 29.1 %all_to_all.21 = f32[128,24,128]{2,1,0:T(8,128)S(1)} all-to-all(f32[128,24,128]{2,1,0:T(8,128)S(1)} %bitcast.15), channel_id=1, replica_groups=mesh['tm'=8,'azim'=16] {'tm','azim'}, dimensions={0} | all-to-all | bytes 3145728 | tf_op jit(solution)/shard_map/all_to_all | solution.py:573
  82.5 0.0 copy-done.2
  82.5 0.8 from_units.1
  83.3 22.8 %all_to_all.22 = f32[16,144,128]{2,1,0:T(8,128)S(1)} all-to-all(f32[16,144,128]{2,1,0:T(8,128)S(1)} %bitcast.17), channel_id=1, replica_groups=mesh['tm'=8,'azim'=16] {'azim'}, dimensions={0} | all-to-all | bytes 2359296 | tf_op jit(solution)/shard_map/all_to_all | solution.py:573
  106.1 1.1 %place.1 = f32[12,96,256]{2,1,0:T(8,128)} custom-call(f32[2304,128]{1,0:T(8,128)S(1)} %bitcast.16), custom_call_target="tpu_custom_call" | custom-call | tf_op jit(solution)/shard_map/place/pallas_call | solution.py:671
  (1 shorter events, 0.0 us)
Async XLA Ops:
  1.0 18.8 %copy-start.3 = (bf16[192,576]{1,0:T(8,128)(2,1)S(1)}, bf16[192,576]{1,0:T(8,128)(2,1)}, u32[]{:S(2)}) copy-start(bf16[192,576]{1,0:T(8,128)(2,1)} %constant.7.clone.transform_ref) | copy-start | bytes 663556
  19.8 6.8 %copy-start = (f32[256,256]{1,0:T(8,128)S(1)}, f32[256,256]{1,0:T(8,128)}, u32[]{:S(2)}) copy-start(f32[256,256]{1,0:T(8,128)} %forward_axial_ref.1) | copy-start | bytes 786436
  19.9 6.8 %copy-start.1 = (f32[256,256]{1,0:T(8,128)S(1)}, f32[256,256]{1,0:T(8,128)}, u32[]{:S(2)}) copy-start(f32[256,256]{1,0:T(8,128)} %backward_axial_ref.1) | copy-start | bytes 786436
  19.9 6.8 %copy-start.4 = (f32[96,256]{1,0:T(8,128)S(1)}, f32[96,256]{1,0:T(8,128)}, u32[]{:S(2)}) copy-start(f32[96,256]{1,0:T(8,128)} %advection_ref.1) | copy-start | bytes 294916
  19.9 6.8 %copy-start.5 = (f32[128,128]{1,0:T(8,128)S(1)}, f32[128,128]{1,0:T(8,128)}, u32[]{:S(2)}) copy-start(f32[128,128]{1,0:T(8,128)} %forward_axial_c_ref.1) | copy-start | bytes 196612
  19.9 6.8 %copy-start.6 = (f32[128,128]{1,0:T(8,128)S(1)}, f32[128,128]{1,0:T(8,128)}, u32[]{:S(2)}) copy-start(f32[128,128]{1,0:T(8,128)} %backward_axial_c_ref.1) | copy-start | bytes 196612
  19.9 6.8 %copy-start.7 = (f32[128,4]{1,0:T(8,128)S(1)}, f32[128,4]{1,0:T(8,128)}, u32[]{:S(2)}) copy-start(f32[128,4]{1,0:T(8,128)} %constant.6.clone.scalars_ref) | copy-start | bytes 6148
  19.9 6.8 %copy-start.8 = (f32[96,96]{1,0:T(8,128)S(1)}, f32[96,96]{1,0:T(8,128)}, u32[]{:S(2)}) copy-start(f32[96,96]{1,0:T(8,128)} %forward_radial_ref.1) | copy-start | bytes 110596
  19.9 6.8 %copy-start.9 = (f32[96,96]{1,0:T(8,128)S(1)}, f32[96,96]{1,0:T(8,128)}, u32[]{:S(2)}) copy-start(f32[96,96]{1,0:T(8,128)} %backward_radial_ref.1) | copy-start | bytes 110596
  19.9 6.8 %copy-start.10 = (f32[48,48]{1,0:T(8,128)S(1)}, f32[48,48]{1,0:T(8,128)}, u32[]{:S(2)}) copy-start(f32[48,48]{1,0:T(8,128)} %forward_radial_c_ref.1) | copy-start | bytes 27652
  19.9 6.8 %copy-start.11 = (f32[48,48]{1,0:T(8,128)S(1)}, f32[48,48]{1,0:T(8,128)}, u32[]{:S(2)}) copy-start(f32[48,48]{1,0:T(8,128)} %backward_radial_c_ref.1) | copy-start | bytes 27652
  20.0 6.8 %copy-start.12 = (f32[256]{0:T(256)S(1)}, f32[256]{0:T(256)}, u32[]{:S(2)}) copy-start(f32[256]{0:T(256)} %param.28) | copy-start | bytes 3076
  20.0 6.8 %copy-start.13 = (f32[96]{0:T(128)S(1)}, f32[96]{0:T(128)}, u32[]{:S(2)}) copy-start(f32[96]{0:T(128)} %param.27) | copy-start | bytes 1156
  20.0 6.8 %copy-start.14 = (f32[96]{0:T(128)S(1)}, f32[96]{0:T(128)}, u32[]{:S(2)}) copy-start(f32[96]{0:T(128)} %param.30) | copy-start | bytes 1156
  21.2 18.9 %all-to-all-start.1 = ((f32[128,8,128]{2,1,0:T(8,128)}), f32[128,8,128]{2,1,0:T(8,128)S(1)}, u32[]{:S(2)}, u32[]{:S(2)}) async-start(f32[128,8,128]{2,1,0:T(8,128)} %bitcast.3), calls=%async_computation.1 | async-start | bytes 1048576 | tf_op jit(solution)/shard_map/all_to_all | solution.py:573
  53.4 29.1 %copy-start.2 = (bf16[192,576]{1,0:T(8,128)(2,1)S(1)}, bf16[192,576]{1,0:T(8,128)(2,1)}, u32[]{:S(2)}) copy-start(bf16[192,576]{1,0:T(8,128)(2,1)} %constant.8.clone.transform_ref) | copy-start | bytes 663556

commit v5 on v4

--- a/solution.py
+++ b/solution.py
@@ -297,19 +297,23 @@
         return [jnp.stack(planes[n : n + 2]) for n in range(0, len(planes), 2)]
 
     def to_points(states):
-        inner = axial(flat(states), bz_ref[...])
-        yield
+        inner = []
+        for plane in blocks(flat(states), RADIAL):
+            inner.append(axial(plane, bz_ref[...]))
+            yield
         planes = []
-        for plane in blocks(inner, RADIAL):
+        for plane in inner:
             planes.append(radial_stacked(br_ref[...], plane))
             yield
         return planes
 
     def to_modes(planes):
-        inner = axial(jnp.concatenate(planes, axis=0), fz_ref[...])
-        yield
+        inner = []
+        for plane in planes:
+            inner.append(axial(plane, fz_ref[...]))
+            yield
         planes = []
-        for plane in blocks(inner, RADIAL):
+        for plane in inner:
             planes.append(radial_stacked(fr_ref[...], plane))
             yield
         return pairs(planes)

time: 108 us -> 107 us (level)
  no operation moved by 1% of the time
where the time goes in v5:
time: 107 us
  blocking collectives  70.7 us (66%)
  Pallas kernels  18.7 us (17%)
  waiting for transfers between devices  11.3 us (11%)
  starting transfers between devices  5.47 us (5%)
    all_to_all x3, blocking collectives, exchange(): moved = lax.all_to_all(value.reshape(peers, rows, 128), axes, 0, 0)  70.7 us
    pallas_call x1, Pallas kernels, per_device(): pl.pallas_call(units_kernel, out_shape=array(SLICES, 16 * 24, 128), in_sp...  12.6 us
    all_to_all x1, waiting for transfers between devices, exchange(): moved = lax.all_to_all(value.reshape(peers, rows, 128), axes, 0, 0)  11.3 us
    all_to_all x1, starting transfers between devices, exchange(): moved = lax.all_to_all(value.reshape(peers, rows, 128), axes, 0, 0)  5.47 us
  transfers between devices with their start and end apart: 1, of which 1 were waited for; matrix products, arithmetic and copies ran while one was open for 0% of the time, Pallas kernels for 2%

profile of v5, /device:TPU:1, one launch (start us, length us, event | category | flops | bytes accessed | tf_op | source)
XLA Modules:
  0.0 106.6 jit_solution(14805782905319662799)
XLA Ops:
  0.0 1.0 gather_points.1
  1.0 0.0 copy-start.3
  1.1 18.7 %all_to_all.20 = f32[16,40,128]{2,1,0:T(8,128)S(1)} all-to-all(f32[16,40,128]{2,1,0:T(8,128)S(1)} %bitcast.19), channel_id=1, replica_groups=mesh['tm'=8,'azim'=16] {'azim'}, dimensions={0} | all-to-all | bytes 655360 | tf_op jit(solution)/shard_map/all_to_all | solution.py:577
  19.8 0.0 copy-done.3
  19.8 0.0 copy-start
  19.9 0.0 copy-start.1
  19.9 0.0 copy-start.4
  19.9 0.0 copy-start.5
  19.9 0.0 copy-start.6
  19.9 0.0 copy-start.7
  19.9 0.0 copy-start.8
  19.9 0.0 copy-start.9
  19.9 0.0 copy-start.10
  19.9 0.0 copy-start.11
  20.0 0.0 copy-start.12
  20.0 0.0 copy-start.13
  20.0 0.0 copy-start.14
  20.0 1.2 %to_units.1 = f32[1024,128]{1,0:T(8,128)} custom-call(bf16[192,576]{1,0:T(8,128)(2,1)S(1)} %copy-done.3, f32[576,128]{1,0:T(8,128)S(1)} %reshape.42.received_ref), custom_call_target="tpu_custom_call" | custom-call | tf_op jit(solution)/shard_map/to_units/pallas_call | solution.py:635
  21.2 5.5 %all-to-all-start.1 = ((f32[128,8,128]{2,1,0:T(8,128)}), f32[128,8,128]{2,1,0:T(8,128)S(1)}, u32[]{:S(2)}, u32[]{:S(2)}) async-start(f32[128,8,128]{2,1,0:T(8,128)} %bitcast.3), calls=%async_computation.1 | async-start | bytes 1048576 | tf_op jit(solution)/shard_map/all_to_all | solution.py:577
  26.6 0.0 copy-done
  26.6 0.0 copy-done.1
  26.7 0.0 copy-done.4
  26.7 0.0 copy-done.5
  26.7 0.0 copy-done.6
  26.7 0.0 copy-done.7
  26.7 0.0 copy-done.8
  26.7 0.0 copy-done.9
  26.7 0.0 copy-done.10
  26.7 0.0 copy-done.11
  26.7 0.0 copy-done.12
  26.7 0.0 copy-done.13
  26.8 0.0 copy-done.14
  26.8 2.1 %operators.1 = (bf16[1536,256]{1,0:T(8,128)(2,1)S(1)}, bf16[384,192]{1,0:T(8,128)(2,1)S(1)}, bf16[768,128]{1,0:T(8,128)(2,1)S(1)}, bf16[192,144]{1,0:T(8,128)(2,...) custom-call(f32[128,4]{1,0:T(8,128)S(1)} %copy-done.7, f32[96,96]{1,0:T(8,128)S(1)} %copy-done.8, ...), custom_call_target="tpu_custom_call" | custom-call | tf_op jit(solution)/shard_map/operators/pallas_call | solution.py:597
  28.8 11.3 %all-to-all-done.1 = f32[128,8,128]{2,1,0:T(8,128)S(1)} async-done(((f32[128,8,128]{2,1,0:T(8,128)}), f32[128,8,128]{2,1,0:T(8,128)S(1)}, u32[]{:S(2)}, u32[]{:S(2)}) %all-to-all-start.1) | async-done | bytes 524320 | tf_op jit(solution)/shard_map/all_to_all | solution.py:577
  40.1 12.6 %units.1 = f32[8,384,128]{2,1,0:T(8,128)S(1)} custom-call(f32[1024,128]{1,0:T(8,128)S(1)} %bitcast.18, bf16[1536,256]{1,0:T(8,128)(2,1)S(1)} %get-tuple-element.11.axial_ref, bf16[384,192]{1,0:T(8,128)(2,1)S(1)} %get-tuple-element.12.radial_ref, bf16[768,128]{1,0:T(8,128)(2,1)S(1)} %get-tuple-element.13.axial_c_ref, ...), custom_call_target="tpu_custom_call" | custom-call | tf_op jit(solution)/shard_map/units/pallas_call | solution.py:646
  52.7 0.0 copy-start.2
  52.7 29.1 %all_to_all.21 = f32[128,24,128]{2,1,0:T(8,128)S(1)} all-to-all(f32[128,24,128]{2,1,0:T(8,128)S(1)} %bitcast.15), channel_id=1, replica_groups=mesh['tm'=8,'azim'=16] {'tm','azim'}, dimensions={0} | all-to-all | bytes 3145728 | tf_op jit(solution)/shard_map/all_to_all | solution.py:577
  81.9 0.0 copy-done.2
  81.9 0.7 from_units.1
  82.6 22.8 %all_to_all.22 = f32[16,144,128]{2,1,0:T(8,128)S(1)} all-to-all(f32[16,144,128]{2,1,0:T(8,128)S(1)} %bitcast.17), channel_id=1, replica_groups=mesh['tm'=8,'azim'=16] {'azim'}, dimensions={0} | all-to-all | bytes 2359296 | tf_op jit(solution)/shard_map/all_to_all | solution.py:577
  105.5 1.1 %place.1 = f32[12,96,256]{2,1,0:T(8,128)} custom-call(f32[2304,128]{1,0:T(8,128)S(1)} %bitcast.16), custom_call_target="tpu_custom_call" | custom-call | tf_op jit(solution)/shard_map/place/pallas_call | solution.py:675
  (1 shorter events, 0.0 us)
Async XLA Ops:
  1.0 18.8 %copy-start.3 = (bf16[192,576]{1,0:T(8,128)(2,1)S(1)}, bf16[192,576]{1,0:T(8,128)(2,1)}, u32[]{:S(2)}) copy-start(bf16[192,576]{1,0:T(8,128)(2,1)} %constant.7.clone.transform_ref) | copy-start | bytes 663556
  19.8 6.8 %copy-start = (f32[256,256]{1,0:T(8,128)S(1)}, f32[256,256]{1,0:T(8,128)}, u32[]{:S(2)}) copy-start(f32[256,256]{1,0:T(8,128)} %forward_axial_ref.1) | copy-start | bytes 786436
  19.9 6.8 %copy-start.1 = (f32[256,256]{1,0:T(8,128)S(1)}, f32[256,256]{1,0:T(8,128)}, u32[]{:S(2)}) copy-start(f32[256,256]{1,0:T(8,128)} %backward_axial_ref.1) | copy-start | bytes 786436
  19.9 6.8 %copy-start.4 = (f32[96,256]{1,0:T(8,128)S(1)}, f32[96,256]{1,0:T(8,128)}, u32[]{:S(2)}) copy-start(f32[96,256]{1,0:T(8,128)} %advection_ref.1) | copy-start | bytes 294916
  19.9 6.8 %copy-start.5 = (f32[128,128]{1,0:T(8,128)S(1)}, f32[128,128]{1,0:T(8,128)}, u32[]{:S(2)}) copy-start(f32[128,128]{1,0:T(8,128)} %forward_axial_c_ref.1) | copy-start | bytes 196612
  19.9 6.8 %copy-start.6 = (f32[128,128]{1,0:T(8,128)S(1)}, f32[128,128]{1,0:T(8,128)}, u32[]{:S(2)}) copy-start(f32[128,128]{1,0:T(8,128)} %backward_axial_c_ref.1) | copy-start | bytes 196612
  19.9 6.8 %copy-start.7 = (f32[128,4]{1,0:T(8,128)S(1)}, f32[128,4]{1,0:T(8,128)}, u32[]{:S(2)}) copy-start(f32[128,4]{1,0:T(8,128)} %constant.6.clone.scalars_ref) | copy-start | bytes 6148
  19.9 6.8 %copy-start.8 = (f32[96,96]{1,0:T(8,128)S(1)}, f32[96,96]{1,0:T(8,128)}, u32[]{:S(2)}) copy-start(f32[96,96]{1,0:T(8,128)} %forward_radial_ref.1) | copy-start | bytes 110596
  19.9 6.8 %copy-start.9 = (f32[96,96]{1,0:T(8,128)S(1)}, f32[96,96]{1,0:T(8,128)}, u32[]{:S(2)}) copy-start(f32[96,96]{1,0:T(8,128)} %backward_radial_ref.1) | copy-start | bytes 110596
  19.9 6.8 %copy-start.10 = (f32[48,48]{1,0:T(8,128)S(1)}, f32[48,48]{1,0:T(8,128)}, u32[]{:S(2)}) copy-start(f32[48,48]{1,0:T(8,128)} %forward_radial_c_ref.1) | copy-start | bytes 27652
  19.9 6.8 %copy-start.11 = (f32[48,48]{1,0:T(8,128)S(1)}, f32[48,48]{1,0:T(8,128)}, u32[]{:S(2)}) copy-start(f32[48,48]{1,0:T(8,128)} %backward_radial_c_ref.1) | copy-start | bytes 27652
  20.0 6.8 %copy-start.12 = (f32[256]{0:T(256)S(1)}, f32[256]{0:T(256)}, u32[]{:S(2)}) copy-start(f32[256]{0:T(256)} %param.28) | copy-start | bytes 3076
  20.0 6.8 %copy-start.13 = (f32[96]{0:T(128)S(1)}, f32[96]{0:T(128)}, u32[]{:S(2)}) copy-start(f32[96]{0:T(128)} %param.27) | copy-start | bytes 1156
  20.0 6.8 %copy-start.14 = (f32[96]{0:T(128)S(1)}, f32[96]{0:T(128)}, u32[]{:S(2)}) copy-start(f32[96]{0:T(128)} %param.30) | copy-start | bytes 1156
  21.2 18.9 %all-to-all-start.1 = ((f32[128,8,128]{2,1,0:T(8,128)}), f32[128,8,128]{2,1,0:T(8,128)S(1)}, u32[]{:S(2)}, u32[]{:S(2)}) async-start(f32[128,8,128]{2,1,0:T(8,128)} %bitcast.3), calls=%async_computation.1 | async-start | bytes 1048576 | tf_op jit(solution)/shard_map/all_to_all | solution.py:577
  52.7 29.1 %copy-start.2 = (bf16[192,576]{1,0:T(8,128)(2,1)S(1)}, bf16[192,576]{1,0:T(8,128)(2,1)}, u32[]{:S(2)}) copy-start(bf16[192,576]{1,0:T(8,128)(2,1)} %constant.8.clone.transform_ref) | copy-start | bytes 663556

commit v6 on v5

--- a/solution.py
+++ b/solution.py
@@ -112,16 +112,28 @@
             send_ref[pl.ds(first * 40 + plane * 3 + group, 8, stride=40), :] = values
 
 
-def to_units_kernel(transform_ref, received_ref, send_ref):
-    columns = [received_ref[pl.ds(group, 192, stride=3), :] for group in range(3)]
+def to_units_kernel(transform_ref, received_ref, out_ref, send_ref, sems):
+    def copy(piece, first, size):
+        own = pl.ds(first * 8, size * 8)
+        return pltpu.make_async_copy(send_ref.at[own], out_ref.at[own], sems.at[piece])
+
+    copies = [copy(0, UNITS, 128 - UNITS), copy(1, 0, UNITS // 2), copy(2, UNITS // 2, UNITS // 2)]
     send_ref[UNITS * 8 :, :] = jnp.zeros((32 * 8, 128), F32)
-    zero = jnp.zeros((UNITS, 128), F32)
-    send_ref[pl.ds(6, UNITS, stride=8), :] = zero
-    send_ref[pl.ds(7, UNITS, stride=8), :] = zero
-    for group in range(3):
-        units = radial(transform_ref[...], columns[group])
-        for part in range(2):
-            send_ref[pl.ds(part * 3 + group, UNITS, stride=8), :] = units[part * UNITS : (part + 1) * UNITS]
+    copies[0].start()
+    columns = jnp.concatenate([received_ref[pl.ds(group, 192, stride=3), :] for group in range(3)], axis=1)
+    size = UNITS // 2
+    zero = jnp.zeros((size, 128), F32)
+    for half in range(2):
+        rows = [transform_ref[part * UNITS + half * size : part * UNITS + half * size + size, :] for part in range(2)]
+        units = radial(jnp.concatenate(rows, axis=0), columns)
+        for row in range(8):
+            part, group = row // 3, row % 3
+            send_ref[pl.ds(half * size * 8 + row, size, stride=8), :] = (
+                units[part * size : part * size + size, group * 128 : group * 128 + 128] if row < 6 else zero
+            )
+        copies[1 + half].start()
+    for made in copies:
+        made.wait()
 
 
 def column_of(row, size):
@@ -286,8 +298,9 @@
 
     def fine_forces(planes):
         moved = []
-        for n in range(0, len(planes), 2):
-            moved += forces(planes[n], planes[n + 1], cross_ref[...], first_ref[...], second_ref[...])
+        for re, im in zip(planes[::2], planes[1::2]):
+            moved.append(lambda re=re, im=im: first_ref[...] * re - cross_ref[...] * im)
+            moved.append(lambda re=re, im=im: second_ref[...] * im + cross_ref[...] * re)
         return moved
 
     def flat(states):
@@ -296,31 +309,32 @@
     def pairs(planes):
         return [jnp.stack(planes[n : n + 2]) for n in range(0, len(planes), 2)]
 
-    def to_points(states):
-        inner = []
-        for plane in blocks(flat(states), RADIAL):
-            inner.append(axial(plane, bz_ref[...]))
-            yield
-        planes = []
-        for plane in inner:
-            planes.append(radial_stacked(br_ref[...], plane))
-            yield
-        return planes
-
-    def to_modes(planes):
+    def to_points(planes):
         inner = []
         for plane in planes:
-            inner.append(axial(plane, fz_ref[...]))
+            inner.append(axial(plane(), bz_ref[...]))
             yield
-        planes = []
+        points = []
         for plane in inner:
-            planes.append(radial_stacked(fr_ref[...], plane))
+            points.append(radial_stacked(br_ref[...], plane))
             yield
-        return pairs(planes)
+        return points
+
+    def to_modes(planes, finish=lambda part, plane: plane):
+        inner = []
+        for plane in planes:
+            inner.append(axial(plane(), fz_ref[...]))
+            yield
+        modes = []
+        for part, plane in enumerate(inner):
+            modes.append(finish(part, radial_stacked(fr_ref[...], plane)))
+            yield
+        return modes
 
     def explicit(states):
-        planes = yield from to_points(states)
-        return (yield from to_modes(fine_forces(planes)))
+        planes = [lambda state=state, part=part: state[part] for state in states for part in range(2)]
+        points = yield from to_points(planes)
+        return pairs((yield from to_modes(fine_forces(points))))
 
     def explicit_of_coarse(states):
         narrow = jnp.concatenate([bz_ref[n * AXIAL : n * AXIAL + AXIAL_C, :] for n in range(3)], axis=0)
@@ -330,18 +344,18 @@
         for plane in blocks(inner, RADIAL_C):
             planes.append(radial(br_narrow_ref[...], plane))
             yield
-        return (yield from to_modes(fine_forces(planes)))
-
-    def restricted_explicit(states):
-        planes = fine_forces((yield from to_points(states)))
+        return pairs((yield from to_modes(fine_forces(planes))))
+
+    def restricted_explicit(planes):
+        points = yield from to_points(planes)
         rows = jnp.concatenate([fr_ref[:RADIAL_C, :], fr_ref[RADIAL : RADIAL + RADIAL_C, :]], axis=0)
         narrow = []
-        for plane in planes:
-            narrow.append(radial_stacked(rows, plane))
+        for plane in fine_forces(points):
+            narrow.append(radial_stacked(rows, plane()))
             yield
         inner = axial(jnp.concatenate(narrow, axis=0), fz_ref[:, :AXIAL_C])
         yield
-        return pairs(blocks(inner, RADIAL_C))
+        return inner.reshape(2, RADIAL_C, AXIAL_C)
 
     def coarse_explicit(modes):
         inner = axial(modes.reshape(2 * RADIAL_C, AXIAL_C), bzc_ref[...])
@@ -463,33 +477,37 @@
         return
         yield
 
-    def sweep(places, kinds):
-        middles = [
-            inverse_ref[...] * (const_ref[kind] + ahead_ref[n] + behind_ref[n + 1])
-            for n, kind in zip(places, kinds)
-        ]
-        middle_pushes = yield from explicit(middles)
-        endings = [
-            inverse_ref[...] * (middle + HALF * push + const_ref[2] + behind_ref[n + 1] - behind_ref[n])
-            for n, middle, push in zip(places, middles, middle_pushes)
-        ]
-        ending_pushes = yield from restricted_explicit(endings)
+    def sweep(n, kind):
+        middles, pushes, endings = {}, {}, {}
+
+        def middle(part):
+            middles[part] = inverse_ref[...] * (const_ref[kind, part] + ahead_ref[n, part] + behind_ref[n + 1, part])
+            return middles[part]
+
+        def ending(part, push):
+            pushes[part] = push[:RADIAL_C, :AXIAL_C]
+            endings[part] = inverse_ref[...] * (
+                middles[part] + HALF * push + const_ref[2, part] + behind_ref[n + 1, part] - behind_ref[n, part]
+            )
+            for half in range(2):
+                for j in range(0 if half else 3, 6):
+                    out_ref[n, pl.ds(part * 12 + half * 6 + j, 16, stride=24), :] = endings[part][
+                        16 * j : 16 * j + 16, half * 128 : half * 128 + 128
+                    ]
+            return endings[part]
+
+        points = yield from to_points([lambda part=part: middle(part) for part in range(2)])
+        yield from to_modes(fine_forces(points), ending)
+        last = yield from restricted_explicit([lambda part=part: endings[part] for part in range(2)])
         spectrum_c = spectrum_ref[:RADIAL_C, :AXIAL_C]
-        for at, n in enumerate(places):
-            middle, ending = middles[at], endings[at]
-            gain_ref[n] = (
-                gain_ref[8 + kinds[at]]
-                + (STEP / 6.0) * (push_ref[n] + spectrum_c * coarse_ref[n])
-                + (STEP * 2.0 / 3.0) * (corner(middle_pushes[at]) + spectrum_c * corner(middle))
-                + (STEP / 6.0) * ending_pushes[at]
-                - (STEP * 5.0 / 6.0) * spectrum_c * corner(ending)
+        for part in range(2):
+            gain_ref[n, part] = (
+                gain_ref[8 + kind, part]
+                + (STEP / 6.0) * (push_ref[n, part] + spectrum_c * coarse_ref[n, part])
+                + (STEP * 2.0 / 3.0) * (pushes[part] + spectrum_c * middles[part][:RADIAL_C, :AXIAL_C])
+                + (STEP / 6.0) * last[part]
+                - (STEP * 5.0 / 6.0) * spectrum_c * endings[part][:RADIAL_C, :AXIAL_C]
             )
-            for part in range(2):
-                for half in range(2):
-                    for j in range(0 if half else 3, 6):
-                        out_ref[n, pl.ds(part * 12 + half * 6 + j, 16, stride=24), :] = ending[
-                            part, 16 * j : 16 * j + 16, half * 128 : half * 128 + 128
-                        ]
 
     def chain_again(places):
         for n in places:
@@ -507,9 +525,8 @@
     def spreading(*places):
         return ["S%d" % n for n in places], ["E%d" % n for n in places], spread(places)
 
-    def sweeping(*places):
-        needs = ["E%d" % n for n in range(places[0], places[-1] + 2)] + ["constants"]
-        return needs, ["J%d" % n for n in places], sweep(places, [min(n, 1) for n in places])
+    def sweeping(n):
+        return ["E%d" % n, "E%d" % (n + 1), "constants"], ["J%d" % n], sweep(n, min(n, 1))
 
     def chaining_again(n):
         return ["J%d" % n, "T%d" % n], ["T%d" % (n + 1)], chain_again([n])
@@ -636,7 +653,8 @@
         to_units_kernel,
         out_shape=array(128 * 8, 128),
         in_specs=[VMEM, VMEM],
-        out_specs=VMEM,
+        out_specs=HBM,
+        scratch_shapes=[pltpu.VMEM((128 * 8, 128), F32), pltpu.SemaphoreType.DMA((3,))],
         compiler_params=params(4),
         name="to_units",
     )(jnp.asarray(TO_UNITS), received)

time: 107 us -> 107 us (level)
  no operation moved by 1% of the time
where the time goes in v6:
time: 107 us; the launch traced here: 106 us
  blocking collectives  70.7 us (66%)
  Pallas kernels  18.6 us (17%)
  waiting for transfers between devices  11.3 us (11%)
  starting transfers between devices  5.48 us (5%)
    all_to_all x3, blocking collectives, exchange(): moved = lax.all_to_all(value.reshape(peers, rows, 128), axes, 0, 0)  70.7 us
    pallas_call x1, Pallas kernels, per_device(): pl.pallas_call(units_kernel, out_shape=array(SLICES, 16 * 24, 128), in_sp...  12.6 us
    all_to_all x1, waiting for transfers between devices, exchange(): moved = lax.all_to_all(value.reshape(peers, rows, 128), axes, 0, 0)  11.3 us
    all_to_all x1, starting transfers between devices, exchange(): moved = lax.all_to_all(value.reshape(peers, rows, 128), axes, 0, 0)  5.48 us
  transfers between devices with their start and end apart: 1, of which 1 were waited for; matrix products, arithmetic and copies ran while one was open for 0% of the time, Pallas kernels for 2%

profile of v6, /device:TPU:1, one launch (start us, length us, event | category | flops | bytes accessed | tf_op | source)
XLA Modules:
  0.0 106.4 jit_solution(862407208031559846)
XLA Ops:
  0.0 1.0 gather_points.1
  1.0 0.0 copy-start.3
  1.1 18.7 %all_to_all.20 = f32[16,40,128]{2,1,0:T(8,128)S(1)} all-to-all(f32[16,40,128]{2,1,0:T(8,128)S(1)} %bitcast.19), channel_id=1, replica_groups=mesh['tm'=8,'azim'=16] {'azim'}, dimensions={0} | all-to-all | bytes 655360 | tf_op jit(solution)/shard_map/all_to_all | solution.py:594
  19.8 0.0 copy-done.3
  19.8 0.0 copy-start
  19.9 0.0 copy-start.1
  19.9 0.0 copy-start.4
  19.9 0.0 copy-start.5
  19.9 0.0 copy-start.6
  19.9 0.0 copy-start.7
  19.9 0.0 copy-start.8
  19.9 0.0 copy-start.9
  19.9 0.0 copy-start.10
  19.9 0.0 copy-start.11
  20.0 0.0 copy-start.12
  20.0 0.0 copy-start.13
  20.0 0.0 copy-start.14
  20.0 1.0 to_units.1
  21.0 5.5 %all-to-all-start.1 = ((f32[128,8,128]{2,1,0:T(8,128)}), f32[128,8,128]{2,1,0:T(8,128)S(1)}, u32[]{:S(2)}, u32[]{:S(2)}) async-start(f32[128,8,128]{2,1,0:T(8,128)} %bitcast.3), calls=%async_computation.1 | async-start | bytes 1048576 | tf_op jit(solution)/shard_map/all_to_all | solution.py:594
  26.5 0.0 copy-done
  26.5 0.0 copy-done.1
  26.5 0.0 copy-done.4
  26.5 0.0 copy-done.5
  26.6 0.0 copy-done.6
  26.6 0.0 copy-done.7
  26.6 0.0 copy-done.8
  26.6 0.0 copy-done.9
  26.6 0.0 copy-done.10
  26.6 0.0 copy-done.11
  26.6 0.0 copy-done.12
  26.6 0.0 copy-done.13
  26.6 0.0 copy-done.14
  26.6 2.1 %operators.1 = (bf16[1536,256]{1,0:T(8,128)(2,1)S(1)}, bf16[384,192]{1,0:T(8,128)(2,1)S(1)}, bf16[768,128]{1,0:T(8,128)(2,1)S(1)}, bf16[192,144]{1,0:T(8,128)(2,...) custom-call(f32[128,4]{1,0:T(8,128)S(1)} %copy-done.7, f32[96,96]{1,0:T(8,128)S(1)} %copy-done.8, ...), custom_call_target="tpu_custom_call" | custom-call | tf_op jit(solution)/shard_map/operators/pallas_call | solution.py:614
  28.7 11.3 %all-to-all-done.1 = f32[128,8,128]{2,1,0:T(8,128)S(1)} async-done(((f32[128,8,128]{2,1,0:T(8,128)}), f32[128,8,128]{2,1,0:T(8,128)S(1)}, u32[]{:S(2)}, u32[]{:S(2)}) %all-to-all-start.1) | async-done | bytes 524320 | tf_op jit(solution)/shard_map/all_to_all | solution.py:594
  40.0 12.6 %units.1 = f32[8,384,128]{2,1,0:T(8,128)S(1)} custom-call(f32[1024,128]{1,0:T(8,128)S(1)} %bitcast.18, bf16[1536,256]{1,0:T(8,128)(2,1)S(1)} %get-tuple-element.11.axial_ref, bf16[384,192]{1,0:T(8,128)(2,1)S(1)} %get-tuple-element.12.radial_ref, bf16[768,128]{1,0:T(8,128)(2,1)S(1)} %get-tuple-element.13.axial_c_ref, ...), custom_call_target="tpu_custom_call" | custom-call | tf_op jit(solution)/shard_map/units/pallas_call | solution.py:664
  52.6 0.0 copy-start.2
  52.6 29.1 %all_to_all.21 = f32[128,24,128]{2,1,0:T(8,128)S(1)} all-to-all(f32[128,24,128]{2,1,0:T(8,128)S(1)} %bitcast.15), channel_id=1, replica_groups=mesh['tm'=8,'azim'=16] {'tm','azim'}, dimensions={0} | all-to-all | bytes 3145728 | tf_op jit(solution)/shard_map/all_to_all | solution.py:594
  81.7 0.0 copy-done.2
  81.7 0.8 from_units.1
  82.5 22.8 %all_to_all.22 = f32[16,144,128]{2,1,0:T(8,128)S(1)} all-to-all(f32[16,144,128]{2,1,0:T(8,128)S(1)} %bitcast.17), channel_id=1, replica_groups=mesh['tm'=8,'azim'=16] {'azim'}, dimensions={0} | all-to-all | bytes 2359296 | tf_op jit(solution)/shard_map/all_to_all | solution.py:594
  105.3 1.1 %place.1 = f32[12,96,256]{2,1,0:T(8,128)} custom-call(f32[2304,128]{1,0:T(8,128)S(1)} %bitcast.16), custom_call_target="tpu_custom_call" | custom-call | tf_op jit(solution)/shard_map/place/pallas_call | solution.py:693
  (1 shorter events, 0.0 us)
Async XLA Ops:
  1.0 18.8 %copy-start.3 = (bf16[192,576]{1,0:T(8,128)(2,1)S(1)}, bf16[192,576]{1,0:T(8,128)(2,1)}, u32[]{:S(2)}) copy-start(bf16[192,576]{1,0:T(8,128)(2,1)} %constant.7.clone.transform_ref) | copy-start | bytes 663556
  19.8 6.7 %copy-start = (f32[256,256]{1,0:T(8,128)S(1)}, f32[256,256]{1,0:T(8,128)}, u32[]{:S(2)}) copy-start(f32[256,256]{1,0:T(8,128)} %forward_axial_ref.1) | copy-start | bytes 786436
  19.9 6.7 %copy-start.1 = (f32[256,256]{1,0:T(8,128)S(1)}, f32[256,256]{1,0:T(8,128)}, u32[]{:S(2)}) copy-start(f32[256,256]{1,0:T(8,128)} %backward_axial_ref.1) | copy-start | bytes 786436
  19.9 6.7 %copy-start.4 = (f32[96,256]{1,0:T(8,128)S(1)}, f32[96,256]{1,0:T(8,128)}, u32[]{:S(2)}) copy-start(f32[96,256]{1,0:T(8,128)} %advection_ref.1) | copy-start | bytes 294916
  19.9 6.7 %copy-start.5 = (f32[128,128]{1,0:T(8,128)S(1)}, f32[128,128]{1,0:T(8,128)}, u32[]{:S(2)}) copy-start(f32[128,128]{1,0:T(8,128)} %forward_axial_c_ref.1) | copy-start | bytes 196612
  19.9 6.7 %copy-start.6 = (f32[128,128]{1,0:T(8,128)S(1)}, f32[128,128]{1,0:T(8,128)}, u32[]{:S(2)}) copy-start(f32[128,128]{1,0:T(8,128)} %backward_axial_c_ref.1) | copy-start | bytes 196612
  19.9 6.7 %copy-start.7 = (f32[128,4]{1,0:T(8,128)S(1)}, f32[128,4]{1,0:T(8,128)}, u32[]{:S(2)}) copy-start(f32[128,4]{1,0:T(8,128)} %constant.6.clone.scalars_ref) | copy-start | bytes 6148
  19.9 6.7 %copy-start.8 = (f32[96,96]{1,0:T(8,128)S(1)}, f32[96,96]{1,0:T(8,128)}, u32[]{:S(2)}) copy-start(f32[96,96]{1,0:T(8,128)} %forward_radial_ref.1) | copy-start | bytes 110596
  19.9 6.7 %copy-start.9 = (f32[96,96]{1,0:T(8,128)S(1)}, f32[96,96]{1,0:T(8,128)}, u32[]{:S(2)}) copy-start(f32[96,96]{1,0:T(8,128)} %backward_radial_ref.1) | copy-start | bytes 110596
  19.9 6.7 %copy-start.10 = (f32[48,48]{1,0:T(8,128)S(1)}, f32[48,48]{1,0:T(8,128)}, u32[]{:S(2)}) copy-start(f32[48,48]{1,0:T(8,128)} %forward_radial_c_ref.1) | copy-start | bytes 27652
  19.9 6.7 %copy-start.11 = (f32[48,48]{1,0:T(8,128)S(1)}, f32[48,48]{1,0:T(8,128)}, u32[]{:S(2)}) copy-start(f32[48,48]{1,0:T(8,128)} %backward_radial_c_ref.1) | copy-start | bytes 27652
  20.0 6.7 %copy-start.12 = (f32[256]{0:T(256)S(1)}, f32[256]{0:T(256)}, u32[]{:S(2)}) copy-start(f32[256]{0:T(256)} %param.28) | copy-start | bytes 3076
  20.0 6.7 %copy-start.13 = (f32[96]{0:T(128)S(1)}, f32[96]{0:T(128)}, u32[]{:S(2)}) copy-start(f32[96]{0:T(128)} %param.27) | copy-start | bytes 1156
  20.0 6.7 %copy-start.14 = (f32[96]{0:T(128)S(1)}, f32[96]{0:T(128)}, u32[]{:S(2)}) copy-start(f32[96]{0:T(128)} %param.30) | copy-start | bytes 1156
  21.0 18.9 %all-to-all-start.1 = ((f32[128,8,128]{2,1,0:T(8,128)}), f32[128,8,128]{2,1,0:T(8,128)S(1)}, u32[]{:S(2)}, u32[]{:S(2)}) async-start(f32[128,8,128]{2,1,0:T(8,128)} %bitcast.3), calls=%async_computation.1 | async-start | bytes 1048576 | tf_op jit(solution)/shard_map/all_to_all | solution.py:594
  52.6 29.1 %copy-start.2 = (bf16[192,576]{1,0:T(8,128)(2,1)S(1)}, bf16[192,576]{1,0:T(8,128)(2,1)}, u32[]{:S(2)}) copy-start(bf16[192,576]{1,0:T(8,128)(2,1)} %constant.8.clone.transform_ref) | copy-start | bytes 663556

commit v7 on v6

--- a/solution.py
+++ b/solution.py
@@ -112,28 +112,16 @@
             send_ref[pl.ds(first * 40 + plane * 3 + group, 8, stride=40), :] = values
 
 
-def to_units_kernel(transform_ref, received_ref, out_ref, send_ref, sems):
-    def copy(piece, first, size):
-        own = pl.ds(first * 8, size * 8)
-        return pltpu.make_async_copy(send_ref.at[own], out_ref.at[own], sems.at[piece])
-
-    copies = [copy(0, UNITS, 128 - UNITS), copy(1, 0, UNITS // 2), copy(2, UNITS // 2, UNITS // 2)]
+def to_units_kernel(transform_ref, received_ref, send_ref):
+    columns = [received_ref[pl.ds(group, 192, stride=3), :] for group in range(3)]
     send_ref[UNITS * 8 :, :] = jnp.zeros((32 * 8, 128), F32)
-    copies[0].start()
-    columns = jnp.concatenate([received_ref[pl.ds(group, 192, stride=3), :] for group in range(3)], axis=1)
-    size = UNITS // 2
-    zero = jnp.zeros((size, 128), F32)
-    for half in range(2):
-        rows = [transform_ref[part * UNITS + half * size : part * UNITS + half * size + size, :] for part in range(2)]
-        units = radial(jnp.concatenate(rows, axis=0), columns)
-        for row in range(8):
-            part, group = row // 3, row % 3
-            send_ref[pl.ds(half * size * 8 + row, size, stride=8), :] = (
-                units[part * size : part * size + size, group * 128 : group * 128 + 128] if row < 6 else zero
-            )
-        copies[1 + half].start()
-    for made in copies:
-        made.wait()
+    zero = jnp.zeros((UNITS, 128), F32)
+    send_ref[pl.ds(6, UNITS, stride=8), :] = zero
+    send_ref[pl.ds(7, UNITS, stride=8), :] = zero
+    for group in range(3):
+        units = radial(transform_ref[...], columns[group])
+        for part in range(2):
+            send_ref[pl.ds(part * 3 + group, UNITS, stride=8), :] = units[part * UNITS : (part + 1) * UNITS]
 
 
 def column_of(row, size):
@@ -653,8 +641,7 @@
         to_units_kernel,
         out_shape=array(128 * 8, 128),
         in_specs=[VMEM, VMEM],
-        out_specs=HBM,
-        scratch_shapes=[pltpu.VMEM((128 * 8, 128), F32), pltpu.SemaphoreType.DMA((3,))],
+        out_specs=VMEM,
         compiler_params=params(4),
         name="to_units",
     )(jnp.asarray(TO_UNITS), received)

time: 107 us -> 107 us (level)
  no operation moved by 1% of the time
where the time goes in v7:
time: 107 us
  blocking collectives  70.7 us (66%)
  Pallas kernels  18.7 us (17%)
  waiting for transfers between devices  11.3 us (11%)
  starting transfers between devices  5.47 us (5%)
    all_to_all x3, blocking collectives, exchange(): moved = lax.all_to_all(value.reshape(peers, rows, 128), axes, 0, 0)  70.7 us
    pallas_call x1, Pallas kernels, per_device(): pl.pallas_call(units_kernel, out_shape=array(SLICES, 16 * 24, 128), in_sp...  12.6 us
    all_to_all x1, waiting for transfers between devices, exchange(): moved = lax.all_to_all(value.reshape(peers, rows, 128), axes, 0, 0)  11.3 us
    all_to_all x1, starting transfers between devices, exchange(): moved = lax.all_to_all(value.reshape(peers, rows, 128), axes, 0, 0)  5.47 us
  transfers between devices with their start and end apart: 1, of which 1 were waited for; matrix products, arithmetic and copies ran while one was open for 0% of the time, Pallas kernels for 2%

profile of v7, /device:TPU:1, one launch (start us, length us, event | category | flops | bytes accessed | tf_op | source)
XLA Modules:
  0.0 106.6 jit_solution(11498896691630965149)
XLA Ops:
  0.0 1.0 gather_points.1
  1.0 0.0 copy-start.3
  1.1 18.7 %all_to_all.20 = f32[16,40,128]{2,1,0:T(8,128)S(1)} all-to-all(f32[16,40,128]{2,1,0:T(8,128)S(1)} %bitcast.19), channel_id=1, replica_groups=mesh['tm'=8,'azim'=16] {'azim'}, dimensions={0} | all-to-all | bytes 655360 | tf_op jit(solution)/shard_map/all_to_all | solution.py:582
  19.8 0.0 copy-done.3
  19.8 0.0 copy-start
  19.9 0.0 copy-start.1
  19.9 0.0 copy-start.4
  19.9 0.0 copy-start.5
  19.9 0.0 copy-start.6
  19.9 0.0 copy-start.7
  19.9 0.0 copy-start.8
  19.9 0.0 copy-start.9
  19.9 0.0 copy-start.10
  19.9 0.0 copy-start.11
  20.0 0.0 copy-start.12
  20.0 0.0 copy-start.13
  20.0 0.0 copy-start.14
  20.0 1.2 %to_units.1 = f32[1024,128]{1,0:T(8,128)} custom-call(bf16[192,576]{1,0:T(8,128)(2,1)S(1)} %copy-done.3, f32[576,128]{1,0:T(8,128)S(1)} %reshape.42.received_ref), custom_call_target="tpu_custom_call" | custom-call | tf_op jit(solution)/shard_map/to_units/pallas_call | solution.py:640
  21.2 5.5 %all-to-all-start.1 = ((f32[128,8,128]{2,1,0:T(8,128)}), f32[128,8,128]{2,1,0:T(8,128)S(1)}, u32[]{:S(2)}, u32[]{:S(2)}) async-start(f32[128,8,128]{2,1,0:T(8,128)} %bitcast.3), calls=%async_computation.1 | async-start | bytes 1048576 | tf_op jit(solution)/shard_map/all_to_all | solution.py:582
  26.6 0.0 copy-done
  26.6 0.0 copy-done.1
  26.7 0.0 copy-done.4
  26.7 0.0 copy-done.5
  26.7 0.0 copy-done.6
  26.7 0.0 copy-done.7
  26.7 0.0 copy-done.8
  26.7 0.0 copy-done.9
  26.7 0.0 copy-done.10
  26.7 0.0 copy-done.11
  26.7 0.0 copy-done.12
  26.7 0.0 copy-done.13
  26.8 0.0 copy-done.14
  26.8 2.1 %operators.1 = (bf16[1536,256]{1,0:T(8,128)(2,1)S(1)}, bf16[384,192]{1,0:T(8,128)(2,1)S(1)}, bf16[768,128]{1,0:T(8,128)(2,1)S(1)}, bf16[192,144]{1,0:T(8,128)(2,...) custom-call(f32[128,4]{1,0:T(8,128)S(1)} %copy-done.7, f32[96,96]{1,0:T(8,128)S(1)} %copy-done.8, ...), custom_call_target="tpu_custom_call" | custom-call | tf_op jit(solution)/shard_map/operators/pallas_call | solution.py:602
  28.8 11.3 %all-to-all-done.1 = f32[128,8,128]{2,1,0:T(8,128)S(1)} async-done(((f32[128,8,128]{2,1,0:T(8,128)}), f32[128,8,128]{2,1,0:T(8,128)S(1)}, u32[]{:S(2)}, u32[]{:S(2)}) %all-to-all-start.1) | async-done | bytes 524320 | tf_op jit(solution)/shard_map/all_to_all | solution.py:582
  40.1 12.6 %units.1 = f32[8,384,128]{2,1,0:T(8,128)S(1)} custom-call(f32[1024,128]{1,0:T(8,128)S(1)} %bitcast.18, bf16[1536,256]{1,0:T(8,128)(2,1)S(1)} %get-tuple-element.11.axial_ref, bf16[384,192]{1,0:T(8,128)(2,1)S(1)} %get-tuple-element.12.radial_ref, bf16[768,128]{1,0:T(8,128)(2,1)S(1)} %get-tuple-element.13.axial_c_ref, ...), custom_call_target="tpu_custom_call" | custom-call | tf_op jit(solution)/shard_map/units/pallas_call | solution.py:651
  52.7 0.0 copy-start.2
  52.7 29.1 %all_to_all.21 = f32[128,24,128]{2,1,0:T(8,128)S(1)} all-to-all(f32[128,24,128]{2,1,0:T(8,128)S(1)} %bitcast.15), channel_id=1, replica_groups=mesh['tm'=8,'azim'=16] {'tm','azim'}, dimensions={0} | all-to-all | bytes 3145728 | tf_op jit(solution)/shard_map/all_to_all | solution.py:582
  81.8 0.0 copy-done.2
  81.8 0.8 from_units.1
  82.6 22.8 %all_to_all.22 = f32[16,144,128]{2,1,0:T(8,128)S(1)} all-to-all(f32[16,144,128]{2,1,0:T(8,128)S(1)} %bitcast.17), channel_id=1, replica_groups=mesh['tm'=8,'azim'=16] {'azim'}, dimensions={0} | all-to-all | bytes 2359296 | tf_op jit(solution)/shard_map/all_to_all | solution.py:582
  105.4 1.1 %place.1 = f32[12,96,256]{2,1,0:T(8,128)} custom-call(f32[2304,128]{1,0:T(8,128)S(1)} %bitcast.16), custom_call_target="tpu_custom_call" | custom-call | tf_op jit(solution)/shard_map/place/pallas_call | solution.py:680
  (1 shorter events, 0.0 us)
Async XLA Ops:
  1.0 18.8 %copy-start.3 = (bf16[192,576]{1,0:T(8,128)(2,1)S(1)}, bf16[192,576]{1,0:T(8,128)(2,1)}, u32[]{:S(2)}) copy-start(bf16[192,576]{1,0:T(8,128)(2,1)} %constant.7.clone.transform_ref) | copy-start | bytes 663556
  19.8 6.8 %copy-start = (f32[256,256]{1,0:T(8,128)S(1)}, f32[256,256]{1,0:T(8,128)}, u32[]{:S(2)}) copy-start(f32[256,256]{1,0:T(8,128)} %forward_axial_ref.1) | copy-start | bytes 786436
  19.9 6.8 %copy-start.1 = (f32[256,256]{1,0:T(8,128)S(1)}, f32[256,256]{1,0:T(8,128)}, u32[]{:S(2)}) copy-start(f32[256,256]{1,0:T(8,128)} %backward_axial_ref.1) | copy-start | bytes 786436
  19.9 6.8 %copy-start.4 = (f32[96,256]{1,0:T(8,128)S(1)}, f32[96,256]{1,0:T(8,128)}, u32[]{:S(2)}) copy-start(f32[96,256]{1,0:T(8,128)} %advection_ref.1) | copy-start | bytes 294916
  19.9 6.8 %copy-start.5 = (f32[128,128]{1,0:T(8,128)S(1)}, f32[128,128]{1,0:T(8,128)}, u32[]{:S(2)}) copy-start(f32[128,128]{1,0:T(8,128)} %forward_axial_c_ref.1) | copy-start | bytes 196612
  19.9 6.8 %copy-start.6 = (f32[128,128]{1,0:T(8,128)S(1)}, f32[128,128]{1,0:T(8,128)}, u32[]{:S(2)}) copy-start(f32[128,128]{1,0:T(8,128)} %backward_axial_c_ref.1) | copy-start | bytes 196612
  19.9 6.8 %copy-start.7 = (f32[128,4]{1,0:T(8,128)S(1)}, f32[128,4]{1,0:T(8,128)}, u32[]{:S(2)}) copy-start(f32[128,4]{1,0:T(8,128)} %constant.6.clone.scalars_ref) | copy-start | bytes 6148
  19.9 6.8 %copy-start.8 = (f32[96,96]{1,0:T(8,128)S(1)}, f32[96,96]{1,0:T(8,128)}, u32[]{:S(2)}) copy-start(f32[96,96]{1,0:T(8,128)} %forward_radial_ref.1) | copy-start | bytes 110596
  19.9 6.8 %copy-start.9 = (f32[96,96]{1,0:T(8,128)S(1)}, f32[96,96]{1,0:T(8,128)}, u32[]{:S(2)}) copy-start(f32[96,96]{1,0:T(8,128)} %backward_radial_ref.1) | copy-start | bytes 110596
  19.9 6.8 %copy-start.10 = (f32[48,48]{1,0:T(8,128)S(1)}, f32[48,48]{1,0:T(8,128)}, u32[]{:S(2)}) copy-start(f32[48,48]{1,0:T(8,128)} %forward_radial_c_ref.1) | copy-start | bytes 27652
  19.9 6.8 %copy-start.11 = (f32[48,48]{1,0:T(8,128)S(1)}, f32[48,48]{1,0:T(8,128)}, u32[]{:S(2)}) copy-start(f32[48,48]{1,0:T(8,128)} %backward_radial_c_ref.1) | copy-start | bytes 27652
  20.0 6.8 %copy-start.12 = (f32[256]{0:T(256)S(1)}, f32[256]{0:T(256)}, u32[]{:S(2)}) copy-start(f32[256]{0:T(256)} %param.28) | copy-start | bytes 3076
  20.0 6.8 %copy-start.13 = (f32[96]{0:T(128)S(1)}, f32[96]{0:T(128)}, u32[]{:S(2)}) copy-start(f32[96]{0:T(128)} %param.27) | copy-start | bytes 1156
  20.0 6.8 %copy-start.14 = (f32[96]{0:T(128)S(1)}, f32[96]{0:T(128)}, u32[]{:S(2)}) copy-start(f32[96]{0:T(128)} %param.30) | copy-start | bytes 1156
  21.2 18.9 %all-to-all-start.1 = ((f32[128,8,128]{2,1,0:T(8,128)}), f32[128,8,128]{2,1,0:T(8,128)S(1)}, u32[]{:S(2)}, u32[]{:S(2)}) async-start(f32[128,8,128]{2,1,0:T(8,128)} %bitcast.3), calls=%async_computation.1 | async-start | bytes 1048576 | tf_op jit(solution)/shard_map/all_to_all | solution.py:582
  52.7 29.1 %copy-start.2 = (bf16[192,576]{1,0:T(8,128)(2,1)S(1)}, bf16[192,576]{1,0:T(8,128)(2,1)}, u32[]{:S(2)}) copy-start(bf16[192,576]{1,0:T(8,128)(2,1)} %constant.8.clone.transform_ref) | copy-start | bytes 663556
